TPU v7x, 32 devices: a whole 2x2x4 slice. The times are simulated.
32 devices in a mesh: dp: 16 (over z, y, core), mp: 2 (over x).
Axes of the slice: x: 2, y: 2, z: 4, core: 2. Of those that a mesh axis runs over, the one named last changes fastest.
Arguments:
- patch_counts: int32 [128], P('dp'), may hold values from 100 to 240, as said below
- tokens: bfloat16 [128, 280, 768], P('dp'), may hold values from -6 to 6
- cotangent: bfloat16 [128, 280, 768], P('dp'), may hold values from -6 to 6
- attn_gain: float32 [768], P('dp'), may hold values from 0.1 to 1.9
- attn_shift: float32 [768], P('dp'), may hold values from -1.75 to 1.75
- w_qkv: float32 [768, 3, 768], P('dp', None, 'mp'), may hold values from -0.21875 to 0.21875
- b_qv: float32 [2, 768], P(None, 'mp'), may hold values from -3 to 3
- w_proj: float32 [768, 768], P('mp', 'dp'), may hold values from -0.875 to 0.875
- b_proj: float32 [768], P('dp'), may hold values from -3 to 3
- ffn_gain: float32 [768], P('dp'), may hold values from 0.1 to 1.9
- ffn_shift: float32 [768], P('dp'), may hold values from -1.75 to 1.75
- w_up: float32 [768, 3072], P('dp', 'mp'), may hold values from -0.21875 to 0.21875
- b_up: float32 [3072], P('mp'), may hold values from -3 to 3
- w_down: float32 [3072, 768], P('mp', 'dp'), may hold values from -0.109375 to 0.109375
- b_down: float32 [768], P('dp'), may hold values from -3 to 3
Outputs:
- block_out: bfloat16 [128, 280, 768], P('dp')
- tokens_grad: bfloat16 [128, 280, 768], P('dp')
- attn_gain_grad: float32 [768], P('dp')
- attn_shift_grad: float32 [768], P('dp')
- w_qkv_grad: float32 [768, 3, 768], P('dp', None, 'mp')
- b_qv_grad: float32 [2, 768], P(None, 'mp')
- w_proj_grad: float32 [768, 768], P('mp', 'dp')
- b_proj_grad: float32 [768], P('dp')
- ffn_gain_grad: float32 [768], P('dp')
- ffn_shift_grad: float32 [768], P('dp')
- w_up_grad: float32 [768, 3072], P('dp', 'mp')
- b_up_grad: float32 [3072], P('mp')
- w_down_grad: float32 [3072, 768], P('mp', 'dp')
- b_down_grad: float32 [768], P('dp')
Inputs may be any that keep to these rules, and one draw needn't show every extreme that they name: `patch_counts`: patch count of each pair; in every draw some pair has exactly 240 patches and some exactly 100.
All inputs are finite; a program needn't handle non-finite values.
Results may differ from a plain program's by a relative error of at most 0.022.
Values may be sent and summed in bfloat16 or wider, within the bound.
A program may use at most 192 MiB of HBM per device.

v0:
```python
import math

import jax
import jax.numpy as jnp
from jax import lax
from jax.sharding import PartitionSpec as P

HEADS = 12
HEAD_DIM = 64
TEXT = 40


def normalize(values, gain, shift):
    center = values - jnp.mean(values, axis=-1, keepdims=True)
    spread = jnp.mean(center * center, axis=-1, keepdims=True)
    return center * lax.rsqrt(spread + 1e-06) * gain + shift


def norm_back(values, gain, incoming):
    _, pullback = jax.vjp(lambda member, scaling: normalize(member, scaling, 0.0), values, gain)
    d_values, d_gain = pullback(incoming)
    return (d_values, d_gain, jnp.sum(incoming, axis=(0, 1)))


def per_device(
    patch_counts,
    tokens,
    cotangent,
    attn_gain,
    attn_shift,
    w_qkv,
    b_qv,
    w_proj,
    b_proj,
    ffn_gain,
    ffn_shift,
    w_up,
    b_up,
    w_down,
    b_down,
):
    low_type = jnp.bfloat16
    pair_count, rows_pair, _ = tokens.shape
    head_count = HEADS // lax.axis_size("mp")
    local_width = w_qkv.shape[2]
    score_scale = HEAD_DIM ** (-0.5)
    pair_block = math.gcd(pair_count, -(-512 // rows_pair))
    block_count = pair_count // pair_block
    gathered = (
        lax.all_gather(w_qkv.astype(low_type), "dp", axis=0, tiled=True),
        lax.all_gather(w_proj.astype(low_type), "dp", axis=1, tiled=True),
        lax.all_gather(w_up.astype(low_type), "dp", axis=0, tiled=True),
        lax.all_gather(w_down.astype(low_type), "dp", axis=1, tiled=True),
        lax.all_gather(attn_gain.astype(low_type), "dp", axis=0, tiled=True),
        lax.all_gather(attn_shift.astype(low_type), "dp", axis=0, tiled=True),
        lax.all_gather(b_proj.astype(low_type), "dp", axis=0, tiled=True),
        lax.all_gather(ffn_gain.astype(low_type), "dp", axis=0, tiled=True),
        lax.all_gather(ffn_shift.astype(low_type), "dp", axis=0, tiled=True),
        lax.all_gather(b_down.astype(low_type), "dp", axis=0, tiled=True),
    )
    qkv_full, proj_full, up_full, down_full = (gathered[0], gathered[1], gathered[2], gathered[3])
    gain_one = gathered[4].astype(jnp.float32)
    shift_one = gathered[5].astype(jnp.float32)
    proj_bias = gathered[6].astype(jnp.float32)
    gain_two = gathered[7].astype(jnp.float32)
    shift_two = gathered[8].astype(jnp.float32)
    down_bias = gathered[9].astype(jnp.float32)
    bias_qv = b_qv.astype(low_type).astype(jnp.float32)
    up_bias = b_up.astype(low_type).astype(jnp.float32)
    row_valid = (
        jnp.arange(rows_pair, dtype=jnp.int32)[None, :] < (TEXT + patch_counts)[:, None]
    ).astype(jnp.float32)
    inputs = tokens.astype(jnp.float32)
    normed_one = normalize(inputs, gain_one, shift_one).astype(low_type)
    qkv = jnp.einsum("psd,dtc->pstc", normed_one, qkv_full, preferred_element_type=jnp.float32)
    queries = (qkv[:, :, 0] + bias_qv[0]).astype(low_type)
    key_rows = qkv[:, :, 1].astype(low_type)
    values = (qkv[:, :, 2] + bias_qv[1]).astype(low_type)

    def by_blocks(array):
        return array.reshape(block_count, pair_block, rows_pair, head_count, HEAD_DIM)

    key_mask = row_valid.reshape(block_count, pair_block, rows_pair)

    def score_rows(query_block, key_block, mask_block):
        raw = (
            jnp.einsum(
                "bqhe,bkhe->bhqk", query_block, key_block, preferred_element_type=jnp.float32
            )
            * score_scale
        )
        return jnp.where(mask_block[:, None, None, :] > 0, raw, -1e30)

    def attend(operands):
        query_block, key_block, value_block, mask_block = operands
        scores = score_rows(query_block, key_block, mask_block)
        row_max = jnp.max(scores, axis=-1, keepdims=True)
        expo = jnp.exp(scores - row_max)
        row_total = jnp.sum(expo, axis=-1, keepdims=True)
        probabilities = (expo / row_total).astype(low_type)
        attended_block = jnp.einsum(
            "bhqk,bkhe->bqhe", probabilities, value_block, preferred_element_type=jnp.float32
        ).astype(low_type)
        log_total = row_max[..., 0] + jnp.log(row_total[..., 0])
        return (attended_block, log_total)

    attended_blocks, log_totals = lax.map(
        attend, (by_blocks(queries), by_blocks(key_rows), by_blocks(values), key_mask)
    )
    attended = attended_blocks.reshape(pair_count, rows_pair, local_width)
    proj_part = jnp.einsum("psc,cd->psd", attended, proj_full, preferred_element_type=jnp.float32)
    attn_sum = lax.psum(proj_part.astype(jnp.bfloat16), "mp").astype(jnp.float32)
    hidden = inputs + attn_sum + proj_bias
    normed_two = normalize(hidden, gain_two, shift_two).astype(low_type)
    pre_act = (
        jnp.einsum("psd,df->psf", normed_two, up_full, preferred_element_type=jnp.float32) + up_bias
    )
    active = jax.nn.gelu(pre_act, approximate=False).astype(low_type)
    down_part = jnp.einsum("psf,fd->psd", active, down_full, preferred_element_type=jnp.float32)
    mlp_sum = lax.psum(down_part.astype(jnp.bfloat16), "mp").astype(jnp.float32)
    block_out = ((hidden + mlp_sum + down_bias) * row_valid[:, :, None]).astype(low_type)
    qkv_back, proj_back, up_back, down_back = (qkv_full, proj_full, up_full, down_full)
    gain_one_back, gain_two_back = (gain_one, gain_two)
    upstream = cotangent.astype(jnp.float32) * row_valid[:, :, None]
    upstream_low = upstream.astype(low_type)
    grad_b_down = jnp.sum(upstream, axis=(0, 1))
    grad_w_down = jnp.einsum(
        "psf,psd->fd", active, upstream_low, preferred_element_type=jnp.float32
    )
    d_active = jnp.einsum(
        "psd,fd->psf", upstream_low, down_back, preferred_element_type=jnp.float32
    )
    _, gelu_pull = jax.vjp(lambda member: jax.nn.gelu(member, approximate=False), pre_act)
    d_pre = gelu_pull(d_active)[0].astype(low_type)
    grad_b_up = jnp.sum(d_pre, axis=(0, 1), dtype=jnp.float32)
    grad_w_up = jnp.einsum("psd,psf->df", normed_two, d_pre, preferred_element_type=jnp.float32)
    d_normed_two = lax.psum(
        jnp.einsum("psf,df->psd", d_pre, up_back, preferred_element_type=jnp.float32).astype(
            jnp.bfloat16
        ),
        "mp",
    ).astype(jnp.float32)
    d_hidden_norm, grad_gain_two, grad_shift_two = norm_back(hidden, gain_two_back, d_normed_two)
    d_hidden = upstream + d_hidden_norm
    grad_b_proj = jnp.sum(d_hidden, axis=(0, 1))
    d_hidden_low = d_hidden.astype(low_type)
    grad_w_proj = jnp.einsum(
        "psc,psd->cd", attended, d_hidden_low, preferred_element_type=jnp.float32
    )
    d_attended = jnp.einsum(
        "psd,cd->psc", d_hidden_low, proj_back, preferred_element_type=jnp.float32
    ).astype(low_type)

    def attend_back(operands):
        query_block, key_block, value_block, mask_block, log_total, d_out = operands
        scores = score_rows(query_block, key_block, mask_block)
        probabilities = jnp.exp(scores - log_total[..., None])
        d_probs = jnp.einsum(
            "bqhe,bkhe->bhqk", d_out, value_block, preferred_element_type=jnp.float32
        )
        d_value = jnp.einsum(
            "bhqk,bqhe->bkhe",
            probabilities.astype(low_type),
            d_out,
            preferred_element_type=jnp.float32,
        )
        inner = jnp.sum(probabilities * d_probs, axis=-1, keepdims=True)
        d_scores = (probabilities * (d_probs - inner)).astype(low_type)
        d_query = score_scale * jnp.einsum(
            "bhqk,bkhe->bqhe", d_scores, key_block, preferred_element_type=jnp.float32
        )
        d_key = score_scale * jnp.einsum(
            "bhqk,bqhe->bkhe", d_scores, query_block, preferred_element_type=jnp.float32
        )
        return jnp.stack([d_query, d_key, d_value], axis=2).astype(low_type)

    d_blocks = lax.map(
        attend_back,
        (
            by_blocks(queries),
            by_blocks(key_rows),
            by_blocks(values),
            key_mask,
            log_totals,
            by_blocks(d_attended),
        ),
    )
    d_qkv = d_blocks.reshape(pair_count, rows_pair, 3, local_width)
    column_sums = jnp.sum(d_qkv, axis=(0, 1), dtype=jnp.float32)
    grad_b_qv = jnp.stack([column_sums[0], column_sums[2]], axis=0)
    grad_w_qkv = jnp.einsum("psd,pstc->dtc", normed_one, d_qkv, preferred_element_type=jnp.float32)
    d_normed_one = lax.psum(
        jnp.einsum("pstc,dtc->psd", d_qkv, qkv_back, preferred_element_type=jnp.float32).astype(
            jnp.bfloat16
        ),
        "mp",
    ).astype(jnp.float32)
    d_input_norm, grad_gain_one, grad_shift_one = norm_back(inputs, gain_one_back, d_normed_one)
    tokens_grad = (d_hidden + d_input_norm).astype(low_type)
    bias_grads = lax.psum((grad_b_qv, grad_b_up), "dp")
    summed = (
        lax.psum_scatter(grad_w_qkv, "dp", scatter_dimension=0, tiled=True),
        lax.psum_scatter(grad_w_proj, "dp", scatter_dimension=1, tiled=True),
        lax.psum_scatter(grad_w_up, "dp", scatter_dimension=0, tiled=True),
        lax.psum_scatter(grad_w_down, "dp", scatter_dimension=1, tiled=True),
        lax.psum_scatter(grad_gain_one, "dp", scatter_dimension=0, tiled=True),
        lax.psum_scatter(grad_shift_one, "dp", scatter_dimension=0, tiled=True),
        lax.psum_scatter(grad_b_proj, "dp", scatter_dimension=0, tiled=True),
        lax.psum_scatter(grad_gain_two, "dp", scatter_dimension=0, tiled=True),
        lax.psum_scatter(grad_shift_two, "dp", scatter_dimension=0, tiled=True),
        lax.psum_scatter(grad_b_down, "dp", scatter_dimension=0, tiled=True),
    )
    out_qkv, out_proj, out_up, out_down = (summed[0], summed[1], summed[2], summed[3])
    out_gain_one, out_shift_one, out_bproj = (summed[4], summed[5], summed[6])
    out_gain_two, out_shift_two, out_bdown = (summed[7], summed[8], summed[9])
    return (
        block_out,
        tokens_grad,
        out_gain_one,
        out_shift_one,
        out_qkv,
        bias_grads[0],
        out_proj,
        out_bproj,
        out_gain_two,
        out_shift_two,
        out_up,
        bias_grads[1],
        out_down,
        out_bdown,
    )


def solution(mesh):
    in_specs = (
        P("dp"),
        P("dp", None, None),
        P("dp", None, None),
        P("dp"),
        P("dp"),
        P("dp", None, "mp"),
        P(None, "mp"),
        P("mp", "dp"),
        P("dp"),
        P("dp"),
        P("dp"),
        P("dp", "mp"),
        P("mp"),
        P("mp", "dp"),
        P("dp"),
    )
    out_specs = (
        P("dp", None, None),
        P("dp", None, None),
        P("dp"),
        P("dp"),
        P("dp", None, "mp"),
        P(None, "mp"),
        P("mp", "dp"),
        P("dp"),
        P("dp"),
        P("dp"),
        P("dp", "mp"),
        P("mp"),
        P("mp", "dp"),
        P("dp"),
    )
    return jax.shard_map(
        per_device, mesh=mesh, in_specs=in_specs, out_specs=out_specs, check_vma=False
    )
```

profile of v0, /device:TPU:8, one launch (start us, length us, event | category | flops | bytes accessed | tf_op | source)
XLA Modules:
  0.0 1067.8 jit_solution(13060933296893398383)
XLA Ops:
  20.8 53.7 %all-reduce.13 = (bf16[768]{0:T(1024)(128)(2,1)}, bf16[768]{0:T(1024)(128)(2,1)}, bf16[768]{0:T(1024)(128)(2,1)}, bf16[768]{0:T(1024)(128)(2,1)}, bf16[768]{0:T(1024)(128)(2,1)}, /*index=5*/bf16[768]{0:T(1024)(128)(2,1)}) all-reduce(bf16[768]{0:T(1024)(128)(2,1)} %dynamic-update-slice.4, ...), channel_id=1, replica_groups=mesh['dp'=16,'mp'=2] {'dp'}, use_global_device_ids=true, to_apply=%add.4 | all-reduce | flops 4608 | bytes 18432
  87.8 25.5 %all_gather.33 = bf16[384,768]{0,1:T(8,128)(2,1)} all-gather(bf16[384,48]{0,1:T(8,128)(2,1)S(1)} %convert_element_type.183), channel_id=1, replica_groups=mesh['dp'=16,'mp'=2] {'dp'}, dimensions={1}, use_global_device_ids=true | all-gather | bytes 626688 | tf_op jit(solution)/shard_map/all_gather | solution.py:51
  113.2 7.1 fusion.96
  120.3 3.3 fusion.113
  125.1 5.7 copy.58
  130.7 5.5 copy.59
  136.3 4.0 copy.60
  140.2 7.3 add_convert_fusion.3
  147.6 32.6 %while.22 = (s32[]{:T(128)}, bf16[4,2,280,6,64]{2,4,3,1,0:T(8,128)(2,1)}, f32[4,2,6,280]{3,2,1,0:T(8,128)S(1)}, bf16[4,2,280,6,64]{2,4,3,1,0:T(8,128)(2,1)}, f32...) while((s32[]{:T(128)}, ...), condition=%wide.region_5.6_spmd, body=%wide.region_2.5_spmd.sunk | while | flops 252346640 | bytes 13796445 | solution.py:107
  152.3 3.5 fusion.145
  160.4 3.5 fusion.145
  168.6 3.5 fusion.145
  176.8 3.5 fusion.145
  180.2 6.0 convolution_convert_fusion.2
  193.5 86.5 %all-reduce.19.cloned.1.call-done = bf16[8,280,768]{2,1,0:T(8,128)(2,1)} async-done(((bf16[8,280,768]{2,1,0:T(8,128)(2,1)}), bf16[8,280,768]{2,1,0:T(8,128)(2,1)}) %all-reduce.19.cloned.1.call-update) | async-done | bytes 3440656 | tf_op jit(solution)/shard_map/psum | solution.py:112
  280.0 3.3 fusion.82
  286.7 37.8 %all-gather.6.cloned.1.call-done = bf16[768,1536]{1,0:T(8,128)(2,1)} async-done(((bf16[48,1536]{1,0:T(8,128)(2,1)}), bf16[768,1536]{1,0:T(8,128)(2,1)}) %all-gather.6.cloned.1.call-update) | async-done | bytes 2359312 | tf_op jit(solution)/shard_map/all_gather | solution.py:52
  324.6 13.9 %fusion.86 = (u8[280,1536]{1,0:T(8,128)(4,1)S(1)}, u8[280,1536]{1,0:T(8,128)(4,1)S(1)}, f32[8,280,1536]{2,1,0:T(8,128)S(1)}) fusion(f32[1536]{0:T(1024)} %convert_convert_fusion, bf16[768,1536]{1,0:T(8,128)(2,1)} %all-gather.6.cloned.1.call-done, f32[768]{0:T(1024)} %convert_element_type.191, f32[768]{0:T(1024)} %convert_element_type.189, ...), kind=kOutput, calls=%fused_computation.134 | convolution fusion | flops 5347614720 | bytes 23896576 | tf_op jit(solution)/shard_map/psd,df->psf/dot_general | solution.py:116
  338.5 4.9 copy-done.6
  343.4 32.9 %multiply_convert_fusion.1 = (bf16[8,280,1536]{2,1,0:T(8,128)(2,1)}, f32[8,280,1536]{2,1,0:T(8,128)}) fusion(f32[8,280,1536]{2,1,0:T(8,128)S(1)} %get-tuple-element.187, f32[1536]{0:T(1024)S(1)} %copy-done.25, u8[280,1536]{1,0:T(8,128)(4,1)S(1)} %get-tuple-element.113, u8[280,1536]{1,0:T(8,128)(4,1)S(1)} %get-tuple-element.112), kind=kLoop, calls=%fused_computation.75 | loop fusion | flops 244285440 | bytes 35272704 | tf_op jit(solution)/shard_map/convert_element_type | solution.py:118
  376.3 18.8 %convert_reduce_fusion.1 = (f32[1536]{0:T(1024)}, bf16[8,280,1536]{2,1,0:T(8,128)(2,1)}) fusion(f32[8,280,1536]{2,1,0:T(8,128)} %get-tuple-element.173, bf16[1536,768]{0,1:T(8,128)(2,1)} %all-gather.8.cloned.1.call-done, bf16[8,280,768]{2,1,0:T(8,128)(2,1)} %param.21, f32[8,280]{1,0:T(8,128)} %fusion.108, f32[8,280,1536]{2,1,0:T(8,128)} %copy-done.6, ...), kind=kOutput, calls=%fused_computation.73 | convolution fusion | flops 5348473344 | bytes 40227584 | tf_op jit(solution)/shard_map/psd,fd->psf/dot_general | solution.py:130
  395.1 10.0 convolution_convert_fusion
  405.2 10.2 convolution_convert_fusion.1
  415.4 81.6 %all-reduce.21.cloned.1.call-done = bf16[8,280,768]{2,1,0:T(8,128)(2,1)} async-done(((bf16[8,280,768]{2,1,0:T(8,128)(2,1)}), bf16[8,280,768]{2,1,0:T(8,128)(2,1)}) %all-reduce.21.cloned.1.call-update) | async-done | bytes 3440656 | tf_op jit(solution)/shard_map/psum | solution.py:137
  497.0 6.4 convert_reduce_fusion.3
  503.5 5.6 fusion.77
  509.0 4.9 fusion.111
  519.8 4.0 copy.62
  523.8 63.8 %while.23 = (s32[]{:T(128)}, bf16[4,2,280,3,6,64]{2,5,4,1,3,0:T(8,128)(2,1)}, bf16[4,2,280,6,64]{2,4,3,1,0:T(8,128)(2,1)}, f32[4,2,280]{2,1,0:T(2,128)}, bf16[4,...) while((s32[]{:T(128)}, ...), condition=%wide.region_15.16_spmd, body=%wide.region_13.15_spmd.sunk | while | flops 621167104 | bytes 36805476 | solution.py:177
  527.0 3.4 multiply_reduce_fusion.3
  542.9 3.4 multiply_reduce_fusion.3
  558.8 3.4 multiply_reduce_fusion.3
  574.7 3.4 multiply_reduce_fusion.3
  587.6 4.3 copy.63
  594.8 7.7 bitcast_convert_fusion
  602.8 7.4 fusion.101
  610.3 12.6 %convolution_bitcast_fusion.1 = f32[768,1536]{1,0:T(8,128)} fusion(bf16[8,280,1536]{2,1,0:T(8,128)(2,1)} %get-tuple-element.189, f32[768]{0:T(1024)S(1)} %copy-done.35, f32[768]{0:T(1024)S(1)} %copy-done.24, f32[8,280]{1,0:T(8,128)S(1)} %copy-done.20, f32[8,280]{1,0:T(8,128)S(1)} %broadcast_multiply_fusion, f32[768]{0:T(1024)S(1)} %convert_element_type.187, ...), kind=kOutput, calls=%fused_computation.130 | convolution fusion | flops 5300305920 | bytes 18508288 | tf_op jit(solution)/shard_map/psd,psf->df/dot_general | solution.py:136
  622.9 11.0 %convolution_bitcast_fusion = f32[1536,768]{0,1:T(8,128)} fusion(bf16[8,280,1536]{2,1,0:T(8,128)(2,1)} %get-tuple-element.172, bf16[8,280,768]{2,1,0:T(8,128)(2,1)} %param.21, f32[8,280]{1,0:T(8,128)S(1)} %copy-done.18), kind=kOutput, calls=%fused_computation.129 | convolution fusion | flops 5289984000 | bytes 15049472 | tf_op jit(solution)/shard_map/psf,psd->fd/dot_general | solution.py:127
  634.3 13.7 %convolution_bitcast_fusion.2 = f32[768,3,384]{2,0,1:T(8,128)} fusion(bf16[8,280,3,384]{1,3,2,0:T(8,128)(2,1)} %bitcast.170, bf16[8,280,768]{2,1,0:T(8,128)(2,1)S(1)} %copy-done, f32[768]{0:T(1024)S(1)} %copy-done.34, f32[768]{0:T(1024)S(1)} %copy-done.22, f32[8,280]{1,0:T(8,128)S(1)} %copy-done.16, f32[8,280]{1,0:T(8,128)S(1)} %copy-done.11), kind=kOutput, calls=%fused_computation.144 | convolution fusion | flops 3973939200 | bytes 12164608 | tf_op jit(solution)/shard_map/psd,pstc->dtc/dot_general | solution.py:191
  648.7 4.3 convert_reduce_fusion
  653.2 115.4 %all-reduce.23.cloned.1.call-done = (bf16[8,280,768]{2,1,0:T(8,128)(2,1)}, bf16[8,280,768]{2,1,0:T(8,128)(2,1)}) async-done(((bf16[8,280,768]{2,1,0:T(8,128)(2,1)}, bf16[8,280,768]{2,1,0:T(8,128)(2,1)}), (bf16[8,280,768]{2,1,0:T(8,128)(2,1)}, bf16[8,280,768]{2,1,0:T(8,128)(2,1)})) %all-reduce.23.cloned.1.call-update) | async-done | bytes 6881296 | tf_op jit(solution)/shard_map/psum | solution.py:120
  768.7 4.2 convert_reduce_fusion.2
  772.9 4.3 fusion.78
  777.2 53.3 %all-reduce.12 = (f32[768]{0:T(1024)S(1)}, f32[768]{0:T(1024)S(1)}, f32[2,384]{1,0:T(2,128)}, f32[768]{0:T(1024)}, f32[768]{0:T(1024)}, /*index=5*/f32[768]{0:T(1024)}, f32[1536]{0:T(1024)}, f32[768]{0:T(1024)S(1)}) all-reduce(f32[768]{0:T(1024)S(1)} %get-tuple-element.116, ...), channel_id=2, replica_groups=mesh['dp'=16,'mp'=2] {'dp'}, use_global_device_ids=true, to_apply=%region_20.21.clone | all-reduce | flops 6912 | bytes 55296
  836.0 10.6 add_convert_fusion.1
  846.6 63.0 %reduce-scatter.9.cloned.1.call-done = f32[48,1536]{1,0:T(8,128)} async-done(((f32[768,1536]{1,0:T(8,128)}), f32[48,1536]{1,0:T(8,128)}) %reduce-scatter.9.cloned.1.call-update) | async-done | bytes 294928 | tf_op jit(solution)/shard_map/reduce_scatter | solution.py:204
  909.7 79.2 %reduce-scatter.11.cloned.1.call-done = f32[1536,48]{0,1:T(8,128)} async-done(((f32[1536,768]{0,1:T(8,128)}), f32[1536,48]{0,1:T(8,128)}) %reduce-scatter.11.cloned.1.call-update) | async-done | bytes 294928 | tf_op jit(solution)/shard_map/reduce_scatter | solution.py:205
  988.9 71.6 %reduce-scatter.5.cloned.1.call-done = f32[48,3,384]{2,0,1:T(8,128)} async-done(((f32[768,3,384]{2,0,1:T(8,128)}), f32[48,3,384]{2,0,1:T(8,128)}) %reduce-scatter.5.cloned.1.call-update) | async-done | bytes 221200 | tf_op jit(solution)/shard_map/reduce_scatter | solution.py:202
  (218 shorter events, 122.2 us)
Async XLA Ops:
  7.2 106.1 %copy-start = (bf16[8,280,768]{2,1,0:T(8,128)(2,1)S(1)}, bf16[8,280,768]{2,1,0:T(8,128)(2,1)}, u32[]{:S(2)}) copy-start(bf16[8,280,768]{2,1,0:T(8,128)(2,1)} %param.20) | copy-start | bytes 10321924
  7.2 106.1 %all-gather.4.cloned.1.call-start = ((), (), s32[]{:S(2)}) async-start(), calls=%async_computation.4 | async-start | bytes 1880064 | tf_op jit(solution)/shard_map/all_gather | solution.py:50
  9.0 271.0 %all-reduce.19.cloned.1.call-start = ((), (), s32[]{:S(2)}) async-start(), calls=%async_computation.5 | async-start | bytes 6881280 | tf_op jit(solution)/shard_map/psum | solution.py:112
  75.2 45.1 %copy-start.21 = (f32[768]{0:T(1024)}, f32[768]{0:T(1024)S(1)}, u32[]{:S(2)}) copy-start(f32[768]{0:T(1024)S(1)} %convert_element_type.172) | copy-start | bytes 9220
  83.4 36.9 %copy-start.10 = (f32[8,280]{1,0:T(8,128)}, f32[8,280]{1,0:T(8,128)S(1)}, u32[]{:S(2)}) copy-start(f32[8,280]{1,0:T(8,128)S(1)} %broadcast_multiply_fusion.1) | copy-start | bytes 26884
  130.7 9.5 copy-start.28
  130.7 9.5 copy-start.29
  180.2 9.5 copy-start.39
  180.2 12.1 %copy-start.37 = (bf16[768]{0:T(1024)(128)(2,1)S(1)}, bf16[768]{0:T(1024)(128)(2,1)}, u32[]{:S(2)}) copy-start(bf16[768]{0:T(1024)(128)(2,1)} %get-tuple-element.162) | copy-start | bytes 4612
  180.2 12.7 %copy-start.32 = (f32[1536]{0:T(1024)S(1)}, f32[1536]{0:T(1024)}, u32[]{:S(2)}) copy-start(f32[1536]{0:T(1024)} %param.31) | copy-start | bytes 18436
  186.2 138.3 %all-gather.6.cloned.1.call-start = ((), (), s32[]{:S(2)}) async-start(), calls=%async_computation.6 | async-start | bytes 2506752 | tf_op jit(solution)/shard_map/all_gather | solution.py:52
  187.9 188.4 %all-gather.8.cloned.1.call-start = ((), (), s32[]{:S(2)}) async-start(), calls=%async_computation.7 | async-start | bytes 2506752 | tf_op jit(solution)/shard_map/all_gather | solution.py:53
  189.7 307.3 %all-reduce.21.cloned.1.call-start = ((), (), s32[]{:S(2)}) async-start(), calls=%async_computation.8 | async-start | bytes 6881280 | tf_op jit(solution)/shard_map/psum | solution.py:137
  280.0 3.3 copy-start.1
  324.5 18.9 %copy-start.25 = (f32[1536]{0:T(1024)S(1)}, f32[1536]{0:T(1024)}, u32[]{:S(2)}) copy-start(f32[1536]{0:T(1024)} %convert_convert_fusion) | copy-start | bytes 18436
  338.5 5.0 copy-start.6
  376.3 18.8 %copy-start.40 = (bf16[768,1536]{1,0:T(8,128)(2,1)S(1)}, bf16[768,1536]{1,0:T(8,128)(2,1)}, u32[]{:S(2)}) copy-start(bf16[768,1536]{1,0:T(8,128)(2,1)} %all-gather.6.cloned.1.call-done) | copy-start | bytes 7077892
  405.2 363.4 %all-reduce.23.cloned.1.call-start = ((), (), s32[]{:S(2)}) async-start(), calls=%async_computation.13 | async-start | bytes 13762560 | tf_op jit(solution)/shard_map/psum | solution.py:120
  497.0 6.4 copy-start.15
  497.0 6.4 copy-start.2
  497.0 6.4 copy-start.5
  497.0 6.4 copy-start.19
  497.0 6.4 copy-start.23
  503.4 5.6 copy-start.8
  503.4 5.6 copy-start.17
  509.0 7.6 copy-start.9
  513.9 2.8 copy-start.3
  587.6 7.2 copy-start.41
  591.9 2.9 copy-start.7
  602.5 7.7 copy-start.20
  602.5 7.7 copy-start.24
  602.5 7.7 copy-start.35
  602.5 244.1 %reduce-scatter.7.cloned.1.call-start = ((), (), s32[]{:S(2)}) async-start(), calls=%async_computation.10 | async-start | bytes 1253376 | tf_op jit(solution)/shard_map/reduce_scatter | solution.py:203
  610.2 12.8 %copy-start.18 = (f32[8,280]{1,0:T(8,128)S(1)}, f32[8,280]{1,0:T(8,128)}, u32[]{:S(2)}) copy-start(f32[8,280]{1,0:T(8,128)} %fusion.108) | copy-start | bytes 26884
  610.2 299.5 %reduce-scatter.9.cloned.1.call-start = ((), (), s32[]{:S(2)}) async-start(), calls=%async_computation.11 | async-start | bytes 5013504 | tf_op jit(solution)/shard_map/reduce_scatter | solution.py:204
  622.8 11.4 %copy-start.11 = (f32[8,280]{1,0:T(8,128)S(1)}, f32[8,280]{1,0:T(8,128)}, u32[]{:S(2)}) copy-start(f32[8,280]{1,0:T(8,128)} %copy-done.10) | copy-start | bytes 26884
  622.8 11.4 %copy-start.16 = (f32[8,280]{1,0:T(8,128)S(1)}, f32[8,280]{1,0:T(8,128)}, u32[]{:S(2)}) copy-start(f32[8,280]{1,0:T(8,128)} %fusion.109) | copy-start | bytes 26884
  622.9 11.4 %copy-start.22 = (f32[768]{0:T(1024)S(1)}, f32[768]{0:T(1024)}, u32[]{:S(2)}) copy-start(f32[768]{0:T(1024)} %copy-done.21) | copy-start | bytes 9220
  622.9 11.4 %copy-start.34 = (f32[768]{0:T(1024)S(1)}, f32[768]{0:T(1024)}, u32[]{:S(2)}) copy-start(f32[768]{0:T(1024)} %convert_element_type.174) | copy-start | bytes 9220
  622.9 366.0 %reduce-scatter.11.cloned.1.call-start = ((), (), s32[]{:S(2)}) async-start(), calls=%async_computation.12 | async-start | bytes 5013504 | tf_op jit(solution)/shard_map/reduce_scatter | solution.py:205
  634.0 14.1 %copy-start.36 = (bf16[768]{0:T(1024)(128)(2,1)S(1)}, bf16[768]{0:T(1024)(128)(2,1)}, u32[]{:S(2)}) copy-start(bf16[768]{0:T(1024)(128)(2,1)} %get-tuple-element.167) | copy-start | bytes 4612
  634.0 426.6 %reduce-scatter.5.cloned.1.call-start = ((), (), s32[]{:S(2)}) async-start(), calls=%async_computation.9 | async-start | bytes 3760128 | tf_op jit(solution)/shard_map/reduce_scatter | solution.py:202
  648.7 124.1 %copy-start.13 = (f32[8,280]{1,0:T(8,128)S(1)}, f32[8,280]{1,0:T(8,128)}, u32[]{:S(2)}) copy-start(f32[8,280]{1,0:T(8,128)} %copy-done.12) | copy-start | bytes 26884
  768.6 4.2 copy-start.4
  768.6 8.5 copy-start.26
  768.6 8.5 copy-start.27
  768.6 8.5 copy-start.30
  768.6 8.5 copy-start.31
  (4 other events, 3.4 us)
Sparse Core Ops, SparseCore 0:
  10.9 40.4 all-gather.3
  186.3 93.6 all-reduce.18
  282.9 41.6 all-gather.5
  327.3 41.0 all-gather.7
  405.3 91.6 all-reduce.20
  602.6 165.9 all-reduce.22
  772.8 58.0 reduce-scatter.6
  835.4 74.2 reduce-scatter.8
  914.1 74.7 reduce-scatter.10
  993.2 67.3 reduce-scatter.4
where the time goes:
time: 1080 us; the launch traced here: 1070 us
  waiting for transfers between devices  535 us (50%)
  matrix products  194 us (18%)
  other arithmetic  135 us (12%)
  blocking collectives  132 us (12%)
  local copies, waits for them, and re-layouts  52.8 us (5%)
  between operations  16.4 us (2%)
    psum x1, waiting for transfers between devices, per_device(): mlp_sum = lax.psum(down_part.astype(jnp.bfloat16), 'mp').astype(jnp.float32)  115 us
    unnamed x2, blocking collectives  107 us
    psum x1, waiting for transfers between devices, per_device(): lax.psum(proj_part.astype(jnp.bfloat16), 'mp').astype(jnp.float32)  86.5 us
    psum x1, waiting for transfers between devices, per_device(): lax.psum(jnp.einsum('psf,df->psd', d_pre, up_back, preferred_element_type...  81.6 us
    reduce_scatter x1, waiting for transfers between devices, per_device(): lax.psum_scatter(grad_w_down, 'dp', scatter_dimension=1, tiled=True)  79.2 us
    reduce_scatter x1, waiting for transfers between devices, per_device(): lax.psum_scatter(grad_w_qkv, 'dp', scatter_dimension=0, tiled=True)  71.6 us
    reduce_scatter x1, waiting for transfers between devices, per_device(): lax.psum_scatter(grad_w_up, 'dp', scatter_dimension=0, tiled=True)  63 us
    all_gather x1, waiting for transfers between devices, per_device(): lax.all_gather(w_up.astype(low_type), 'dp', axis=0, tiled=True)  37.8 us
  transfers between devices with their start and end apart: 10, of which 7 were waited for; matrix products, arithmetic and copies ran while one was open for 16% of the time, Pallas kernels for 0%

commit v1 on v0

v1 whole, which is shorter than its diff:
```python
import jax
import jax.numpy as jnp
from jax import lax
from jax.sharding import PartitionSpec as P

HEADS = 12
HEAD_DIM = 64
TEXT = 40
LOW = jnp.bfloat16
F32 = jnp.float32


def normalize(values, gain, shift):
    center = values - jnp.mean(values, axis=-1, keepdims=True)
    spread = jnp.mean(center * center, axis=-1, keepdims=True)
    return center * lax.rsqrt(spread + 1e-06) * gain + shift


def norm_back(values, gain, incoming):
    center = values - jnp.mean(values, axis=-1, keepdims=True)
    spread = jnp.mean(center * center, axis=-1, keepdims=True)
    r = lax.rsqrt(spread + 1e-06)
    xhat = center * r
    dg = incoming * gain
    d_values = r * (
        dg - jnp.mean(dg, axis=-1, keepdims=True) - xhat * jnp.mean(dg * xhat, axis=-1, keepdims=True)
    )
    axes = tuple(range(values.ndim - 1))
    return d_values, jnp.sum(incoming * xhat, axis=axes), jnp.sum(incoming, axis=axes)


def per_device(
    patch_counts, tokens, cotangent, attn_gain, attn_shift, w_qkv, b_qv, w_proj, b_proj,
    ffn_gain, ffn_shift, w_up, b_up, w_down, b_down,
):
    pairs_all, rows, width = tokens.shape
    n_mp = lax.axis_size("mp")
    n_dp = lax.axis_size("dp")
    pairs = pairs_all // n_mp
    part = w_qkv.shape[0]
    lw = w_qkv.shape[2]
    fw = w_up.shape[1]
    mine = lax.axis_index("mp")
    scale = HEAD_DIM ** (-0.5)
    tokens_here = lax.dynamic_slice_in_dim(tokens, mine * pairs, pairs, 0)
    cot_here = lax.dynamic_slice_in_dim(cotangent, mine * pairs, pairs, 0)
    counts = lax.dynamic_slice_in_dim(patch_counts, mine * pairs, pairs, 0)

    first = jnp.concatenate([w_qkv.astype(LOW).reshape(part, 3 * lw), w_proj.astype(LOW).T], axis=1)
    second = jnp.concatenate([w_up.astype(LOW), w_down.astype(LOW).T], axis=1)
    vectors = jnp.stack([attn_gain, attn_shift, b_proj, ffn_gain, ffn_shift, b_down]).astype(LOW)
    vec_full = lax.all_gather(vectors, "dp", axis=1, tiled=True).astype(F32)
    bias_mine = jnp.concatenate([b_qv.reshape(-1), b_up]).astype(LOW)
    bias_all = lax.all_gather(bias_mine, "mp", axis=0).astype(F32)
    full_one = lax.all_gather(first, ("mp", "dp"), axis=0, tiled=True).reshape(n_mp, width, 4 * lw)
    full_two = lax.all_gather(second, ("mp", "dp"), axis=0, tiled=True).reshape(n_mp, width, 2 * fw)
    qkv_full = full_one[:, :, : 3 * lw].reshape(n_mp, width, 3, lw)
    proj_t = full_one[:, :, 3 * lw :]
    up_full = full_two[:, :, :fw]
    down_t = full_two[:, :, fw:]
    gain_one, shift_one, proj_bias, gain_two, shift_two, down_bias = [vec_full[i] for i in range(6)]
    bias_q = bias_all[:, :lw]
    bias_v = bias_all[:, lw : 2 * lw]
    up_bias = bias_all[:, 2 * lw :]

    valid = (jnp.arange(rows, dtype=jnp.int32)[None, :] < (TEXT + counts)[:, None]).astype(F32)
    inputs = tokens_here.astype(F32)
    n_one = normalize(inputs, gain_one, shift_one).astype(LOW)
    qkv = jnp.einsum("psd,mdtc->tpsmc", n_one, qkv_full, preferred_element_type=F32)
    heads = HEADS // n_mp

    def split(a):
        return a.reshape(pairs, rows, n_mp * heads, HEAD_DIM)

    q = split((qkv[0] + bias_q).astype(LOW))
    k = split(qkv[1].astype(LOW))
    v = split((qkv[2] + bias_v).astype(LOW))
    s = jnp.einsum("bqhe,bkhe->bhqk", q, k, preferred_element_type=F32) * scale
    s = jnp.where(valid[:, None, None, :] > 0, s, -1e30)
    prob = jax.nn.softmax(s, axis=-1)
    prob_low = prob.astype(LOW)
    att = jnp.einsum("bhqk,bkhe->bqhe", prob_low, v, preferred_element_type=F32).astype(LOW)
    att = att.reshape(pairs, rows, n_mp, lw)
    proj = jnp.einsum("psmc,mdc->psd", att, proj_t, preferred_element_type=F32)
    hidden = inputs + proj + proj_bias
    n_two = normalize(hidden, gain_two, shift_two).astype(LOW)
    pre = jnp.einsum("psd,mdf->psmf", n_two, up_full, preferred_element_type=F32) + up_bias
    cdf = 0.5 * (1.0 + lax.erf(pre * (2.0 ** -0.5)))
    act = (pre * cdf).astype(LOW)
    slope = cdf + pre * jnp.exp(-0.5 * pre * pre) * 0.3989422804014327
    down = jnp.einsum("psmf,mdf->psd", act, down_t, preferred_element_type=F32)
    out_here = ((hidden + down + down_bias) * valid[:, :, None]).astype(LOW)

    up_stream = cot_here.astype(F32) * valid[:, :, None]
    up_low = up_stream.astype(LOW)
    g_b_down = jnp.sum(up_stream, axis=(0, 1))
    g_down_t = jnp.einsum("psd,psmf->mdf", up_low, act, preferred_element_type=F32)
    d_act = jnp.einsum("psd,mdf->psmf", up_low, down_t, preferred_element_type=F32)
    d_pre = (slope * d_act).astype(LOW)
    g_b_up = jnp.sum(d_pre.astype(F32), axis=(0, 1))
    g_up = jnp.einsum("psd,psmf->mdf", n_two, d_pre, preferred_element_type=F32)
    d_two = jnp.einsum("psmf,mdf->psd", d_pre, up_full, preferred_element_type=F32)
    d_norm, g_gain_two, g_shift_two = norm_back(hidden, gain_two, d_two)
    d_hidden = up_stream + d_norm
    g_b_proj = jnp.sum(d_hidden, axis=(0, 1))
    d_low = d_hidden.astype(LOW)
    g_proj_t = jnp.einsum("psd,psmc->mdc", d_low, att, preferred_element_type=F32)
    d_att = split(jnp.einsum("psd,mdc->psmc", d_low, proj_t, preferred_element_type=F32).astype(LOW))
    d_prob = jnp.einsum("bqhe,bkhe->bhqk", d_att, v, preferred_element_type=F32)
    d_v = jnp.einsum("bhqk,bqhe->bkhe", prob_low, d_att, preferred_element_type=F32)
    inner = jnp.sum(prob * d_prob, axis=-1, keepdims=True)
    d_s = (prob * (d_prob - inner)).astype(LOW)
    d_q = scale * jnp.einsum("bhqk,bkhe->bqhe", d_s, k, preferred_element_type=F32)
    d_k = scale * jnp.einsum("bhqk,bqhe->bkhe", d_s, q, preferred_element_type=F32)

    def join(a):
        return a.astype(LOW).reshape(pairs, rows, n_mp, lw)

    d_qkv = jnp.stack([join(d_q), join(d_k), join(d_v)], axis=3)
    g_b_q = jnp.sum(d_qkv[:, :, :, 0].astype(F32), axis=(0, 1))
    g_b_v = jnp.sum(d_qkv[:, :, :, 2].astype(F32), axis=(0, 1))
    g_qkv = jnp.einsum("psd,psmtc->mdtc", n_one, d_qkv, preferred_element_type=F32)
    d_one = jnp.einsum("psmtc,mdtc->psd", d_qkv, qkv_full, preferred_element_type=F32)
    d_in, g_gain_one, g_shift_one = norm_back(inputs, gain_one, d_one)
    tok_here = (d_hidden + d_in).astype(LOW)

    def both(array):
        other = lax.ppermute(array, "mp", [(0, 1), (1, 0)])
        return jnp.where(mine == 0, jnp.concatenate([array, other]), jnp.concatenate([other, array]))

    block_out = both(out_here)
    tokens_grad = both(tok_here)
    grads_two = jnp.concatenate([g_up, g_down_t], axis=2).reshape(n_mp * width, 2 * fw)
    grads_one = jnp.concatenate([g_qkv.reshape(n_mp, width, 3 * lw), g_proj_t], axis=2).reshape(n_mp * width, 4 * lw)
    red_two = lax.psum_scatter(grads_two, ("mp", "dp"), scatter_dimension=0, tiled=True)
    red_one = lax.psum_scatter(grads_one, ("mp", "dp"), scatter_dimension=0, tiled=True)
    small = jnp.concatenate([
        g_gain_one, g_shift_one, g_b_proj, g_gain_two, g_shift_two, g_b_down,
        g_b_q.reshape(-1), g_b_v.reshape(-1), g_b_up.reshape(-1)])
    small = lax.psum(small, ("mp", "dp"))
    place = lax.axis_index("dp") * part

    def piece(i):
        return lax.dynamic_slice_in_dim(small, i * width + place, part, 0)

    rest = small[6 * width :]
    o_b_q = lax.dynamic_slice_in_dim(rest, mine * lw, lw, 0)
    o_b_v = lax.dynamic_slice_in_dim(rest, (n_mp + mine) * lw, lw, 0)
    o_b_up = lax.dynamic_slice_in_dim(rest, 2 * n_mp * lw + mine * fw, fw, 0)
    return (
        block_out, tokens_grad, piece(0), piece(1),
        red_one[:, : 3 * lw].reshape(part, 3, lw), jnp.stack([o_b_q, o_b_v]),
        red_one[:, 3 * lw :].T, piece(2), piece(3), piece(4), red_two[:, :fw], o_b_up,
        red_two[:, fw:].T, piece(5),
    )


def solution(mesh):
    vec, mat = P("dp"), P("dp", "mp")
    tok = P("dp", None, None)
    in_specs = (
        vec, tok, tok, vec, vec, P("dp", None, "mp"), P(None, "mp"), P("mp", "dp"), vec, vec, vec,
        mat, P("mp"), P("mp", "dp"), vec,
    )
    out_specs = (
        tok, tok, vec, vec, P("dp", None, "mp"), P(None, "mp"), P("mp", "dp"), vec, vec, vec,
        mat, P("mp"), P("mp", "dp"), vec,
    )
    return jax.shard_map(per_device, mesh=mesh, in_specs=in_specs, out_specs=out_specs, check_vma=False)
```

time: 1080 us -> 719 us (0.67)
  waiting for transfers between devices: 535 us -> 202 us
  other arithmetic: 135 us -> 59.2 us
  local copies, waits for them, and re-layouts: 52.8 us -> 107 us
    psum x3 -> x0, waiting for transfers between devices: 283 us -> none  [the longest x1 115 us: per_device(): mlp_sum = lax.psum(down_part.astype(jnp.bfloat16), 'mp').astype(jnp.float32)]
    psum x0 -> x1, blocking collectives: none -> 116 us  [per_device(): small = lax.psum(small, ('mp', 'dp'))]
    unnamed x2 -> x0, blocking collectives: 107 us -> none
    reduce_scatter x4 -> x1, waiting for transfers between devices: 214 us -> 158 us  [per_device(): lax.psum_scatter(grads_two, ('mp', 'dp'), scatter_dimension=0, tiled=True)]
    convert_element_type x27 -> x5, other arithmetic: 76.1 us -> 21.1 us  [the longest x1 18.1 us: per_device(): d_s = (prob * (d_prob - inner)).astype(LOW)]
    reduce_sum x10 -> x1, other arithmetic: 34.6 us -> 2.35 us  [per_device(): g_b_proj = jnp.sum(d_hidden, axis=(0, 1))]
    dot_general x40 -> x17, matrix products: 194 us -> 171 us  [the longest x1 20.7 us: per_device(): d_prob = jnp.einsum('bqhe,bkhe->bhqk', d_att, v, preferred_element_type=F32)]
    concatenate x0 -> x4, local copies, waits for them, and re-layouts: none -> 22.3 us  [the longest x1 19.1 us: per_device(): jnp.concatenate([g_up, g_down_t], axis=2).reshape(n_mp * width, 2 * fw)]
  transfers between devices with their start and end apart: 10 -> 6, of which waited for: 7 -> 3; matrix products, arithmetic and copies ran while one was open for 16% -> 22% of each run, Pallas kernels for 0% -> 0%
where the time goes in v1:
time: 719 us; the launch traced here: 713 us
  waiting for transfers between devices  202 us (28%)
  matrix products  188 us (26%)
  blocking collectives  140 us (19%)
  local copies, waits for them, and re-layouts  107 us (15%)
  other arithmetic  59.2 us (8%)
  between operations  14.5 us (2%)
    reduce_scatter x1, waiting for transfers between devices, per_device(): lax.psum_scatter(grads_two, ('mp', 'dp'), scatter_dimension=0, tiled=True)  158 us
    psum x1, blocking collectives, per_device(): small = lax.psum(small, ('mp', 'dp'))  116 us
    all_gather x1, waiting for transfers between devices, per_device(): lax.all_gather(first, ('mp', 'dp'), axis=0, tiled=True)  30.6 us
    unnamed x84, local copies, waits for them, and re-layouts  22.5 us
    dot_general x1, matrix products, per_device(): d_prob = jnp.einsum('bqhe,bkhe->bhqk', d_att, v, preferred_element_type=F32)  20.7 us
    concatenate x1, local copies, waits for them, and re-layouts, per_device(): jnp.concatenate([g_up, g_down_t], axis=2).reshape(n_mp * width, 2 * fw)  19.1 us
    all_gather x1, blocking collectives, per_device(): vec_full = lax.all_gather(vectors, 'dp', axis=1, tiled=True).astype(F32)  19 us
    convert_element_type x1, other arithmetic, per_device(): d_s = (prob * (d_prob - inner)).astype(LOW)  18.1 us
  transfers between devices with their start and end apart: 6, of which 3 were waited for; matrix products, arithmetic and copies ran while one was open for 22% of the time, Pallas kernels for 0%

profile of v1, /device:TPU:8, one launch (start us, length us, event | category | flops | bytes accessed | tf_op | source)
XLA Modules:
  0.0 712.8 jit_solution(5426264129812576893)
XLA Ops:
  14.2 4.4 all-gather.1
  22.0 19.0 %all-gather = bf16[16,48,6]{1,2,0:T(8,128)(2,1)S(1)} all-gather(bf16[1,48,6]{1,2,0:T(8,128)(2,1)S(1)} %bitcast.228), channel_id=1, replica_groups=mesh['dp'=16,'mp'=2] {'dp'}, dimensions={0}, use_global_device_ids=true | all-gather | bytes 9792 | tf_op jit(solution)/shard_map/all_gather | solution.py:52
  45.6 30.6 %all-gather.5.cloned.1.call-done = bf16[1536,1536]{1,0:T(8,128)(2,1)} async-done(((bf16[48,1536]{1,0:T(8,128)(2,1)}), bf16[1536,1536]{1,0:T(8,128)(2,1)}) %all-gather.5.cloned.1.call-update) | async-done | bytes 4718608 | tf_op jit(solution)/shard_map/all_gather | solution.py:55
  76.2 2.3 slice.85
  78.4 3.8 copy.96
  82.2 7.2 %convolution_bitcast_fusion.2 = f32[3,4,280,2,384]{4,2,1,0,3:T(8,128)S(1)} fusion(bf16[2,768,3,384,1]{1,3,4,2,0:T(8,128)(2,1)} %bitcast.214, f32[768]{0:T(1024)} %get-tuple-element.68, f32[768]{0:T(1024)} %get-tuple-element.69, f32[4,280]{1,0:T(4,128)} %add_rsqrt_fusion.1, f32[4,280]{1,0:T(4,128)S(1)} %broadcast_multiply_fusion.5, ...), kind=kOutput, calls=%fused_computation.48 | convolution fusion | flops 3968778240 | bytes 15600004 | tf_op jit(solution)/shard_map/psd,mdtc->tpsmc/dot_general | solution.py:69
  89.4 3.9 copy-done.4
  93.5 2.5 copy.101
  96.0 5.2 fusion.85
  101.3 5.5 copy.100
  106.7 3.4 copy.99
  110.1 16.5 %fusion.89 = (f32[4,12,280]{2,1,0:T(8,128)S(1)}, f32[4,12,280,280]{2,3,1,0:T(8,128)}) fusion(pred[4,280]{1,0:T(4,128)(4,1)} %get-tuple-element.88, bf16[4,280,12,64]{1,3,2,0:T(8,128)(2,1)} %bitcast.207, f32[4,280,12,64]{1,3,2,0:T(8,128)} %bitcast.205, f32[12,64]{1,0:T(8,128)S(1)} %add.177), kind=kOutput, calls=%fused_computation.161 | convolution fusion | flops 498463008 | bytes 20271712 | tf_op jit(solution)/shard_map/sub | solution.py:80
  126.7 13.3 %fusion.47 = bf16[4,12,64,280]{3,2,1,0:T(8,128)(2,1)} fusion(f32[4,280,12,64]{1,3,2,0:T(8,128)} %bitcast.212, f32[12,64]{1,0:T(8,128)S(1)} %copy-done.25, f32[4,12,280,280]{2,3,1,0:T(8,128)} %get-tuple-element.90, f32[4,12,280]{2,1,0:T(8,128)S(1)} %get-tuple-element.89), kind=kOutput, calls=%fused_computation.86 | convolution fusion | flops 491796480 | bytes 20270592 | tf_op jit(solution)/shard_map/bhqk,bkhe->bqhe/dot_general | solution.py:82
  140.0 4.8 fusion.90
  145.9 13.5 %all-gather.7.cloned.1.call-done = bf16[1536,3072]{1,0:T(8,128)(2,1)} async-done(((bf16[48,3072]{1,0:T(8,128)(2,1)}), bf16[1536,3072]{1,0:T(8,128)(2,1)}) %all-gather.7.cloned.1.call-update) | async-done | bytes 9437200 | tf_op jit(solution)/shard_map/all_gather | solution.py:56
  159.3 15.5 %multiply_convert_fusion.1 = (bf16[4,280,2,1536]{3,1,2,0:T(8,128)(2,1)}, f32[4,280,2,1536]{3,1,2,0:T(8,128)}) fusion(f32[2,1536]{1,0:T(2,128)} %slice.98, bf16[2,768,3072]{2,1,0:T(8,128)(2,1)} %bitcast.229, f32[4,280,768]{2,1,0:T(8,128)S(1)} %get-tuple-element.92, f32[768]{0:T(1024)} %get-tuple-element.65, f32[768]{0:T(1024)} %get-tuple-element.66, ...), kind=kOutput, calls=%fused_computation.15 | convolution fusion | flops 5309767680 | bytes 28834176 | tf_op jit(solution)/shard_map/psd,mdf->psmf/dot_general | solution.py:87
  174.9 14.2 %convert_reduce_fusion = (f32[2,1536]{1,0:T(2,128)}, bf16[4,280,2,1536]{3,1,2,0:T(8,128)(2,1)}) fusion(bf16[2,768,3072]{2,1,0:T(8,128)(2,1)S(1)} %bitcast.231, f32[4,280]{1,0:T(4,128)S(1)} %copy-done.15, bf16[8,280,768]{2,1,0:T(8,128)(2,1)S(1)} %copy-done.9, s32[]{:T(128)S(6)} %select_n.49, f32[4,280,2,1536]{3,1,2,0:T(8,128)} %get-tuple-element.104, ...), kind=kOutput, calls=%fused_computation.14 | convolution fusion | flops 5332128768 | bytes 27113476 | tf_op jit(solution)/shard_map/psd,mdf->psmf/dot_general | solution.py:98
  189.1 9.3 %fusion.36 = (f32[768]{0:T(1024)}, f32[4,280]{1,0:T(4,128)S(1)}, f32[4,280]{1,0:T(4,128)S(1)}, f32[768]{0:T(1024)}, f32[4,280,768,1]{2,1,3,0:T(8,128)S(1)}) fusion(f32[4,280,768]{2,1,0:T(8,128)S(1)} %get-tuple-element.92, f32[4,280]{1,0:T(4,128)S(1)} %copy-done.13, f32[4,280]{1,0:T(4,128)S(1)} %broadcast_multiply_fusion.4, f32[768]{0:T(1024)S(1)} %copy-done.20, ...), kind=kOutput, calls=%fused_computation.70 | convolution fusion | flops 5292560384 | bytes 18512640 | tf_op jit(solution)/shard_map/psmf,mdf->psd/dot_general | solution.py:102
  198.4 2.4 fusion.84
  200.8 5.1 convolution_convert_fusion
  205.9 3.2 fusion.62
  209.1 4.0 copy.104
  213.1 13.0 %convert_reduce_fusion.2 = (f32[12,64]{1,0:T(8,128)}, bf16[4,12,64,280]{3,2,1,0:T(8,128)(2,1)}) fusion(bf16[4,280,12,64]{1,3,2,0:T(8,128)(2,1)} %bitcast.220, f32[4,12,280,280]{2,3,1,0:T(8,128)} %get-tuple-element.90, f32[4,12,280]{2,1,0:T(8,128)S(1)} %get-tuple-element.89), kind=kOutput, calls=%fused_computation.36 | convolution fusion | flops 491795712 | bytes 18550272 | tf_op jit(solution)/shard_map/bhqk,bqhe->bkhe/dot_general | solution.py:110
  226.1 20.7 %multiply_reduce_fusion = (f32[4,12,280]{2,1,0:T(8,128)}, f32[4,12,280,280]{2,3,1,0:T(8,128)}) fusion(f32[4,12,280,280]{2,3,1,0:T(8,128)} %get-tuple-element.90, f32[4,12,280]{2,1,0:T(8,128)S(1)} %get-tuple-element.89, bf16[4,280,12,64]{1,3,2,0:T(8,128)(2,1)} %bitcast.221, f32[4,280,12,64]{1,3,2,0:T(8,128)} %bitcast.213, f32[12,64]{1,0:T(8,128)} %add.173), kind=kOutput, calls=%fused_computation.2 | convolution fusion | flops 494686080 | bytes 35377152 | tf_op jit(solution)/shard_map/bqhe,bkhe->bhqk/dot_general | solution.py:109
  246.8 18.1 %multiply_convert_fusion = bf16[4,12,280,280]{2,3,1,0:T(8,128)(2,1)} fusion(f32[4,12,280,280]{2,3,1,0:T(8,128)} %get-tuple-element.95, f32[4,12,280]{2,1,0:T(8,128)} %get-tuple-element.94, f32[4,12,280,280]{2,3,1,0:T(8,128)} %get-tuple-element.90, f32[4,12,280]{2,1,0:T(8,128)S(1)} %get-tuple-element.89), kind=kLoop, calls=%fused_computation.1 | loop fusion | flops 15052800 | bytes 37739520 | tf_op jit(solution)/shard_map/convert_element_type | solution.py:112
  264.9 10.6 %multiply_convert_fusion.2 = bf16[4,12,64,280]{3,2,1,0:T(8,128)(2,1)} fusion(bf16[4,12,280,280]{2,3,1,0:T(8,128)(2,1)} %multiply_convert_fusion, f32[4,280,12,64]{1,3,2,0:T(8,128)} %bitcast.206, f32[12,64]{1,0:T(8,128)S(1)} %add.177), kind=kOutput, calls=%fused_computation.38 | convolution fusion | flops 485130240 | bytes 12690432 | tf_op jit(solution)/shard_map/bhqk,bqhe->bkhe/dot_general | solution.py:114
  275.5 8.4 %convert_reduce_fusion.3 = (f32[12,64]{1,0:T(8,128)S(1)}, bf16[4,12,64,280]{3,2,1,0:T(8,128)(2,1)}) fusion(bf16[4,280,12,64]{1,3,2,0:T(8,128)(2,1)} %bitcast.208, bf16[4,12,280,280]{2,3,1,0:T(8,128)(2,1)} %multiply_convert_fusion), kind=kOutput, calls=%fused_computation.37 | convolution fusion | flops 485129472 | bytes 10970112 | tf_op jit(solution)/shard_map/bhqk,bkhe->bqhe/dot_general | solution.py:113
  283.8 3.0 copy.115
  286.9 3.2 copy.116
  290.0 4.0 copy.110
  294.1 4.2 copy.108
  298.3 4.5 copy.109
  302.8 11.0 %fusion.44 = f32[2,768,3,384]{1,3,0,2:T(8,128)} fusion(f32[768]{0:T(1024)S(1)} %copy-done.30, f32[768]{0:T(1024)S(1)} %copy-done.19, f32[4,280]{1,0:T(4,128)S(1)} %copy-done.12, f32[4,280]{1,0:T(4,128)S(1)} %copy-done.11, bf16[8,280,768]{2,1,0:T(8,128)(2,1)} %param.16, s32[]{:T(128)S(6)} %select_n.49, bf16[4,280,2,1,384]{4,1,3,0,2:T(8,128)(2,1)} %copy.110, ...), kind=kOutput, calls=%fused_computation.85 | convolution fusion | flops 3973939200 | bytes 13974276 | tf_op jit(solution)/shard_map/psd,psmtc->mdtc/dot_general | solution.py:122
  313.8 11.4 %copy.113 = f32[2,768,3,384]{1,0,3,2:T(2,128)} copy(f32[2,768,3,384]{1,3,0,2:T(8,128)} %fusion.44) | data formatting | bytes 14155776 | tf_op jit(solution)/shard_map/psd,psmtc->mdtc/transpose | solution.py:122
  325.2 6.4 copy.152
  331.6 8.4 %pad_maximum_fusion.1 = f32[1536,1536]{0,1:T(8,128)} fusion(f32[1536,384]{0,1:T(8,128)} %copy.116, f32[1536,1152]{0,1:T(8,128)} %bitcast.203), kind=kLoop, calls=%fused_computation.21 | loop fusion | flops 2359296 | bytes 18874368 | tf_op jit(solution)/shard_map/concatenate | solution.py:134
  340.0 9.6 %copy.144 = f32[1536,1536]{1,0:T(8,128)} copy(f32[1536,1536]{0,1:T(8,128)} %pad_maximum_fusion.1) | data formatting | bytes 18874368
  350.3 9.8 %convolution_bitcast_fusion = f32[2,768,1536]{1,2,0:T(8,128)S(1)} fusion(bf16[4,280,2,1536]{3,1,2,0:T(8,128)(2,1)} %get-tuple-element.103, f32[4,280]{1,0:T(4,128)S(1)} %copy-done.16, bf16[8,280,768]{2,1,0:T(8,128)(2,1)} %param.17, s32[]{:T(128)S(6)} %select_n.49), kind=kOutput, calls=%fused_computation.22 | convolution fusion | flops 5287403520 | bytes 18043268 | tf_op jit(solution)/shard_map/psd,psmf->mdf/dot_general | solution.py:97
  360.1 9.7 %convolution_bitcast_fusion.1 = f32[2,768,1536]{1,2,0:T(8,128)S(1)} fusion(bf16[4,280,2,1536]{3,1,2,0:T(8,128)(2,1)} %get-tuple-element.102, f32[4,280,768]{2,1,0:T(8,128)S(1)} %get-tuple-element.92, f32[768]{0:T(1024)S(1)} %copy-done.29, f32[768]{0:T(1024)S(1)} %copy-done.21, f32[4,280]{1,0:T(4,128)S(1)} %copy-done.14, ...), kind=kOutput, calls=%fused_computation.23 | convolution fusion | flops 5289123840 | bytes 19774208 | tf_op jit(solution)/shard_map/psd,psmf->mdf/dot_general | solution.py:101
  369.8 7.1 pad_maximum_fusion
  376.9 19.1 %copy.118 = f32[2,768,3072]{2,1,0:T(8,128)} copy(f32[2,768,3072]{1,2,0:T(8,128)} %pad_maximum_fusion) | data formatting | bytes 37748736 | tf_op jit(solution)/shard_map/concatenate | solution.py:133
  396.7 10.4 %fusion.39 = bf16[4,280,768]{2,1,0:T(8,128)(2,1)} fusion(f32[4,280,768]{2,1,0:T(8,128)S(1)} %get-tuple-element.92, bf16[4,280,2,1536]{3,1,2,0:T(8,128)(2,1)} %get-tuple-element.103, bf16[2,768,3072]{2,1,0:T(8,128)(2,1)} %bitcast.230, f32[4,280]{1,0:T(4,128)S(1)} %copy-done.16, f32[768]{0:T(1024)S(1)} %copy-done.28), kind=kOutput, calls=%fused_computation.74 | convolution fusion | flops 5288263680 | bytes 16768384 | tf_op jit(solution)/shard_map/psmf,mdf->psd/dot_general | solution.py:91
  408.6 5.1 fusion.33
  416.1 116.4 %psum.7 = f32[9216]{0:T(1024)S(1)} all-reduce(f32[9216]{0:T(1024)S(1)} %constant_dynamic-update-slice_fusion), channel_id=1, replica_groups=mesh['dp'=16,'mp'=2] {'mp','dp'}, use_global_device_ids=true, to_apply=%region_20.21 | all-reduce | flops 9216 | bytes 73728 | tf_op jit(solution)/shard_map/psum | solution.py:140
  534.5 3.8 maximum_select_fusion
  538.3 3.9 maximum_select_fusion.1
  545.9 158.2 %reduce-scatter.5.cloned.1.call-done = f32[48,3072]{1,0:T(8,128)} async-done(((f32[1536,3072]{1,0:T(8,128)}), f32[48,3072]{1,0:T(8,128)}) %reduce-scatter.5.cloned.1.call-update) | async-done | bytes 589840 | tf_op jit(solution)/shard_map/reduce_scatter | solution.py:135
  704.1 1.9 slice_bitcast_fusion.11
  (145 shorter events, 27.0 us)
Async XLA Ops:
  7.2 36.5 %copy-start.2 = (bf16[8,280,768]{2,1,0:T(8,128)(2,1)S(1)}, bf16[8,280,768]{2,1,0:T(8,128)(2,1)}, u32[]{:S(2)}) copy-start(bf16[8,280,768]{2,1,0:T(8,128)(2,1)} %param.16) | copy-start | bytes 10321924
  7.2 35.7 %copy-start.33 = (s32[8]{0:T(128)S(1)}, s32[8]{0:T(128)}, u32[]{:S(2)}) copy-start(s32[8]{0:T(128)} %param.15) | copy-start | bytes 100
  7.2 69.0 %all-gather.5.cloned.1.call-start = ((), (), s32[]{:S(2)}) async-start(), calls=%async_computation.2 | async-start | bytes 4866048 | tf_op jit(solution)/shard_map/all_gather | solution.py:55
  10.0 149.4 %all-gather.7.cloned.1.call-start = ((), (), s32[]{:S(2)}) async-start(), calls=%async_computation.3 | async-start | bytes 9732096 | tf_op jit(solution)/shard_map/all_gather | solution.py:56
  12.7 529.4 %reduce-scatter.7.cloned.1.call-start = ((), (), s32[]{:S(2)}) async-start(), calls=%async_computation.5 | async-start | bytes 9732096
  43.6 38.6 %copy-start.10 = (f32[4,280]{1,0:T(4,128)}, f32[4,280]{1,0:T(4,128)S(1)}, u32[]{:S(2)}) copy-start(f32[4,280]{1,0:T(4,128)S(1)} %broadcast_multiply_fusion.5) | copy-start | bytes 13444
  89.4 3.9 copy-start.4
  110.1 16.6 %copy-start.25 = (f32[12,64]{1,0:T(8,128)S(1)}, f32[12,64]{1,0:T(8,128)}, u32[]{:S(2)}) copy-start(f32[12,64]{1,0:T(8,128)} %add.173) | copy-start | bytes 9220
  126.7 13.3 %copy-start.31 = (f32[768]{0:T(1024)S(1)}, f32[768]{0:T(1024)}, u32[]{:S(2)}) copy-start(f32[768]{0:T(1024)} %get-tuple-element.67) | copy-start | bytes 9220
  159.3 15.5 %copy-start.9 = (bf16[8,280,768]{2,1,0:T(8,128)(2,1)S(1)}, bf16[8,280,768]{2,1,0:T(8,128)(2,1)}, u32[]{:S(2)}) copy-start(bf16[8,280,768]{2,1,0:T(8,128)(2,1)} %param.17) | copy-start | bytes 10321924
  159.3 15.5 %copy-start.15 = (f32[4,280]{1,0:T(4,128)S(1)}, f32[4,280]{1,0:T(4,128)}, u32[]{:S(2)}) copy-start(f32[4,280]{1,0:T(4,128)} %get-tuple-element.87) | copy-start | bytes 13444
  159.3 15.5 %copy-start.23 = (f32[2,1536]{1,0:T(2,128)S(1)}, f32[2,1536]{1,0:T(2,128)}, u32[]{:S(2)}) copy-start(f32[2,1536]{1,0:T(2,128)} %slice.98) | copy-start | bytes 36868
  159.3 15.5 %copy-start.32 = (bf16[1536,3072]{1,0:T(8,128)(2,1)S(1)}, bf16[1536,3072]{1,0:T(8,128)(2,1)}, u32[]{:S(2)}) copy-start(bf16[1536,3072]{1,0:T(8,128)(2,1)} %all-gather.7.cloned.1.call-done) | copy-start | bytes 28311556
  174.8 14.2 %copy-start.13 = (f32[4,280]{1,0:T(4,128)S(1)}, f32[4,280]{1,0:T(4,128)}, u32[]{:S(2)}) copy-start(f32[4,280]{1,0:T(4,128)} %add_rsqrt_fusion) | copy-start | bytes 13444
  174.9 14.2 %copy-start.20 = (f32[768]{0:T(1024)S(1)}, f32[768]{0:T(1024)}, u32[]{:S(2)}) copy-start(f32[768]{0:T(1024)} %get-tuple-element.66) | copy-start | bytes 9220
  200.8 5.1 copy-start
  200.8 5.1 copy-start.34
  294.1 8.7 %copy-start.11 = (f32[4,280]{1,0:T(4,128)S(1)}, f32[4,280]{1,0:T(4,128)}, u32[]{:S(2)}) copy-start(f32[4,280]{1,0:T(4,128)} %copy-done.10) | copy-start | bytes 13444
  294.1 8.7 %copy-start.12 = (f32[4,280]{1,0:T(4,128)S(1)}, f32[4,280]{1,0:T(4,128)}, u32[]{:S(2)}) copy-start(f32[4,280]{1,0:T(4,128)} %add_rsqrt_fusion.1) | copy-start | bytes 13444
  294.1 8.7 %copy-start.19 = (f32[768]{0:T(1024)S(1)}, f32[768]{0:T(1024)}, u32[]{:S(2)}) copy-start(f32[768]{0:T(1024)} %get-tuple-element.69) | copy-start | bytes 9220
  294.1 8.7 %copy-start.30 = (f32[768]{0:T(1024)S(1)}, f32[768]{0:T(1024)}, u32[]{:S(2)}) copy-start(f32[768]{0:T(1024)} %get-tuple-element.68) | copy-start | bytes 9220
  349.6 0.7 copy-start.16
  349.6 354.5 %reduce-scatter.5.cloned.1.call-start = ((), (), s32[]{:S(2)}) async-start(), calls=%async_computation.4 | async-start | bytes 19464192 | tf_op jit(solution)/shard_map/reduce_scatter | solution.py:135
  350.3 9.8 %copy-start.14 = (f32[4,280]{1,0:T(4,128)S(1)}, f32[4,280]{1,0:T(4,128)}, u32[]{:S(2)}) copy-start(f32[4,280]{1,0:T(4,128)} %add_rsqrt_fusion) | copy-start | bytes 13444
  350.3 9.8 %copy-start.21 = (f32[768]{0:T(1024)S(1)}, f32[768]{0:T(1024)}, u32[]{:S(2)}) copy-start(f32[768]{0:T(1024)} %get-tuple-element.66) | copy-start | bytes 9220
  350.3 9.8 %copy-start.29 = (f32[768]{0:T(1024)S(1)}, f32[768]{0:T(1024)}, u32[]{:S(2)}) copy-start(f32[768]{0:T(1024)} %get-tuple-element.65) | copy-start | bytes 9220
  396.0 0.7 copy-start.28
  396.7 11.9 %copy-start.3 = (bf16[8,280,768]{2,1,0:T(8,128)(2,1)S(1)}, bf16[8,280,768]{2,1,0:T(8,128)(2,1)}, u32[]{:S(2)}) copy-start(bf16[8,280,768]{2,1,0:T(8,128)(2,1)} %param.16) | copy-start | bytes 10321924
  396.7 11.9 %copy-start.5 = (bf16[2,768,1152]{1,2,0:T(8,128)(2,1)S(1)}, bf16[2,768,1152]{1,2,0:T(8,128)(2,1)}, u32[]{:S(2)}) copy-start(bf16[2,768,1152]{1,2,0:T(8,128)(2,1)} %copy.96) | copy-start | bytes 10616836
  396.7 11.9 %copy-start.6 = (bf16[4,280,2,1,384]{4,1,3,0,2:T(8,128)(2,1)S(1)}, bf16[4,280,2,1,384]{4,1,3,0,2:T(8,128)(2,1)}, u32[]{:S(2)}) copy-start(bf16[4,280,2,1,384]{4,1,3,0,2:T(8,128)(2,1)} %copy.110) | copy-start | bytes 5160964
  396.7 11.9 %copy-start.7 = (bf16[4,280,2,1,384]{4,1,3,0,2:T(8,128)(2,1)S(1)}, bf16[4,280,2,1,384]{4,1,3,0,2:T(8,128)(2,1)}, u32[]{:S(2)}) copy-start(bf16[4,280,2,1,384]{4,1,3,0,2:T(8,128)(2,1)} %copy.108) | copy-start | bytes 5160964
  396.7 11.9 %copy-start.8 = (bf16[4,280,2,1,384]{4,1,3,0,2:T(8,128)(2,1)S(1)}, bf16[4,280,2,1,384]{4,1,3,0,2:T(8,128)(2,1)}, u32[]{:S(2)}) copy-start(bf16[4,280,2,1,384]{4,1,3,0,2:T(8,128)(2,1)} %copy.109) | copy-start | bytes 5160964
  407.1 127.4 %collective-permute-start = (bf16[4,280,768]{2,1,0:T(8,128)(2,1)}, bf16[4,280,768]{2,1,0:T(8,128)(2,1)S(1)}, u32[]{:S(2)}, u32[]{:S(2)}) collective-permute-start(bf16[4,280,768]{2,1,0:T(8,128)(2,1)} %fusion.39), channel_id=1, source_target_pairs={{0,1},{1,0},{2,3},{3,2},{4,5},{5,4},{6,7},{7,6},{8,9},{9,8},{10,11... | collective-permute-start | bytes 5160968 | tf_op jit(solution)/shard_map/ppermute | solution.py:128
  408.6 5.1 copy-start.1
  413.7 2.1 copy-start.22
  413.7 2.1 copy-start.24
  413.7 2.2 copy-start.18
  413.7 2.2 copy-start.27
  413.8 2.2 copy-start.26
  413.8 2.3 copy-start.17
  415.1 123.2 %collective-permute-start.1 = (bf16[4,280,768]{2,1,0:T(8,128)(2,1)S(1)}, bf16[4,280,768]{2,1,0:T(8,128)(2,1)}, u32[]{:S(2)}, u32[]{:S(2)}) collective-permute-start(bf16[4,280,768]{2,1,0:T(8,128)(2,1)S(1)} %fusion.32), channel_id=1, source_target_pairs={{0,1},{1,0},{2,3},{3,2},{4,5},{5,4},{6,7},{7,6},{8,9},{9,8},{10,11... | collective-permute-start | bytes 5160968 | tf_op jit(solution)/shard_map/ppermute | solution.py:128
Sparse Core Ops, SparseCore 0:
  11.5 64.6 all-gather.4
  79.6 79.6 all-gather.6
  349.8 143.7 reduce-scatter.6
  499.8 204.2 reduce-scatter.4

commit v2 on v1

v2 whole, which is shorter than its diff:
```python
import functools

import jax
import jax.numpy as jnp
from jax import lax
from jax.experimental import pallas as pl
from jax.experimental.pallas import tpu as pltpu
from jax.sharding import PartitionSpec as P

HEADS = 12
HEAD_DIM = 64
TEXT = 40
LOW = jnp.bfloat16
F32 = jnp.float32
EXTRA = 128
NT = (((1,), (1,)), ((), ()))
NN = (((1,), (0,)), ((), ()))


def dot(a, b, dims=NN):
    return lax.dot_general(a, b, dims, preferred_element_type=F32)


def moments(v):
    center = v - jnp.mean(v, axis=-1, keepdims=True)
    spread = jnp.mean(center * center, axis=-1, keepdims=True)
    r = lax.rsqrt(spread + 1e-06)
    return center * r, r


def row_ids(rows):
    return lax.broadcasted_iota(jnp.int32, (rows, 1), 0)


def attn_kernel(lens, off, x_ref, w_ref, bias_ref, qkv_ref, att_ref, prob_ref, hid_ref, n1_ref, n2_ref, vec_ref):
    p = pl.program_id(0)
    rows, width = x_ref.shape[1], x_ref.shape[2]
    groups = w_ref.shape[0]
    lw = width // groups
    tiles = lw // 128

    @pl.when(p == 0)
    def _():
        vec_ref[...] = w_ref[0, :, 4 * lw :].astype(F32).T[:8]

    x = x_ref[0].astype(F32)
    xhat, _ = moments(x)
    n1 = (xhat * vec_ref[0:1] + vec_ref[1:2]).astype(LOW)
    n1_ref[0] = n1
    for m in range(groups):
        y = dot(n1, w_ref[m, :, : 3 * lw])
        base = m * 3 * lw
        qkv_ref[0, :, base : base + lw] = (y[:, :lw] + bias_ref[m, 0:1, :lw]).astype(LOW)
        qkv_ref[0, :, base + lw : base + 2 * lw] = y[:, lw : 2 * lw].astype(LOW)
        qkv_ref[0, :, base + 2 * lw : base + 3 * lw] = (
            y[:, 2 * lw :] + bias_ref[m, 0:1, lw : 2 * lw]
        ).astype(LOW)
    count = lens[p]
    keep = row_ids(rows) < count
    first = lax.broadcasted_iota(jnp.int32, (1, 128), 1) < HEAD_DIM

    def pair(hp, carry):
        base = (hp // tiles) * 3 * lw + (hp % tiles) * 128

        def cols(t):
            return pl.ds(pl.multiple_of(base + t * lw, 128), 128)

        q2 = qkv_ref[0, :, cols(0)] * 0.125
        k2 = qkv_ref[0, :, cols(1)]
        v2t = qkv_ref[0, :, cols(2)].T
        outs = []
        for h in range(2):
            qh = jnp.where(first if h == 0 else ~first, q2, 0)
            st = dot(k2, qh, NT)
            st = jnp.where(keep, st, -1e30)
            e = jnp.exp(st - jnp.max(st, axis=0, keepdims=True))
            pt = (e * (1.0 / jnp.sum(e, axis=0, keepdims=True))).astype(LOW)
            prob_ref[0, hp * 2 + h] = pt
            outs.append(dot(v2t[h * HEAD_DIM : (h + 1) * HEAD_DIM], pt))
        att_ref[0, :, pl.ds(pl.multiple_of(hp * 128, 128), 128)] = jnp.concatenate(outs, axis=0).T.astype(LOW)
        return carry

    lax.fori_loop(0, groups * tiles, pair, 0)
    proj = sum(dot(att_ref[0, :, m * lw : (m + 1) * lw], w_ref[m, :, 3 * lw : 4 * lw], NT) for m in range(groups))
    hid = x + proj + vec_ref[2:3]
    hid_ref[0] = hid
    xhat2, _ = moments(hid)
    n2_ref[0] = (xhat2 * vec_ref[3:4] + vec_ref[4:5]).astype(LOW)


def const_spec(shape):
    return pl.BlockSpec(shape, lambda *_: (0,) * len(shape), pipeline_mode=pl.Buffered(1))


def pair_spec(*shape):
    return pl.BlockSpec((1,) + shape, lambda p, *_: (p,) + (0,) * len(shape))


def attention_forward(lens, off, tokens, w_one, bias):
    pairs = lens.shape[0]
    _, rows, width = tokens.shape
    out = lambda dt, *s: jax.ShapeDtypeStruct((pairs,) + s, dt)
    return pl.pallas_call(
        attn_kernel,
        grid_spec=pltpu.PrefetchScalarGridSpec(
            num_scalar_prefetch=2,
            grid=(pairs,),
            in_specs=[
                pl.BlockSpec((1, rows, width), lambda p, lens, off: (off[0] + p, 0, 0)),
                const_spec(w_one.shape),
                const_spec(bias.shape),
            ],
            out_specs=[
                pair_spec(rows, 3 * width), pair_spec(rows, width), pair_spec(HEADS, rows, rows),
                pair_spec(rows, width), pair_spec(rows, width), pair_spec(rows, width),
                pl.BlockSpec((8, width), lambda *_: (0, 0)),
            ],
        ),
        out_shape=[
            out(LOW, rows, 3 * width), out(LOW, rows, width), out(LOW, HEADS, rows, rows),
            out(F32, rows, width), out(LOW, rows, width), out(LOW, rows, width),
            jax.ShapeDtypeStruct((8, width), F32),
        ],
        compiler_params=pltpu.CompilerParams(vmem_limit_bytes=60 * 2**20),
        name="attention_forward",
    )(lens, off, tokens, w_one, bias)


def ffn_kernel(lens, off, n2_ref, hid_ref, cot_ref, w_ref, bias_ref, vec_ref,
               out_ref, act_ref, dpre_ref, dhid_ref, dlow_ref, upl_ref, sums_ref, bsum_ref):
    p = pl.program_id(0)
    rows, width = n2_ref.shape[1], n2_ref.shape[2]
    groups = w_ref.shape[0]
    fw = w_ref.shape[2] // 2
    lw = width // groups
    step = 512
    keep = row_ids(rows) < lens[p]
    n2 = n2_ref[0]
    upl = jnp.where(keep, cot_ref[0], 0)
    upl_ref[0] = upl

    @pl.when(p == 0)
    def _():
        sums_ref[...] = jnp.zeros_like(sums_ref)
        bsum_ref[...] = jnp.zeros_like(bsum_ref)

    for m in range(groups):
        for c in range(0, fw, step):
            pre = dot(n2, w_ref[m, :, c : c + step]) + bias_ref[m, 0:1, 2 * lw + c : 2 * lw + c + step]
            cdf = 0.5 * (1.0 + lax.erf(pre * (2.0 ** -0.5)))
            at = m * fw + c
            act_ref[0, :, at : at + step] = (pre * cdf).astype(LOW)
            slope = cdf + pre * (0.3989422804014327 * jnp.exp(-0.5 * pre * pre))
            dpre = slope * dot(upl, w_ref[m, :, fw + c : fw + c + step])
            dpre_ref[0, :, at : at + step] = dpre.astype(LOW)
            bsum_ref[0:1, at : at + step] += jnp.sum(dpre, axis=0, keepdims=True)
    hid = hid_ref[0]
    down = sum(dot(act_ref[0, :, m * fw : (m + 1) * fw], w_ref[m, :, fw:], NT) for m in range(groups))
    out_ref[0] = jnp.where(keep, hid + down + vec_ref[5:6], 0.0).astype(LOW)
    dtwo = sum(dot(dpre_ref[0, :, m * fw : (m + 1) * fw], w_ref[m, :, :fw], NT) for m in range(groups))
    xhat, r = moments(hid)
    dg = dtwo * vec_ref[3:4]
    dn = r * (dg - jnp.mean(dg, axis=-1, keepdims=True) - xhat * jnp.mean(dg * xhat, axis=-1, keepdims=True))
    upf = upl.astype(F32)
    dhid = upf + dn
    dhid_ref[0] = dhid
    dlow_ref[0] = dhid.astype(LOW)
    sums_ref[0:1] += jnp.sum(dtwo * xhat, axis=0, keepdims=True)
    sums_ref[1:2] += jnp.sum(dtwo, axis=0, keepdims=True)
    sums_ref[2:3] += jnp.sum(dhid, axis=0, keepdims=True)
    sums_ref[3:4] += jnp.sum(upf, axis=0, keepdims=True)


def ffn(lens, off, n2, hid, cotangent, w_two, bias, vec):
    pairs, rows, width = n2.shape
    ff = w_two.shape[0] * w_two.shape[2] // 2
    out = lambda dt, *s: jax.ShapeDtypeStruct((pairs,) + s, dt)
    return pl.pallas_call(
        ffn_kernel,
        grid_spec=pltpu.PrefetchScalarGridSpec(
            num_scalar_prefetch=2,
            grid=(pairs,),
            in_specs=[
                pair_spec(rows, width), pair_spec(rows, width),
                pl.BlockSpec((1, rows, width), lambda p, lens, off: (off[0] + p, 0, 0)),
                const_spec(w_two.shape), const_spec(bias.shape), const_spec(vec.shape),
            ],
            out_specs=[
                pair_spec(rows, width), pair_spec(rows, ff), pair_spec(rows, ff), pair_spec(rows, width),
                pair_spec(rows, width), pair_spec(rows, width),
                pl.BlockSpec((8, width), lambda *_: (0, 0)), pl.BlockSpec((8, ff), lambda *_: (0, 0)),
            ],
        ),
        out_shape=[
            out(LOW, rows, width), out(LOW, rows, ff), out(LOW, rows, ff), out(F32, rows, width),
            out(LOW, rows, width), out(LOW, rows, width),
            jax.ShapeDtypeStruct((8, width), F32), jax.ShapeDtypeStruct((8, ff), F32),
        ],
        compiler_params=pltpu.CompilerParams(vmem_limit_bytes=60 * 2**20),
        name="feed_forward",
    )(lens, off, n2, hid, cotangent, w_two, bias, vec)


def back_kernel(lens, off, x_ref, dhid_ref, qkv_ref, prob_ref, w_ref, vec_ref,
                tok_ref, dqkv_ref, sums_ref, bsum_ref, do_ref):
    p = pl.program_id(0)
    rows, width = x_ref.shape[1], x_ref.shape[2]
    groups = w_ref.shape[0]
    lw = width // groups
    tiles = lw // 128

    @pl.when(p == 0)
    def _():
        sums_ref[...] = jnp.zeros_like(sums_ref)
        bsum_ref[...] = jnp.zeros_like(bsum_ref)

    dhid = dhid_ref[0]
    dlow = dhid.astype(LOW)
    for m in range(groups):
        do_ref[:, m * lw : (m + 1) * lw] = dot(dlow, w_ref[m, :, 3 * lw : 4 * lw]).astype(LOW)
    first = lax.broadcasted_iota(jnp.int32, (1, 128), 1) < HEAD_DIM

    def pair(hp, carry):
        base = (hp // tiles) * 3 * lw + (hp % tiles) * 128

        def cols(t):
            return pl.ds(pl.multiple_of(base + t * lw, 128), 128)

        q2 = qkv_ref[0, :, cols(0)] * 0.125
        k2t = qkv_ref[0, :, cols(1)].T
        v2 = qkv_ref[0, :, cols(2)]
        do2 = do_ref[:, pl.ds(pl.multiple_of(hp * 128, 128), 128)]
        dq_t = []
        dk = dv = 0.0
        for h in range(2):
            mine = first if h == 0 else ~first
            doh = jnp.where(mine, do2, 0)
            qh = jnp.where(mine, q2, 0)
            dpt = dot(v2, doh, NT)
            plow = prob_ref[0, hp * 2 + h]
            pt = plow.astype(F32)
            inner = jnp.sum(pt * dpt, axis=0, keepdims=True)
            dst = (pt * (dpt - inner)).astype(LOW)
            dv = dv + dot(plow, doh)
            dk = dk + dot(dst, qh)
            dq_t.append(dot(k2t[h * HEAD_DIM : (h + 1) * HEAD_DIM], dst))
        dq = (jnp.concatenate(dq_t, axis=0) * 0.125).T
        dqkv_ref[0, :, cols(0)] = dq.astype(LOW)
        dqkv_ref[0, :, cols(1)] = dk.astype(LOW)
        dqkv_ref[0, :, cols(2)] = dv.astype(LOW)
        bsum_ref[0:1, cols(0)] += jnp.sum(dq, axis=0, keepdims=True)
        bsum_ref[0:1, cols(2)] += jnp.sum(dv, axis=0, keepdims=True)
        return carry

    lax.fori_loop(0, groups * tiles, pair, 0)
    done = sum(dot(dqkv_ref[0, :, m * 3 * lw : (m + 1) * 3 * lw], w_ref[m, :, : 3 * lw], NT) for m in range(groups))
    xhat, r = moments(x_ref[0].astype(F32))
    dg = done * vec_ref[0:1]
    dn = r * (dg - jnp.mean(dg, axis=-1, keepdims=True) - xhat * jnp.mean(dg * xhat, axis=-1, keepdims=True))
    tok_ref[0] = (dhid + dn).astype(LOW)
    sums_ref[0:1] += jnp.sum(done * xhat, axis=0, keepdims=True)
    sums_ref[1:2] += jnp.sum(done, axis=0, keepdims=True)


def attention_backward(lens, off, tokens, dhid, qkv, prob, w_one, vec):
    pairs, rows, width = dhid.shape
    out = lambda dt, *s: jax.ShapeDtypeStruct((pairs,) + s, dt)
    return pl.pallas_call(
        back_kernel,
        grid_spec=pltpu.PrefetchScalarGridSpec(
            num_scalar_prefetch=2,
            grid=(pairs,),
            in_specs=[
                pl.BlockSpec((1, rows, width), lambda p, lens, off: (off[0] + p, 0, 0)),
                pair_spec(rows, width), pair_spec(rows, 3 * width), pair_spec(HEADS, rows, rows),
                const_spec(w_one.shape), const_spec(vec.shape),
            ],
            out_specs=[
                pair_spec(rows, width), pair_spec(rows, 3 * width),
                pl.BlockSpec((8, width), lambda *_: (0, 0)), pl.BlockSpec((8, 3 * width), lambda *_: (0, 0)),
            ],
            scratch_shapes=[pltpu.VMEM((rows, width), LOW)],
        ),
        out_shape=[
            out(LOW, rows, width), out(LOW, rows, 3 * width),
            jax.ShapeDtypeStruct((8, width), F32), jax.ShapeDtypeStruct((8, 3 * width), F32),
        ],
        compiler_params=pltpu.CompilerParams(vmem_limit_bytes=60 * 2**20),
        name="attention_backward",
    )(lens, off, tokens, dhid, qkv, prob, w_one, vec)
MESH_ID = pl.DeviceIdType.MESH
Z, Y, C = 4, 2, 2


def place():
    dp = lax.axis_index("dp")
    m = lax.axis_index("mp")
    c = lax.rem(dp, 2)
    y = lax.rem(dp // 2, 2)
    z = dp // 4
    return z, y, c, m


def index(z, y, c):
    return (z * Y + y) * C + c


def flips(y, c, m):
    one = (y + c * (1 - 2 * y), m + (1 - c) * (1 - 2 * m))
    two = (y + (1 - c) * (1 - 2 * y), m + c * (1 - 2 * m))
    return one, two


def greet(z, y, c, m):
    barrier = pltpu.get_barrier_semaphore()
    (y1, m1), (y2, m2) = flips(y, c, m)
    peers = [(index(lax.rem(z + k, Z), y, c), m) for k in (1, 2, 3)]
    peers += [(index(z, y1, c), m1), (index(z, y2, c), m2), (index(z, y, 1 - c), m)]
    for dp, mp in peers:
        pl.semaphore_signal(barrier, inc=1, device_id={"dp": dp, "mp": mp}, device_id_type=MESH_ID)
    pl.semaphore_wait(barrier, len(peers))
    return peers


def gather_kernel(s0, s1, s2, b_in, w_one, w_two, b_out, send, recv, bsem, local):
    z, y, c, m = place()
    (y1, m1), (y2, m2) = flips(y, c, m)
    part, cols = s1.shape
    peers = greet(z, y, c, m)
    pz, one, two, sib = peers[:3], peers[3], peers[4], peers[5]
    shards = (s0, s1, s2)

    def spot(g, dp, mp):
        rows = pl.ds(pl.multiple_of(dp * part, part), part)
        if g == 0:
            return w_one.at[mp, rows]
        return w_two.at[mp, rows, (g - 1) * cols : g * cols]

    started = []
    count = [0, 0, 0]

    def push(g, src, dp, mp, to):
        copy = pltpu.make_async_remote_copy(
            src_ref=src, dst_ref=spot(g, dp, mp), send_sem=send.at[g, count[g]],
            recv_sem=recv.at[g, mp * (Z * Y * C) + dp],
            device_id={"dp": to[0], "mp": to[1]}, device_id_type=MESH_ID,
        )
        count[g] += 1
        copy.start()
        started.append(copy)

    def arrived(g, dp, mp):
        at = spot(g, dp, mp)
        pltpu.make_async_remote_copy(
            src_ref=at, dst_ref=at, send_sem=send.at[g, 0], recv_sem=recv.at[g, mp * (Z * Y * C) + dp],
            device_id={"dp": sib[0], "mp": sib[1]}, device_id_type=MESH_ID,
        ).wait_recv()
        return at

    me = index(z, y, c)
    bias_copy = pltpu.make_async_remote_copy(
        src_ref=b_in, dst_ref=b_out.at[m], send_sem=bsem.at[0], recv_sem=bsem.at[1],
        device_id={"dp": me, "mp": 1 - m}, device_id_type=MESH_ID,
    )
    bias_copy.start()
    locals_ = [pltpu.make_async_copy(b_in, b_out.at[m], local.at[3])]
    for g in range(3):
        for to in pz + [one, two, sib]:
            push(g, shards[g], me, m, to)
        locals_.append(pltpu.make_async_copy(shards[g], spot(g, me, m), local.at[g]))
    for copy in locals_:
        copy.start()

    def stage_z(g):
        for k in (1, 3, 2):
            dp = index(lax.rem(z + k, Z), y, c)
            at = arrived(g, dp, m)
            for to in (one, two, sib):
                push(g, at, dp, m, to)

    def stage_one(g):
        for k in (0, 1, 3, 2):
            dp = index(lax.rem(z + k, Z), y1, c)
            at = arrived(g, dp, m1)
            for to in (two, sib):
                push(g, at, dp, m1, to)

    def stage_two(g):
        for k in (0, 1, 3, 2):
            for yy, mm in ((y2, m2), (1 - y, 1 - m)):
                dp = index(lax.rem(z + k, Z), yy, c)
                push(g, arrived(g, dp, mm), dp, mm, sib)

    def stage_core(g):
        for k in range(Z):
            for yy in range(Y):
                for mm in range(2):
                    arrived(g, index(k, yy, 1 - c), mm)

    stage_z(0)
    stage_one(0)
    stage_z(1)
    stage_two(0)
    stage_one(1)
    stage_z(2)
    stage_two(1)
    stage_one(2)
    stage_two(2)
    for g in range(3):
        stage_core(g)
    bias_copy.wait()
    for copy in locals_:
        copy.wait()
    for copy in started:
        copy.wait_send()


def gather_weights(first, second_a, second_b, bias):
    part, cols = second_a.shape
    vm = pl.BlockSpec(memory_space=pltpu.VMEM)
    hbm = pl.BlockSpec(memory_space=pl.ANY)
    total = Z * Y * C
    return pl.pallas_call(
        gather_kernel,
        in_specs=[vm] * 4,
        out_specs=[hbm] * 3,
        out_shape=[
            jax.ShapeDtypeStruct((2, total * part, first.shape[1]), LOW),
            jax.ShapeDtypeStruct((2, total * part, 2 * cols), LOW),
            jax.ShapeDtypeStruct((2,) + bias.shape, F32),
        ],
        scratch_shapes=[
            pltpu.SemaphoreType.DMA((3, 31)), pltpu.SemaphoreType.DMA((3, 32)),
            pltpu.SemaphoreType.DMA((2,)), pltpu.SemaphoreType.DMA((4,)),
        ],
        compiler_params=pltpu.CompilerParams(collective_id=0, has_side_effects=True, vmem_limit_bytes=32 * 2**20),
        name="gather_weights",
    )(first, second_a, second_b, bias)


def reduce_kernel(groups, with_small, *refs):
    grads = refs[:groups]
    pos = groups
    small = None
    if with_small:
        small = refs[pos]
        pos += 1
    outs = refs[pos : pos + groups]
    pos += groups
    if with_small:
        small_out = refs[pos]
        pos += 1
    per = [refs[pos + 7 * g : pos + 7 * (g + 1)] for g in range(groups)]
    pos += 7 * groups
    send, recv = refs[pos], refs[pos + 1]
    pos += 2
    z, y, c, m = place()
    (y1, m1), (y2, m2) = flips(y, c, m)
    part = outs[0].shape[0]
    peers = greet(z, y, c, m)
    pz, one, two, sib = peers[:3], peers[3], peers[4], peers[5]
    started = []
    count = [0] * groups

    def push(g, src, dst, sem, to):
        copy = pltpu.make_async_remote_copy(
            src_ref=src, dst_ref=dst, send_sem=send.at[g, count[g]], recv_sem=recv.at[g, sem],
            device_id={"dp": to[0], "mp": to[1]}, device_id_type=MESH_ID,
        )
        count[g] += 1
        copy.start()
        started.append(copy)

    def arrived(g, dst, sem):
        pltpu.make_async_remote_copy(
            src_ref=dst, dst_ref=dst, send_sem=send.at[g, 0], recv_sem=recv.at[g, sem],
            device_id={"dp": sib[0], "mp": sib[1]}, device_id_type=MESH_ID,
        ).wait_recv()

    def grad(g, zz, yy, cc, mm):
        return grads[g].at[mm, pl.ds(pl.multiple_of(index(zz, yy, cc) * part, part), part)]

    if with_small:
        sbuf, ssem = refs[pos], refs[pos + 1]

        def small_push(slot, src, to, sems):
            copy = pltpu.make_async_remote_copy(
                src_ref=src, dst_ref=sbuf.at[slot], send_sem=ssem.at[0, sems], recv_sem=ssem.at[1, sems],
                device_id={"dp": to[0], "mp": to[1]}, device_id_type=MESH_ID,
            )
            copy.start()
            return copy

        copies = [small_push(0, small, sib, 0)]

    (a1, b1), (a2, b2) = flips(y, 1 - c, m)
    order = [(3, 1 - y, 1 - m), (2, a2, b2), (1, a1, b1), (0, y, m)]
    turns = (1, 2, 3, 0)
    for slot, yy, mm in order:
        for k in turns:
            for g in range(groups):
                push(g, grad(g, lax.rem(z + k, Z), yy, 1 - c, mm), per[g][0].at[slot * Z + k], slot * Z + k, sib)

    def base(g, slot, k, yy, mm):
        arrived(g, per[g][0].at[slot * Z + k], slot * Z + k)
        return grad(g, lax.rem(z + k, Z), yy, c, mm)[...].astype(F32) + per[g][0][slot * Z + k].astype(F32)

    for slot, yy, mm in ((3, 1 - y, 1 - m), (2, y2, m2)):
        for k in turns:
            for g in range(groups):
                at = (slot - 2) * Z + k
                per[g][1][at] = base(g, slot, k, yy, mm).astype(LOW)
                push(g, per[g][1].at[at], per[g][2].at[at], 16 + at, two)
    if with_small:
        copies[0].wait()
        sbuf[6] = small[...] + sbuf[0]
        copies.append(small_push(1, sbuf.at[6], one, 1))

    def second(g, slot, k, yy, mm):
        value = base(g, slot, k, yy, mm)
        at = slot * Z + k
        arrived(g, per[g][2].at[at], 16 + at)
        return value + per[g][2][at].astype(F32)

    for k in turns:
        for g in range(groups):
            per[g][3][k] = second(g, 1, k, y1, m1).astype(LOW)
            push(g, per[g][3].at[k], per[g][4].at[k], 24 + k, one)
    if with_small:
        copies[1].wait()
        sbuf[7] = sbuf[6] + sbuf[1]
        copies.append(small_push(2, sbuf.at[7], two, 2))

    def third(g, k):
        value = second(g, 0, k, y, m)
        arrived(g, per[g][4].at[k], 24 + k)
        return value + per[g][4][k].astype(F32)

    for k in (1, 2, 3):
        for g in range(groups):
            per[g][5][k] = third(g, k).astype(LOW)
            push(g, per[g][5].at[k], per[g][6].at[k], 28 + k - 1, pz[k - 1])
    if with_small:
        copies[2].wait()
        sbuf[8] = sbuf[7] + sbuf[2]
        for k in (1, 2, 3):
            copies.append(small_push(2 + k, sbuf.at[8], pz[k - 1], 2 + k))
    for g in range(groups):
        total = third(g, 0)
        for k in (1, 2, 3):
            arrived(g, per[g][6].at[k], 28 + k - 1)
            total = total + per[g][6][k].astype(F32)
        outs[g][...] = total
    if with_small:
        for copy in copies[3:]:
            copy.wait()
        small_out[...] = sbuf[8] + sbuf[3] + sbuf[4] + sbuf[5]
    for copy in started:
        copy.wait_send()


def reduce_grads(grads, small, ident):
    groups = len(grads)
    vm = pl.BlockSpec(memory_space=pltpu.VMEM)
    total = Z * Y * C
    part = grads[0].shape[1] // total
    scratch = []
    for g in grads:
        cols = g.shape[2]
        scratch += [pltpu.VMEM((n, part, cols), LOW) for n in (16, 8, 8, 4, 4, 4, 4)]
    scratch += [pltpu.SemaphoreType.DMA((groups, 31)), pltpu.SemaphoreType.DMA((groups, 31))]
    ins = list(grads)
    out_shape = [jax.ShapeDtypeStruct((part, g.shape[2]), F32) for g in grads]
    if small is not None:
        ins.append(small)
        out_shape.append(jax.ShapeDtypeStruct(small.shape, F32))
        scratch += [pltpu.VMEM((9,) + small.shape, F32), pltpu.SemaphoreType.DMA((2, 6))]
    return pl.pallas_call(
        functools.partial(reduce_kernel, groups, small is not None),
        in_specs=[vm] * len(ins),
        out_specs=[vm] * len(out_shape),
        out_shape=out_shape,
        scratch_shapes=scratch,
        compiler_params=pltpu.CompilerParams(collective_id=ident, has_side_effects=True, vmem_limit_bytes=60 * 2**20),
        name=f"reduce_grads_{ident}",
    )(*ins)


def per_device(
    patch_counts, tokens, cotangent, attn_gain, attn_shift, w_qkv, b_qv, w_proj, b_proj,
    ffn_gain, ffn_shift, w_up, b_up, w_down, b_down,
):
    pairs_all, rows, width = tokens.shape
    n_mp = lax.axis_size("mp")
    n_dp = lax.axis_size("dp")
    direct = n_dp == Z * Y * C and n_mp == 2
    pairs = pairs_all // n_mp
    part = w_qkv.shape[0]
    lw = w_qkv.shape[2]
    fw = w_up.shape[1]
    mine = lax.axis_index("mp")
    off = jnp.reshape(mine * pairs, (1,)).astype(jnp.int32)
    lens = TEXT + lax.dynamic_slice_in_dim(patch_counts, mine * pairs, pairs, 0)

    vectors = jnp.stack([attn_gain, attn_shift, b_proj, ffn_gain, ffn_shift, b_down], axis=1)
    first = jnp.concatenate(
        [w_qkv.reshape(part, 3 * lw), w_proj.T, vectors, jnp.zeros((part, EXTRA - 6), F32)], axis=1
    ).astype(LOW)
    second_a = w_up.astype(LOW)
    second_b = w_down.T.astype(LOW)
    bias = jnp.concatenate([b_qv.reshape(-1), b_up]).astype(LOW).astype(F32)
    bias = jnp.broadcast_to(bias, (8,) + bias.shape)
    if direct:
        w_one, w_two, bias = gather_weights(first, second_a, second_b, bias)
    else:
        both_axes = ("mp", "dp")
        w_one = lax.all_gather(first, both_axes, axis=0, tiled=True).reshape(n_mp, width, -1)
        second = jnp.concatenate([second_a, second_b], axis=1)
        w_two = lax.all_gather(second, both_axes, axis=0, tiled=True).reshape(n_mp, width, -1)
        bias = lax.all_gather(bias, "mp", axis=0)

    qkv, att, prob, hid, n1, n2, vec = attention_forward(lens, off, tokens, w_one, bias)
    out_here, act, dpre, dhid, dlow, upl, sums_two, bsum_up = ffn(lens, off, n2, hid, cotangent, w_two, bias, vec)

    def grad(left, right):
        cols = right.shape[2] // n_mp
        return jnp.einsum(
            "rd,rmf->mdf", left.reshape(pairs * rows, width), right.reshape(pairs * rows, n_mp, cols),
            preferred_element_type=F32,
        )

    def reduce(grads, small, ident):
        if direct:
            return reduce_grads([g.astype(LOW) for g in grads], small, ident)
        axes = ("mp", "dp")
        done = [
            lax.psum_scatter(g.reshape(n_mp * width, -1), axes, scatter_dimension=0, tiled=True) for g in grads
        ]
        if small is not None:
            done.append(lax.psum(small, axes))
        return done

    def both(array):
        other = lax.ppermute(array, "mp", [(0, 1), (1, 0)])
        return jnp.where(mine == 0, jnp.concatenate([array, other]), jnp.concatenate([other, array]))

    r_up, r_down, r_proj = reduce([grad(n2, dpre), grad(upl, act), grad(dlow, att)], None, 1)
    tok_here, dqkv, sums_one, bsum_qkv = attention_backward(lens, off, tokens, dhid, qkv, prob, w_one, vec)
    block_out = both(out_here)
    tokens_grad = both(tok_here)
    flat = bsum_qkv[0].reshape(n_mp, 3, lw)
    small = jnp.concatenate([
        sums_one[0], sums_one[1], sums_two[2], sums_two[0], sums_two[1], sums_two[3],
        flat[:, 0].reshape(-1), flat[:, 2].reshape(-1), bsum_up[0]])
    r_qkv, small = reduce([grad(n1, dqkv)], small.reshape(8, -1), 2)
    small = small.reshape(-1)
    place_dp = lax.axis_index("dp") * part

    def piece(i):
        return lax.dynamic_slice_in_dim(small, i * width + place_dp, part, 0)

    rest = small[6 * width :]
    o_b_q = lax.dynamic_slice_in_dim(rest, mine * lw, lw, 0)
    o_b_v = lax.dynamic_slice_in_dim(rest, (n_mp + mine) * lw, lw, 0)
    o_b_up = lax.dynamic_slice_in_dim(rest, 2 * n_mp * lw + mine * fw, fw, 0)
    return (
        block_out, tokens_grad, piece(0), piece(1),
        r_qkv.reshape(part, 3, lw), jnp.stack([o_b_q, o_b_v]),
        r_proj.T, piece(2), piece(3), piece(4), r_up, o_b_up, r_down.T, piece(5),
    )


def solution(mesh):
    vec, mat = P("dp"), P("dp", "mp")
    tok = P("dp", None, None)
    in_specs = (
        vec, tok, tok, vec, vec, P("dp", None, "mp"), P(None, "mp"), P("mp", "dp"), vec, vec, vec,
        mat, P("mp"), P("mp", "dp"), vec,
    )
    out_specs = (
        tok, tok, vec, vec, P("dp", None, "mp"), P(None, "mp"), P("mp", "dp"), vec, vec, vec,
        mat, P("mp"), P("mp", "dp"), vec,
    )
    return jax.shard_map(per_device, mesh=mesh, in_specs=in_specs, out_specs=out_specs, check_vma=False)
```

time: 719 us -> 445 us (0.62)
  Pallas kernels: 0 us -> 328 us
  waiting for transfers between devices: 202 us -> 0.01 us
  matrix products: 188 us -> 30.5 us
  blocking collectives: 140 us -> 0 us
  local copies, waits for them, and re-layouts: 107 us -> 63.3 us
  other arithmetic: 59.2 us -> 18.2 us
  between operations: 14.5 us -> 0.89 us
    pallas_call x0 -> x6, Pallas kernels: none -> 328 us  [the longest x2 141 us: reduce_grads(): pl.pallas_call(functools.partial(reduce_kernel, groups, small is not None...]
    reduce_scatter x1 -> x0, waiting for transfers between devices: 158 us -> none  [per_device(): lax.psum_scatter(grads_two, ('mp', 'dp'), scatter_dimension=0, tiled=True)]
    dot_general x17 -> x4, matrix products: 171 us -> 30.5 us  [grad(): jnp.einsum('rd,rmf->mdf', left.reshape(pairs * rows, width), right.reshap...]
    psum x1 -> x0, blocking collectives: 116 us -> none  [per_device(): small = lax.psum(small, ('mp', 'dp'))]
    reshape x4 -> x9, local copies, waits for them, and re-layouts: 0.17 us -> 47.8 us  [the longest x4 44.8 us: grad(): right.reshape(pairs * rows, n_mp, cols)]
    all_gather x2 -> x0, waiting for transfers between devices: 44.1 us -> none  [the longest x1 30.6 us: per_device(): lax.all_gather(first, ('mp', 'dp'), axis=0, tiled=True)]
    all_gather x2 -> x0, blocking collectives: 23.4 us -> none  [the longest x1 19 us: per_device(): vec_full = lax.all_gather(vectors, 'dp', axis=1, tiled=True).astype(F32)]
    slice x11 -> x5, local copies, waits for them, and re-layouts: 25.1 us -> 2.72 us  [the longest x1 0.91 us: per_device(): flat = bsum_qkv[0].reshape(n_mp, 3, lw)]
  transfers between devices with their start and end apart: 6 -> 2, of which waited for: 3 -> 0; matrix products, arithmetic and copies ran while one was open for 22% -> 20% of each run, Pallas kernels for 0% -> 32%
where the time goes in v2:
time: 445 us; the launch traced here: 443 us
  Pallas kernels  328 us (74%)
  local copies, waits for them, and re-layouts  63.3 us (14%)
  matrix products  30.5 us (7%)
  other arithmetic  18.2 us (4%)
    pallas_call x2, Pallas kernels, reduce_grads(): pl.pallas_call(functools.partial(reduce_kernel, groups, small is not None...  141 us
    pallas_call x1, Pallas kernels, gather_weights(): pl.pallas_call(gather_kernel, in_specs=[vm] * 4, out_specs=[hbm] * 3, out...  79.6 us
    reshape x4, local copies, waits for them, and re-layouts, grad(): right.reshape(pairs * rows, n_mp, cols)  44.8 us
    pallas_call x1, Pallas kernels, attention_backward(): pl.pallas_call(back_kernel, grid_spec=pltpu.PrefetchScalarGridSpec(num_sc...  37 us
    pallas_call x1, Pallas kernels, attention_forward(): pl.pallas_call(attn_kernel, grid_spec=pltpu.PrefetchScalarGridSpec(num_sc...  36 us
    pallas_call x1, Pallas kernels, ffn(): pl.pallas_call(ffn_kernel, grid_spec=pltpu.PrefetchScalarGridSpec(num_sca...  34.6 us
    dot_general x4, matrix products, grad(): jnp.einsum('rd,rmf->mdf', left.reshape(pairs * rows, width), right.reshap...  30.5 us
    unnamed x41, local copies, waits for them, and re-layouts  9.76 us
  transfers between devices with their start and end apart: 2, of which 0 were waited for; matrix products, arithmetic and copies ran while one was open for 20% of the time, Pallas kernels for 32%

profile of v2, /device:TPU:8, one launch (start us, length us, event | category | flops | bytes accessed | tf_op | source)
XLA Modules:
  0.0 442.9 jit_solution(13527654411740242243)
XLA Ops:
  0.7 1.0 convert_bitcast_fusion.3
  1.6 0.9 convert_bitcast_fusion.4
  2.5 0.7 convert_bitcast_fusion.10
  3.3 0.7 convert_bitcast_fusion.9
  4.1 0.7 convert_bitcast_fusion.8
  4.8 0.7 convert_bitcast_fusion.7
  5.6 0.7 convert_bitcast_fusion.6
  6.4 0.7 convert_bitcast_fusion.5
  7.1 1.0 convert_bitcast_fusion.2.s2
  8.1 1.0 convert_element_type.33.s1
  9.1 0.7 convert.50
  9.8 0.7 convert.49
  10.5 1.2 dynamic-slice_add_fusion.lens
  11.9 79.6 %gather_weights.1 = (bf16[2,768,1664]{2,1,0:T(8,128)(2,1)S(1)}, bf16[2,768,3072]{2,1,0:T(8,128)(2,1)S(1)}, f32[2,8,2304]{2,1,0:T(8,128)S(1)}) custom-call(bf16[48,1664]{1,0:T(8,128)(2,1)S(1)} %concatenate.23.s0, bf16[48,1536]{1,0:T(8,128)(2,1)S(1)} %convert_element_type.33.s1, bf16[48,1536]{1,0:T(8,128)(2,1)S(1)} %convert_bitcast_fusion.2.s2, ...), custom_call_target="tpu_custom_call" | custom-call | tf_op jit(solution)/shard_map/gather_weights/pallas_call | solution.py:423
  91.6 2.3 copy-done
  93.8 3.6 copy-done.1
  97.5 0.7 copy-done.2
  98.1 36.0 %attention_forward.1 = (bf16[4,280,2304]{2,1,0:T(8,128)(2,1)}, bf16[4,280,768]{2,1,0:T(8,128)(2,1)}, bf16[4,12,280,280]{3,2,1,0:T(8,128)(2,1)}, f32[4,280,768]{2...) custom-call(s32[4]{0:T(128)} %dynamic-slice_add_fusion.lens, ...), custom_call_target="tpu_custom_call" | custom-call | tf_op jit(solution)/shard_map/attention_forward/pallas_call | solution.py:103
  134.1 34.6 %feed_forward.1 = (bf16[4,280,768]{2,1,0:T(8,128)(2,1)}, bf16[4,280,3072]{2,1,0:T(8,128)(2,1)}, bf16[4,280,3072]{2,1,0:T(8,128)(2,1)}, f32[4,280,768]{2,1,0:T(8,...) custom-call(s32[4]{0:T(128)} %dynamic-slice_add_fusion.lens, ...), custom_call_target="tpu_custom_call" | custom-call | tf_op jit(solution)/shard_map/feed_forward/pallas_call | solution.py:178
  168.7 37.0 %attention_backward.1 = (bf16[4,280,768]{2,1,0:T(8,128)(2,1)}, bf16[4,280,2304]{2,1,0:T(8,128)(2,1)}, f32[8,768]{1,0:T(8,128)}, f32[8,2304]{1,0:T(8,128)}) custom-call(s32[4]{0:T(128)} %dynamic-slice_add_fusion.lens, s32[1]{0:T(128)} %bitcast.off, bf16[8,280,768]{2,1,0:T(8,128)(2,1)} %x_ref.3, f32[4,280,768]{2,1,0:T(8,128)} %get-tuple-element.48.dhid_ref, ...), custom_call_target="tpu_custom_call" | custom-call | tf_op jit(solution)/shard_map/attention_backward/pallas_call | solution.py:268
  205.7 1.5 collective-permute-start.1
  207.2 0.6 collective-permute-start
  207.8 0.8 slice_reduce_fusion.7
  208.7 0.9 slice_reduce_fusion
  209.7 0.9 slice.45
  210.7 0.6 reshape.78.refs_1_
  211.3 10.8 %reshape.76 = bf16[1120,2,1152]{2,1,0:T(2,128)(2,1)} reshape(bf16[4,280,2304]{2,1,0:T(8,128)(2,1)} %get-tuple-element.52) | data formatting | bytes 10321920 | tf_op jit(solution)/shard_map/reshape | solution.py:628
  222.2 8.7 %fusion.13.refs_0_ = bf16[2,768,1152]{2,1,0:T(8,128)(2,1)} fusion(bf16[1120,768,1]{1,0,2:T(8,128)(2,1)S(1)} %bitcast.60, bf16[1120,2,1152]{2,1,0:T(2,128)(2,1)} %reshape.76), kind=kOutput, calls=%fused_computation.9 | convolution fusion | flops 3965386752 | bytes 10420224 | tf_op jit(solution)/shard_map/rd,rmf->mdf/dot_general | solution.py:627
  230.9 64.4 %reduce_grads_2.1 = (f32[48,1152]{1,0:T(8,128)}, f32[8,1152]{1,0:T(8,128)}) custom-call(bf16[2,768,1152]{2,1,0:T(8,128)(2,1)} %fusion.13.refs_0_, f32[8,1152]{1,0:T(8,128)} %reshape.78.refs_1_), custom_call_target="tpu_custom_call" | custom-call | tf_op jit(solution)/shard_map/reduce_grads_2/pallas_call | solution.py:578
  295.3 0.8 slice.46
  296.1 0.8 reshape.79
  296.9 16.4 %reshape.83 = bf16[1120,2,1536]{2,1,0:T(2,128)(2,1)} reshape(bf16[4,280,3072]{2,1,0:T(8,128)(2,1)} %get-tuple-element.61) | data formatting | bytes 13762560 | tf_op jit(solution)/shard_map/reshape | solution.py:628
  313.2 1.4 reshape.85
  314.6 16.2 %reshape.81 = bf16[1120,2,1536]{2,1,0:T(2,128)(2,1)} reshape(bf16[4,280,3072]{2,1,0:T(8,128)(2,1)} %get-tuple-element.60) | data formatting | bytes 13762560 | tf_op jit(solution)/shard_map/reshape | solution.py:628
  330.8 10.9 %convert_bitcast_fusion.refs_1_ = bf16[2,768,1536]{2,1,0:T(8,128)(2,1)} fusion(bf16[1120,768,1]{1,0,2:T(8,128)(2,1)} %bitcast.59, bf16[1120,2,1536]{2,1,0:T(2,128)(2,1)} %reshape.83), kind=kOutput, calls=%fused_computation.6 | convolution fusion | flops 5287182336 | bytes 13320192 | tf_op jit(solution)/shard_map/rd,rmf->mdf/dot_general | solution.py:627
  341.7 2.8 fusion.21.refs_2_
  344.5 0.6 copy-done.3
  345.6 8.1 %convert_bitcast_fusion.1.refs_0_ = bf16[2,768,1536]{2,1,0:T(8,128)(2,1)} fusion(bf16[1120,768,1]{1,0,2:T(8,128)(2,1)S(1)} %bitcast.51, bf16[1120,2,1536]{2,1,0:T(2,128)(2,1)S(1)} %copy-done.3), kind=kOutput, calls=%fused_computation.7 | convolution fusion | flops 5287182336 | bytes 13320192 | tf_op jit(solution)/shard_map/rd,rmf->mdf/dot_general | solution.py:627
  353.6 76.3 %reduce_grads_1.1 = (f32[48,1536]{1,0:T(8,128)}, f32[48,1536]{1,0:T(8,128)}, f32[48,384]{1,0:T(8,128)}) custom-call(bf16[2,768,1536]{2,1,0:T(8,128)(2,1)} %convert_bitcast_fusion.1.refs_0_, bf16[2,768,1536]{2,1,0:T(8,128)(2,1)} %convert_bitcast_fusion.refs_1_, bf16[2,768,384]{2,1,0:T(8,128)(2,1)} %fusion.21.refs_2_), custom_call_target="tpu_custom_call" | custom-call | tf_op jit(solution)/shard_map/reduce_grads_1/pallas_call | solution.py:578
  430.1 1.6 copy.88
  431.7 0.7 dynamic_slice.38
  432.4 0.6 pad_maximum_fusion
  433.0 0.6 fusion.24
  433.6 3.6 maximum_select_fusion.1
  437.2 3.6 maximum_select_fusion
  440.8 0.6 copy.101
  441.5 0.7 copy.102
  442.2 0.7 copy.103
  (59 shorter events, 1.6 us)
Async XLA Ops:
  91.5 2.3 copy-start
  93.8 3.6 copy-start.1
  97.5 0.7 copy-start.2
  168.7 38.6 %copy-start.5 = (bf16[4,280,768]{2,1,0:T(8,128)(2,1)S(1)}, bf16[4,280,768]{2,1,0:T(8,128)(2,1)}, u32[]{:S(2)}) copy-start(bf16[4,280,768]{2,1,0:T(8,128)(2,1)} %get-tuple-element.47) | copy-start | bytes 5160964
  168.7 40.0 %copy-start.12 = (f32[8,768]{1,0:T(8,128)S(1)}, f32[8,768]{1,0:T(8,128)}, u32[]{:S(2)}) copy-start(f32[8,768]{1,0:T(8,128)} %get-tuple-element.55) | copy-start | bytes 73732
  205.7 227.8 %collective-permute-start.1 = (bf16[4,280,768]{2,1,0:T(8,128)(2,1)}, bf16[4,280,768]{2,1,0:T(8,128)(2,1)}, u32[]{:S(2)}, u32[]{:S(2)}) collective-permute-start(bf16[4,280,768]{2,1,0:T(8,128)(2,1)} %get-tuple-element.51), channel_id=1, source_target_pairs={{0,1},{1,0},{2,3},{3,2},{4,5},{5,4},{6,7},{7,6},{8,9},{9,8},{10,11... | collective-permute-start | bytes 5160968 | tf_op jit(solution)/shard_map/ppermute | solution.py:644
  207.2 230.0 %collective-permute-start = (bf16[4,280,768]{2,1,0:T(8,128)(2,1)S(1)}, bf16[4,280,768]{2,1,0:T(8,128)(2,1)}, u32[]{:S(2)}, u32[]{:S(2)}) collective-permute-start(bf16[4,280,768]{2,1,0:T(8,128)(2,1)S(1)} %copy-done.5), channel_id=1, source_target_pairs={{0,1},{1,0},{2,3},{3,2},{4,5},{5,4},{6,7},{7,6},{8,9},{9,8},{10,11... | collective-permute-start | bytes 5160968 | tf_op jit(solution)/shard_map/ppermute | solution.py:644
  211.3 10.8 %copy-start.14 = (bf16[4,280,768]{2,1,0:T(8,128)(2,1)S(1)}, bf16[4,280,768]{2,1,0:T(8,128)(2,1)}, u32[]{:S(2)}) copy-start(bf16[4,280,768]{2,1,0:T(8,128)(2,1)} %get-tuple-element.53) | copy-start | bytes 5160964
  296.9 16.4 %copy-start.7 = (bf16[4,280,768]{2,1,0:T(8,128)(2,1)S(1)}, bf16[4,280,768]{2,1,0:T(8,128)(2,1)}, u32[]{:S(2)}) copy-start(bf16[4,280,768]{2,1,0:T(8,128)(2,1)} %get-tuple-element.63) | copy-start | bytes 5160964
  330.8 10.9 %copy-start.8 = (bf16[1120,2,384]{2,1,0:T(2,128)(2,1)S(1)}, bf16[1120,2,384]{2,1,0:T(2,128)(2,1)}, u32[]{:S(2)}) copy-start(bf16[1120,2,384]{2,1,0:T(2,128)(2,1)} %reshape.85) | copy-start | bytes 5160964
  330.8 10.9 %copy-start.13 = (bf16[4,280,768]{2,1,0:T(8,128)(2,1)S(1)}, bf16[4,280,768]{2,1,0:T(8,128)(2,1)}, u32[]{:S(2)}) copy-start(bf16[4,280,768]{2,1,0:T(8,128)(2,1)} %get-tuple-element.64) | copy-start | bytes 5160964
  341.7 3.4 copy-start.3
  341.7 3.8 copy-start.4
  353.6 79.9 %copy-start.6 = (bf16[4,280,768]{2,1,0:T(8,128)(2,1)S(1)}, bf16[4,280,768]{2,1,0:T(8,128)(2,1)}, u32[]{:S(2)}) copy-start(bf16[4,280,768]{2,1,0:T(8,128)(2,1)} %get-tuple-element.51) | copy-start | bytes 5160964
  437.2 3.6 copy-start.11
  437.2 4.3 copy-start.10
  437.2 5.0 %copy-start.9 = (f32[48,1536]{1,0:T(8,128)S(1)}, f32[48,1536]{1,0:T(8,128)}, u32[]{:S(2)}) copy-start(f32[48,1536]{1,0:T(8,128)} %get-tuple-element.67) | copy-start | bytes 884740

commit v3 on v2

--- a/solution.py
+++ b/solution.py
@@ -201,7 +201,7 @@
     )(lens, off, n2, hid, cotangent, w_two, bias, vec)
 
 
-def back_kernel(lens, off, x_ref, dhid_ref, qkv_ref, prob_ref, w_ref, vec_ref,
+def plain_back_kernel(lens, off, x_ref, dhid_ref, qkv_ref, prob_ref, w_ref, vec_ref,
                 tok_ref, dqkv_ref, sums_ref, bsum_ref, do_ref):
     p = pl.program_id(0)
     rows, width = x_ref.shape[1], x_ref.shape[2]
@@ -266,7 +266,7 @@
     pairs, rows, width = dhid.shape
     out = lambda dt, *s: jax.ShapeDtypeStruct((pairs,) + s, dt)
     return pl.pallas_call(
-        back_kernel,
+        plain_back_kernel,
         grid_spec=pltpu.PrefetchScalarGridSpec(
             num_scalar_prefetch=2,
             grid=(pairs,),
@@ -438,152 +438,321 @@
     )(first, second_a, second_b, bias)
 
 
-def reduce_kernel(groups, with_small, *refs):
-    grads = refs[:groups]
-    pos = groups
-    small = None
-    if with_small:
-        small = refs[pos]
-        pos += 1
-    outs = refs[pos : pos + groups]
-    pos += groups
-    if with_small:
-        small_out = refs[pos]
-        pos += 1
-    per = [refs[pos + 7 * g : pos + 7 * (g + 1)] for g in range(groups)]
-    pos += 7 * groups
-    send, recv = refs[pos], refs[pos + 1]
-    pos += 2
+BLOCKS = 31
+
+
+def back_kernel(tok_all, dhid_ref, qkv_ref, prob_ref, n1_ref, w_ref, vec_ref, g_up, g_down, g_proj, sums_two, bsum_up,
+                tok_ref, tok_other, r_up, r_down, r_proj, r_qkv, small_out,
+                do_ref, xbuf, tokbuf, n1t, dq_all, gq, sums, bsum,
+                own_up, own_down, own_proj, rc0, rs0, rz0, rx0, rc1, rs1, rz1, rx1, rc2, rs2, rz2, rx2,
+                rc3, rs3, rz3, rx3, sbuf, send, recv, local, tsem, ssem):
+    p = pl.program_id(0)
+    pairs, rows, width = xbuf.shape
+    groups = w_ref.shape[0]
+    lw = width // groups
+    tiles = lw // 128
     z, y, c, m = place()
-    (y1, m1), (y2, m2) = flips(y, c, m)
-    part = outs[0].shape[0]
-    peers = greet(z, y, c, m)
-    pz, one, two, sib = peers[:3], peers[3], peers[4], peers[5]
-    started = []
-    count = [0] * groups
-
-    def push(g, src, dst, sem, to):
-        copy = pltpu.make_async_remote_copy(
-            src_ref=src, dst_ref=dst, send_sem=send.at[g, count[g]], recv_sem=recv.at[g, sem],
+    outs = (r_up, r_down, r_proj, r_qkv)
+    grads = (g_up, g_down, g_proj, gq)
+    owns = (own_up, own_down, own_proj)
+    rcs, rss, rzs, rxs = (rc0, rc1, rc2, rc3), (rs0, rs1, rs2, rs3), (rz0, rz1, rz2, rz3), (rx0, rx1, rx2, rx3)
+    part = r_up.shape[0]
+    me = index(z, y, c)
+    sib = (index(z, y, 1 - c), m)
+
+    def beside(k):
+        return (index(lax.rem(z + k, Z), y, c), m)
+
+    def x_first(g, cc):
+        return cc if g == 0 else 0
+
+    def target(g, cc, ra, rb):
+        fx = x_first(g, cc)
+        dy = fx * rb + (1 - fx) * ra
+        dm = fx * ra + (1 - fx) * rb
+        return y + dy * (1 - 2 * y), m + dm * (1 - 2 * m)
+
+    def chip(g, ra, rb):
+        yy, mm = target(g, c, ra, rb)
+        return (index(z, yy, c), mm)
+
+    def column(g, mm):
+        cols = outs[g].shape[1]
+        return pl.ds(pl.multiple_of(mm * cols, 128), cols)
+
+    def copy_of(g, src, dst, out_sem, in_sem, to):
+        return pltpu.make_async_remote_copy(
+            src_ref=src, dst_ref=dst, send_sem=send.at[g, out_sem], recv_sem=recv.at[g, in_sem],
             device_id={"dp": to[0], "mp": to[1]}, device_id_type=MESH_ID,
         )
-        count[g] += 1
-        copy.start()
-        started.append(copy)
-
-    def arrived(g, dst, sem):
-        pltpu.make_async_remote_copy(
-            src_ref=dst, dst_ref=dst, send_sem=send.at[g, 0], recv_sem=recv.at[g, sem],
-            device_id={"dp": sib[0], "mp": sib[1]}, device_id_type=MESH_ID,
-        ).wait_recv()
-
-    def grad(g, zz, yy, cc, mm):
-        return grads[g].at[mm, pl.ds(pl.multiple_of(index(zz, yy, cc) * part, part), part)]
-
-    if with_small:
-        sbuf, ssem = refs[pos], refs[pos + 1]
-
-        def small_push(slot, src, to, sems):
-            copy = pltpu.make_async_remote_copy(
-                src_ref=src, dst_ref=sbuf.at[slot], send_sem=ssem.at[0, sems], recv_sem=ssem.at[1, sems],
-                device_id={"dp": to[0], "mp": to[1]}, device_id_type=MESH_ID,
-            )
+
+    def to_sibling(g):
+        def one(i, carry):
+            slot = 15 - i
+            ra, rb, k = slot // 8, lax.rem(slot // 4, 2), lax.rem(slot, 4)
+            yy, mm = target(g, 1 - c, ra, rb)
+            src = grads[g].at[lax.rem(z + k, Z) * Y + yy, 1 - c, :, column(g, mm)]
+            copy_of(g, src, rcs[g].at[slot], slot, slot, sib).start()
+            return carry
+
+        lax.fori_loop(0, 16, one, 0)
+
+    def arrived(g, ref, sem):
+        copy_of(g, ref, ref, 0, sem, sib).wait_recv()
+
+    def base(g, ra, rb, k):
+        slot = (ra * 2 + rb) * 4 + k
+        arrived(g, rcs[g].at[slot], slot)
+        yy, mm = target(g, c, ra, rb)
+        row = lax.rem(z + k, Z) * Y + yy
+        mine = owns[g][row, :, column(g, mm)] if g < 3 else gq[row, c, :, column(g, mm)]
+        return mine.astype(F32) + rcs[g][slot].astype(F32)
+
+    def level(g, rb, k):
+        value = base(g, 0, rb, k)
+        at = rb * 4 + k
+        arrived(g, rss[g].at[at], 16 + at)
+        return value + rss[g][at].astype(F32)
+
+    def lined(g, rb):
+        value = level(g, rb, 0)
+        for k in (1, 2, 3):
+            at = (k - 1) * 2 + rb
+            arrived(g, rzs[g].at[at], 24 + at)
+            value = value + rzs[g][at].astype(F32)
+        return value
+
+    def event_s(g, r):
+        rb, k = 1 - r // 4, lax.rem(r + 1, 4)
+        slot = (2 + rb) * 4 + k
+        at = rb * 4 + k
+        rcs[g][slot] = base(g, 1, rb, k).astype(LOW)
+        copy_of(g, rcs[g].at[slot], rss[g].at[at], 16 + at, 16 + at, chip(g, 1, 0)).start()
+
+    def event_z(g, r):
+        rb, k = 1 - lax.rem(r, 2), 1 + r // 2
+        slot = rb * 4 + k
+        at = (k - 1) * 2 + rb
+        rcs[g][slot] = level(g, rb, k).astype(LOW)
+        copy_of(g, rcs[g].at[slot], rzs[g].at[at], 24 + at, 24 + at, beside(k)).start()
+
+    def event_x(g):
+        rcs[g][4] = lined(g, 1).astype(LOW)
+        copy_of(g, rcs[g].at[4], rxs[g].at[0], 30, 30, chip(g, 0, 1)).start()
+
+    def final(g):
+        value = lined(g, 0)
+        arrived(g, rxs[g].at[0], 30)
+        outs[g][...] = value + rxs[g][0].astype(F32)
+
+        def one(i, carry):
+            copy_of(g, rcs[g].at[0], rcs[g].at[0], i, 0, sib).wait_send()
+            return carry
+
+        lax.fori_loop(0, BLOCKS, one, 0)
+
+    def tok_copy(i):
+        return pltpu.make_async_remote_copy(
+            src_ref=tokbuf.at[i], dst_ref=tok_other.at[i], send_sem=tsem.at[0, i], recv_sem=tsem.at[1, i],
+            device_id={"dp": me, "mp": 1 - m}, device_id_type=MESH_ID,
+        )
+
+    def own_copy(g):
+        return pltpu.make_async_copy(grads[g].at[:, c], owns[g], local.at[g])
+
+    x_copy = pltpu.make_async_copy(tok_all.at[pl.ds(m * pairs, pairs)], xbuf, local.at[3])
+
+    @pl.when(p == 0)
+    def _():
+        for g in range(3):
+            own_copy(g).start()
+        x_copy.start()
+        greet(z, y, c, m)
+        for g in range(3):
+            to_sibling(g)
+        sums[...] = jnp.zeros_like(sums)
+        bsum[...] = jnp.zeros_like(bsum)
+        for g in range(3):
+            own_copy(g).wait()
+        x_copy.wait()
+
+    dhid = dhid_ref[0]
+    dlow = dhid.astype(LOW)
+    for mm in range(groups):
+        do_ref[:, mm * lw : (mm + 1) * lw] = dot(dlow, w_ref[mm, :, 3 * lw : 4 * lw]).astype(LOW)
+    n1t[p] = n1_ref[0].T
+    first = lax.broadcasted_iota(jnp.int32, (1, 128), 1) < HEAD_DIM
+
+    def pair(hp, carry):
+        lane = (hp // tiles) * 3 * lw + lax.rem(hp, tiles) * 128
+
+        def cols(t):
+            return pl.ds(pl.multiple_of(lane + t * lw, 128), 128)
+
+        q2 = qkv_ref[0, :, cols(0)] * 0.125
+        k2t = qkv_ref[0, :, cols(1)].T
+        v2 = qkv_ref[0, :, cols(2)]
+        do2 = do_ref[:, pl.ds(pl.multiple_of(hp * 128, 128), 128)]
+        dq_t = []
+        dk = dv = 0.0
+        for h in range(2):
+            mine = first if h == 0 else ~first
+            doh = jnp.where(mine, do2, 0)
+            qh = jnp.where(mine, q2, 0)
+            dpt = dot(v2, doh, NT)
+            plow = prob_ref[0, hp * 2 + h]
+            pt = plow.astype(F32)
+            inner = jnp.sum(pt * dpt, axis=0, keepdims=True)
+            dst = (pt * (dpt - inner)).astype(LOW)
+            dv = dv + dot(plow, doh)
+            dk = dk + dot(dst, qh)
+            dq_t.append(dot(k2t[h * HEAD_DIM : (h + 1) * HEAD_DIM], dst))
+        dq = (jnp.concatenate(dq_t, axis=0) * 0.125).T
+        dq_all[p, :, cols(0)] = dq.astype(LOW)
+        dq_all[p, :, cols(1)] = dk.astype(LOW)
+        dq_all[p, :, cols(2)] = dv.astype(LOW)
+        bsum[0:1, cols(0)] += jnp.sum(dq, axis=0, keepdims=True)
+        bsum[0:1, cols(2)] += jnp.sum(dv, axis=0, keepdims=True)
+
+        step = p * (groups * tiles) + hp
+        for g in range(3):
+
+            @pl.when((step >= 4 * g) & (step < 4 * g + 4))
+            def _():
+                event_s(g, 2 * step - 8 * g)
+                event_s(g, 2 * step - 8 * g + 1)
+
+        @pl.when((step >= 17) & (step < 23))
+        def _():
+            event_z(0, step - 17)
+
+        return carry
+
+    lax.fori_loop(0, groups * tiles, pair, 0)
+    done = sum(dot(dq_all[p, :, mm * 3 * lw : (mm + 1) * 3 * lw], w_ref[mm, :, : 3 * lw], NT) for mm in range(groups))
+    xhat, r = moments(xbuf[p].astype(F32))
+    dg = done * vec_ref[0:1]
+    dn = r * (dg - jnp.mean(dg, axis=-1, keepdims=True) - xhat * jnp.mean(dg * xhat, axis=-1, keepdims=True))
+    tok = (dhid + dn).astype(LOW)
+    tok_ref[0] = tok
+    tokbuf[p] = tok
+    tok_copy(p).start()
+    sums[0:1] += jnp.sum(done * xhat, axis=0, keepdims=True)
+    sums[1:2] += jnp.sum(done, axis=0, keepdims=True)
+
+    def small_copy(slot, src, to, sem):
+        return pltpu.make_async_remote_copy(
+            src_ref=sbuf.at[src], dst_ref=sbuf.at[slot], send_sem=ssem.at[0, sem], recv_sem=ssem.at[1, sem],
+            device_id={"dp": to[0], "mp": to[1]}, device_id_type=MESH_ID,
+        )
+
+    @pl.when(p == pairs - 1)
+    def _():
+        sbuf[6] = jnp.zeros_like(sbuf[6])
+        sbuf[6, 0:1] = bsum_up[0:1]
+        sbuf[6, 1:2, : 3 * width] = bsum[0:1]
+        sbuf[6, 2:3, :width] = sums[0:1]
+        sbuf[6, 2:3, width : 2 * width] = sums[1:2]
+        sbuf[6, 2:3, 2 * width : 3 * width] = sums_two[2:3]
+        sbuf[6, 2:3, 3 * width :] = sums_two[0:1]
+        sbuf[6, 3:4, :width] = sums_two[1:2]
+        sbuf[6, 3:4, width : 2 * width] = sums_two[3:4]
+        s0 = small_copy(0, 6, sib, 0)
+        s0.start()
+
+        def chunk(i, carry):
+            at = pl.ds(pl.multiple_of(i * lw, 128), lw)
+            acc = dot(n1t[0], dq_all[0, :, at])
+            for q in range(1, pairs):
+                acc = acc + dot(n1t[q], dq_all[q, :, at])
+            gq[:, :, :, at] = acc.astype(LOW).reshape(Z * Y, C, part, lw)
+            event_z(1, i)
+            return carry
+
+        lax.fori_loop(0, 3 * groups, chunk, 0)
+        to_sibling(3)
+        s0.wait()
+        sbuf[7] = sbuf[6] + sbuf[0]
+        s1 = small_copy(1, 7, chip(1, 1, 0), 1)
+        s1.start()
+
+        def loop(n, event, g):
+            def one(i, carry):
+                event(g, i)
+                return carry
+
+            lax.fori_loop(0, n, one, 0)
+
+        loop(8, event_s, 3)
+        s1.wait()
+        sbuf[8] = sbuf[7] + sbuf[1]
+        s2 = small_copy(2, 8, chip(1, 0, 1), 2)
+        s2.start()
+        event_x(0)
+        loop(6, event_z, 2)
+        s2.wait()
+        sbuf[9] = sbuf[8] + sbuf[2]
+        zs = [small_copy(2 + k, 9, beside(k), 2 + k) for k in (1, 2, 3)]
+        for copy in zs:
             copy.start()
-            return copy
-
-        copies = [small_push(0, small, sib, 0)]
-
-    (a1, b1), (a2, b2) = flips(y, 1 - c, m)
-    order = [(3, 1 - y, 1 - m), (2, a2, b2), (1, a1, b1), (0, y, m)]
-    turns = (1, 2, 3, 0)
-    for slot, yy, mm in order:
-        for k in turns:
-            for g in range(groups):
-                push(g, grad(g, lax.rem(z + k, Z), yy, 1 - c, mm), per[g][0].at[slot * Z + k], slot * Z + k, sib)
-
-    def base(g, slot, k, yy, mm):
-        arrived(g, per[g][0].at[slot * Z + k], slot * Z + k)
-        return grad(g, lax.rem(z + k, Z), yy, c, mm)[...].astype(F32) + per[g][0][slot * Z + k].astype(F32)
-
-    for slot, yy, mm in ((3, 1 - y, 1 - m), (2, y2, m2)):
-        for k in turns:
-            for g in range(groups):
-                at = (slot - 2) * Z + k
-                per[g][1][at] = base(g, slot, k, yy, mm).astype(LOW)
-                push(g, per[g][1].at[at], per[g][2].at[at], 16 + at, two)
-    if with_small:
-        copies[0].wait()
-        sbuf[6] = small[...] + sbuf[0]
-        copies.append(small_push(1, sbuf.at[6], one, 1))
-
-    def second(g, slot, k, yy, mm):
-        value = base(g, slot, k, yy, mm)
-        at = slot * Z + k
-        arrived(g, per[g][2].at[at], 16 + at)
-        return value + per[g][2][at].astype(F32)
-
-    for k in turns:
-        for g in range(groups):
-            per[g][3][k] = second(g, 1, k, y1, m1).astype(LOW)
-            push(g, per[g][3].at[k], per[g][4].at[k], 24 + k, one)
-    if with_small:
-        copies[1].wait()
-        sbuf[7] = sbuf[6] + sbuf[1]
-        copies.append(small_push(2, sbuf.at[7], two, 2))
-
-    def third(g, k):
-        value = second(g, 0, k, y, m)
-        arrived(g, per[g][4].at[k], 24 + k)
-        return value + per[g][4][k].astype(F32)
-
-    for k in (1, 2, 3):
-        for g in range(groups):
-            per[g][5][k] = third(g, k).astype(LOW)
-            push(g, per[g][5].at[k], per[g][6].at[k], 28 + k - 1, pz[k - 1])
-    if with_small:
-        copies[2].wait()
-        sbuf[8] = sbuf[7] + sbuf[2]
-        for k in (1, 2, 3):
-            copies.append(small_push(2 + k, sbuf.at[8], pz[k - 1], 2 + k))
-    for g in range(groups):
-        total = third(g, 0)
-        for k in (1, 2, 3):
-            arrived(g, per[g][6].at[k], 28 + k - 1)
-            total = total + per[g][6][k].astype(F32)
-        outs[g][...] = total
-    if with_small:
-        for copy in copies[3:]:
+        event_x(1)
+        loop(6, event_z, 3)
+        final(0)
+        event_x(2)
+        for copy in zs:
             copy.wait()
-        small_out[...] = sbuf[8] + sbuf[3] + sbuf[4] + sbuf[5]
-    for copy in started:
-        copy.wait_send()
-
-
-def reduce_grads(grads, small, ident):
-    groups = len(grads)
-    vm = pl.BlockSpec(memory_space=pltpu.VMEM)
+        small_out[...] = (sbuf[9] + sbuf[3] + sbuf[4] + sbuf[5])[:4]
+        final(1)
+        event_x(3)
+        final(2)
+        final(3)
+
+        def finish(i, carry):
+            tok_copy(i).wait()
+            return carry
+
+        lax.fori_loop(0, pairs, finish, 0)
+
+
+def backward_reduce(tokens, dhid, qkv, prob, n1, w_one, vec, grads, sums_two, bsum_up):
+    pairs, rows, width = dhid.shape
     total = Z * Y * C
-    part = grads[0].shape[1] // total
-    scratch = []
-    for g in grads:
-        cols = g.shape[2]
-        scratch += [pltpu.VMEM((n, part, cols), LOW) for n in (16, 8, 8, 4, 4, 4, 4)]
-    scratch += [pltpu.SemaphoreType.DMA((groups, 31)), pltpu.SemaphoreType.DMA((groups, 31))]
-    ins = list(grads)
-    out_shape = [jax.ShapeDtypeStruct((part, g.shape[2]), F32) for g in grads]
-    if small is not None:
-        ins.append(small)
-        out_shape.append(jax.ShapeDtypeStruct(small.shape, F32))
-        scratch += [pltpu.VMEM((9,) + small.shape, F32), pltpu.SemaphoreType.DMA((2, 6))]
+    part = grads[0].shape[0] // total
+    grads = [g.reshape(Z * Y, C, part, g.shape[1]) for g in grads]
+    widths = [g.shape[3] // 2 for g in grads] + [3 * width // 2]
+    hbm = pl.BlockSpec(memory_space=pl.ANY)
+    scratch = [
+        pltpu.VMEM((rows, width), LOW), pltpu.VMEM((pairs, rows, width), LOW), pltpu.VMEM((pairs, rows, width), LOW),
+        pltpu.VMEM((pairs, width, rows), LOW), pltpu.VMEM((pairs, rows, 3 * width), LOW),
+        pltpu.VMEM((Z * Y, C, part, 3 * width), LOW), pltpu.VMEM((8, width), F32), pltpu.VMEM((8, 3 * width), F32),
+    ]
+    scratch += [pltpu.VMEM((Z * Y, part, 2 * w), LOW) for w in widths[:3]]
+    for w in widths:
+        scratch += [pltpu.VMEM((n, part, w), LOW) for n in (16, 8, 6, 1)]
+    scratch += [
+        pltpu.VMEM((10, 8, bsum_up.shape[1]), F32),
+        pltpu.SemaphoreType.DMA((4, BLOCKS)), pltpu.SemaphoreType.DMA((4, BLOCKS)), pltpu.SemaphoreType.DMA((4,)),
+        pltpu.SemaphoreType.DMA((2, pairs)), pltpu.SemaphoreType.DMA((2, 6)),
+    ]
+    whole = lambda *s: pl.BlockSpec(s, lambda p: (0,) * len(s))
     return pl.pallas_call(
-        functools.partial(reduce_kernel, groups, small is not None),
-        in_specs=[vm] * len(ins),
-        out_specs=[vm] * len(out_shape),
-        out_shape=out_shape,
+        back_kernel,
+        grid=(pairs,),
+        in_specs=[
+            hbm, pair_spec(rows, width), pair_spec(rows, 3 * width), pair_spec(HEADS, rows, rows),
+            pair_spec(rows, width), const_spec(w_one.shape), const_spec(vec.shape), hbm, hbm, hbm,
+            const_spec(sums_two.shape), const_spec(bsum_up.shape),
+        ],
+        out_specs=[pair_spec(rows, width), hbm] + [whole(part, w) for w in widths] + [whole(4, bsum_up.shape[1])],
+        out_shape=[
+            jax.ShapeDtypeStruct((pairs, rows, width), LOW), jax.ShapeDtypeStruct((pairs, rows, width), LOW),
+        ]
+        + [jax.ShapeDtypeStruct((part, w), F32) for w in widths]
+        + [jax.ShapeDtypeStruct((4, bsum_up.shape[1]), F32)],
         scratch_shapes=scratch,
-        compiler_params=pltpu.CompilerParams(collective_id=ident, has_side_effects=True, vmem_limit_bytes=60 * 2**20),
-        name=f"reduce_grads_{ident}",
-    )(*ins)
+        compiler_params=pltpu.CompilerParams(collective_id=1, has_side_effects=True, vmem_limit_bytes=62 * 2**20),
+        name="backward_reduce",
+    )(tokens, dhid, qkv, prob, n1, w_one, vec, *grads, sums_two, bsum_up)
 
 
 def per_device(
@@ -623,37 +792,46 @@
     out_here, act, dpre, dhid, dlow, upl, sums_two, bsum_up = ffn(lens, off, n2, hid, cotangent, w_two, bias, vec)
 
     def grad(left, right):
-        cols = right.shape[2] // n_mp
         return jnp.einsum(
-            "rd,rmf->mdf", left.reshape(pairs * rows, width), right.reshape(pairs * rows, n_mp, cols),
+            "rd,rf->df", left.reshape(pairs * rows, width), right.reshape(pairs * rows, -1),
             preferred_element_type=F32,
         )
 
-    def reduce(grads, small, ident):
-        if direct:
-            return reduce_grads([g.astype(LOW) for g in grads], small, ident)
+    def reduce(grads, small):
         axes = ("mp", "dp")
         done = [
-            lax.psum_scatter(g.reshape(n_mp * width, -1), axes, scatter_dimension=0, tiled=True) for g in grads
+            lax.psum_scatter(
+                g.reshape(width, n_mp, -1).swapaxes(0, 1).reshape(n_mp * width, -1), axes,
+                scatter_dimension=0, tiled=True,
+            )
+            for g in grads
         ]
         if small is not None:
             done.append(lax.psum(small, axes))
         return done
 
-    def both(array):
-        other = lax.ppermute(array, "mp", [(0, 1), (1, 0)])
+    def both(array, other=None):
+        if other is None:
+            other = lax.ppermute(array, "mp", [(0, 1), (1, 0)])
         return jnp.where(mine == 0, jnp.concatenate([array, other]), jnp.concatenate([other, array]))
 
-    r_up, r_down, r_proj = reduce([grad(n2, dpre), grad(upl, act), grad(dlow, att)], None, 1)
-    tok_here, dqkv, sums_one, bsum_qkv = attention_backward(lens, off, tokens, dhid, qkv, prob, w_one, vec)
     block_out = both(out_here)
-    tokens_grad = both(tok_here)
-    flat = bsum_qkv[0].reshape(n_mp, 3, lw)
-    small = jnp.concatenate([
-        sums_one[0], sums_one[1], sums_two[2], sums_two[0], sums_two[1], sums_two[3],
-        flat[:, 0].reshape(-1), flat[:, 2].reshape(-1), bsum_up[0]])
-    r_qkv, small = reduce([grad(n1, dqkv)], small.reshape(8, -1), 2)
-    small = small.reshape(-1)
+    grads = [grad(n2, dpre), grad(upl, act), grad(dlow, att)]
+    if direct:
+        tok_here, tok_other, r_up, r_down, r_proj, r_qkv, small = backward_reduce(
+            tokens, dhid, qkv, prob, n1, w_one, vec, [g.astype(LOW) for g in grads], sums_two, bsum_up)
+        tokens_grad = both(tok_here, tok_other)
+        flat = small[1, : 3 * width].reshape(n_mp, 3, lw)
+        small = jnp.concatenate([
+            small[2], small[3, : 2 * width], flat[:, 0].reshape(-1), flat[:, 2].reshape(-1), small[0]])
+    else:
+        tok_here, dqkv, sums_one, bsum_qkv = attention_backward(lens, off, tokens, dhid, qkv, prob, w_one, vec)
+        tokens_grad = both(tok_here)
+        flat = bsum_qkv[0].reshape(n_mp, 3, lw)
+        small = jnp.concatenate([
+            sums_one[0], sums_one[1], sums_two[2], sums_two[0], sums_two[1], sums_two[3],
+            flat[:, 0].reshape(-1), flat[:, 2].reshape(-1), bsum_up[0]])
+        r_up, r_down, r_proj, r_qkv, small = reduce(grads + [grad(n1, dqkv)], small)
     place_dp = lax.axis_index("dp") * part
 
     def piece(i):

time: 445 us -> 331 us (0.74)
  Pallas kernels: 328 us -> 272 us
  local copies, waits for them, and re-layouts: 63.3 us -> 16 us
  matrix products: 30.5 us -> 21.9 us
    pallas_call x3 -> x1, Pallas kernels: 178 us -> 122 us  [backward_reduce(): pl.pallas_call(back_kernel, grid=(pairs,), in_specs=[hbm, pair_spec(rows,...]
    reshape x6 -> x0, local copies, waits for them, and re-layouts: 46.2 us -> none  [the longest x4 44.8 us: grad(): right.reshape(pairs * rows, n_mp, cols)]
    dot_general x4 -> x3, matrix products: 30.5 us -> 21.9 us  [grad(): jnp.einsum('rd,rf->df', left.reshape(pairs * rows, width), right.reshape(...]
    unnamed x41 -> x31, local copies, waits for them, and re-layouts: 9.76 us -> 9.67 us
  transfers between devices with their start and end apart: 2 -> 1, of which waited for: 0 -> 0; matrix products, arithmetic and copies ran while one was open for 20% -> 10% of each run, Pallas kernels for 32% -> 37%
where the time goes in v3:
time: 331 us
  Pallas kernels  272 us (82%)
  matrix products  21.9 us (7%)
  other arithmetic  17.9 us (5%)
  local copies, waits for them, and re-layouts  16 us (5%)
    pallas_call x1, Pallas kernels, backward_reduce(): pl.pallas_call(back_kernel, grid=(pairs,), in_specs=[hbm, pair_spec(rows,...  122 us
    pallas_call x1, Pallas kernels, gather_weights(): pl.pallas_call(gather_kernel, in_specs=[vm] * 4, out_specs=[hbm] * 3, out...  79.6 us
    pallas_call x1, Pallas kernels, attention_forward(): pl.pallas_call(attn_kernel, grid_spec=pltpu.PrefetchScalarGridSpec(num_sc...  36 us
    pallas_call x1, Pallas kernels, ffn(): pl.pallas_call(ffn_kernel, grid_spec=pltpu.PrefetchScalarGridSpec(num_sca...  34.8 us
    dot_general x3, matrix products, grad(): jnp.einsum('rd,rf->df', left.reshape(pairs * rows, width), right.reshape(...  21.9 us
    unnamed x31, local copies, waits for them, and re-layouts  9.67 us
    select_n x2, other arithmetic, both(): jnp.where(mine == 0, jnp.concatenate([array, other]), jnp.concatenate([ot...  6.95 us
  transfers between devices with their start and end apart: 1, of which 0 were waited for; matrix products, arithmetic and copies ran while one was open for 10% of the time, Pallas kernels for 37%

profile of v3, /device:TPU:8, one launch (start us, length us, event | category | flops | bytes accessed | tf_op | source)
XLA Modules:
  0.0 330.6 jit_solution(8984641559558585393)
XLA Ops:
  0.7 1.0 convert_bitcast_fusion.1
  1.6 0.9 convert_bitcast_fusion.2
  2.5 0.7 convert_bitcast_fusion.8
  3.2 0.1 copy.38
  3.3 0.7 convert_bitcast_fusion.7
  3.9 0.1 copy.39
  4.1 0.7 convert_bitcast_fusion.6
  4.7 0.1 copy.40
  4.8 0.7 convert_bitcast_fusion.5
  5.5 0.1 copy.41
  5.6 0.7 convert_bitcast_fusion.4
  6.3 0.1 copy.42
  6.4 0.7 convert_bitcast_fusion.3
  7.0 0.1 copy.43
  7.1 1.0 convert_bitcast_fusion.s2
  8.1 1.0 convert_element_type.22.s1
  9.1 0.7 convert.50
  9.8 0.7 convert.49
  10.5 1.2 dynamic-slice_add_fusion.lens
  11.8 0.1 concatenate.26.s0
  11.9 79.6 %gather_weights.1 = (bf16[2,768,1664]{2,1,0:T(8,128)(2,1)S(1)}, bf16[2,768,3072]{2,1,0:T(8,128)(2,1)S(1)}, f32[2,8,2304]{2,1,0:T(8,128)S(1)}) custom-call(bf16[48,1664]{1,0:T(8,128)(2,1)S(1)} %concatenate.26.s0, bf16[48,1536]{1,0:T(8,128)(2,1)S(1)} %convert_element_type.22.s1, bf16[48,1536]{1,0:T(8,128)(2,1)S(1)} %convert_bitcast_fusion.s2, ...), custom_call_target="tpu_custom_call" | custom-call | tf_op jit(solution)/shard_map/gather_weights/pallas_call | solution.py:423
  91.5 0.0 copy-start
  91.6 2.2 copy-done
  93.8 3.6 %copy-done.1 = bf16[2,768,3072]{2,1,0:T(8,128)(2,1)} copy-done((bf16[2,768,3072]{2,1,0:T(8,128)(2,1)}, bf16[2,768,3072]{2,1,0:T(8,128)(2,1)S(1)}, u32[]{:S(2)}) %copy-start.1) | copy-done | bytes 9437208
  97.4 0.7 copy-done.2
  98.1 36.0 %attention_forward.1 = (bf16[4,280,2304]{2,1,0:T(8,128)(2,1)}, bf16[4,280,768]{2,1,0:T(8,128)(2,1)}, bf16[4,12,280,280]{3,2,1,0:T(8,128)(2,1)}, f32[4,280,768]{2...) custom-call(s32[4]{0:T(128)} %dynamic-slice_add_fusion.lens, ...), custom_call_target="tpu_custom_call" | custom-call | tf_op jit(solution)/shard_map/attention_forward/pallas_call | solution.py:103
  134.0 34.8 %feed_forward.1 = (bf16[4,280,768]{2,1,0:T(8,128)(2,1)}, bf16[4,280,3072]{2,1,0:T(8,128)(2,1)}, bf16[4,280,3072]{2,1,0:T(8,128)(2,1)}, f32[4,280,768]{2,1,0:T(8,...) custom-call(s32[4]{0:T(128)} %dynamic-slice_add_fusion.lens, ...), custom_call_target="tpu_custom_call" | custom-call | tf_op jit(solution)/shard_map/feed_forward/pallas_call | solution.py:178
  168.8 1.5 collective-permute-start
  170.3 11.2 %bitcast_convert_fusion.1 = bf16[768,3072]{1,0:T(8,128)(2,1)} fusion(bf16[4,280,768]{2,1,0:T(8,128)(2,1)S(1)} %copy-done.3, bf16[4,280,3072]{2,1,0:T(8,128)(2,1)} %get-tuple-element.50), kind=kOutput, calls=%fused_computation.1 | convolution fusion | flops 5287182336 | bytes 13320192 | tf_op jit(solution)/shard_map/rd,rf->df/dot_general | solution.py:795
  181.5 2.8 bitcast_convert_fusion.2
  184.3 0.6 copy-done.8
  184.9 0.5 copy-done.10
  185.4 8.0 %bitcast_convert_fusion = bf16[768,3072]{1,0:T(8,128)(2,1)} fusion(bf16[4,280,768]{2,1,0:T(8,128)(2,1)S(1)} %copy-done.10, bf16[4,280,3072]{2,1,0:T(8,128)(2,1)S(1)} %copy-done.8), kind=kOutput, calls=%fused_computation | convolution fusion | flops 5287182336 | bytes 13320192 | tf_op jit(solution)/shard_map/rd,rf->df/dot_general | solution.py:795
  193.3 122.0 %backward_reduce.1 = (bf16[4,280,768]{2,1,0:T(8,128)(2,1)}, bf16[4,280,768]{2,1,0:T(8,128)(2,1)}, f32[48,1536]{1,0:T(8,128)}, f32[48,1536]{1,0:T(8,128)}, f32[48...) custom-call(bf16[8,280,768]{2,1,0:T(8,128)(2,1)} %tok_all.1, f32[4,280,768]{2,1,0:T(8,128)} %get-tuple-element.46.dhid_ref, ...), custom_call_target="tpu_custom_call" | custom-call | tf_op jit(solution)/shard_map/backward_reduce/pallas_call | solution.py:738
  315.3 0.9 fusion
  316.3 0.8 slice_reduce_fusion
  317.1 0.7 dynamic_slice.38
  317.8 0.1 fusion.2
  317.9 1.6 copy.48
  319.5 0.6 pad_maximum_fusion.1
  320.1 0.8 slice_reduce_fusion.1
  321.0 0.6 fusion.1
  321.6 4.8 %maximum_select_fusion.1 = bf16[8,280,768]{2,1,0:T(8,128)(2,1)} fusion(bf16[4,280,768]{2,1,0:T(8,128)(2,1)} %get-tuple-element.58, bf16[4,280,768]{2,1,0:T(8,128)(2,1)} %get-tuple-element.57, pred[]{:T(512)S(6)} %eq.4), kind=kLoop, calls=%fused_computation.3 | loop fusion | flops 5160960 | bytes 6881281 | tf_op jit(solution)/shard_map/jit(_where)/select_n | solution.py:816
  326.4 0.0 collective-permute-done
  326.4 2.2 maximum_select_fusion
  328.6 0.6 copy.56
  329.2 0.7 copy.57
  329.9 0.7 copy.58
  (35 shorter events, 0.2 us)
Async XLA Ops:
  91.5 2.2 copy-start
  93.8 3.6 %copy-start.1 = (bf16[2,768,3072]{2,1,0:T(8,128)(2,1)}, bf16[2,768,3072]{2,1,0:T(8,128)(2,1)S(1)}, u32[]{:S(2)}) copy-start(bf16[2,768,3072]{2,1,0:T(8,128)(2,1)S(1)} %get-tuple-element.43.w_ref) | copy-start | bytes 28311556
  97.4 0.7 copy-start.2
  134.0 36.3 %copy-start.3 = (bf16[4,280,768]{2,1,0:T(8,128)(2,1)S(1)}, bf16[4,280,768]{2,1,0:T(8,128)(2,1)}, u32[]{:S(2)}) copy-start(bf16[4,280,768]{2,1,0:T(8,128)(2,1)} %get-tuple-element.41.n2_ref) | copy-start | bytes 5160964
  168.8 157.5 %collective-permute-start = (bf16[4,280,768]{2,1,0:T(8,128)(2,1)}, bf16[4,280,768]{2,1,0:T(8,128)(2,1)S(1)}, u32[]{:S(2)}, u32[]{:S(2)}) collective-permute-start(bf16[4,280,768]{2,1,0:T(8,128)(2,1)} %get-tuple-element.45), channel_id=1, source_target_pairs={{0,1},{1,0},{2,3},{3,2},{4,5},{5,4},{6,7},{7,6},{8,9},{9,8},{10,11... | collective-permute-start | bytes 5160968 | tf_op jit(solution)/shard_map/ppermute | solution.py:815
  170.3 11.2 %copy-start.9 = (bf16[4,280,768]{2,1,0:T(8,128)(2,1)S(1)}, bf16[4,280,768]{2,1,0:T(8,128)(2,1)}, u32[]{:S(2)}) copy-start(bf16[4,280,768]{2,1,0:T(8,128)(2,1)} %get-tuple-element.54) | copy-start | bytes 5160964
  170.3 11.2 %copy-start.11 = (bf16[4,280,768]{2,1,0:T(8,128)(2,1)S(1)}, bf16[4,280,768]{2,1,0:T(8,128)(2,1)}, u32[]{:S(2)}) copy-start(bf16[4,280,768]{2,1,0:T(8,128)(2,1)} %get-tuple-element.53) | copy-start | bytes 5160964
  181.5 3.4 %copy-start.8 = (bf16[4,280,3072]{2,1,0:T(8,128)(2,1)S(1)}, bf16[4,280,3072]{2,1,0:T(8,128)(2,1)}, u32[]{:S(2)}) copy-start(bf16[4,280,3072]{2,1,0:T(8,128)(2,1)} %get-tuple-element.52) | copy-start | bytes 20643844
  181.5 3.8 %copy-start.10 = (bf16[4,280,768]{2,1,0:T(8,128)(2,1)S(1)}, bf16[4,280,768]{2,1,0:T(8,128)(2,1)}, u32[]{:S(2)}) copy-start(bf16[4,280,768]{2,1,0:T(8,128)(2,1)} %get-tuple-element.51) | copy-start | bytes 5160964
  321.6 4.8 %copy-start.4 = (bf16[4,280,768]{2,1,0:T(8,128)(2,1)S(1)}, bf16[4,280,768]{2,1,0:T(8,128)(2,1)}, u32[]{:S(2)}) copy-start(bf16[4,280,768]{2,1,0:T(8,128)(2,1)} %get-tuple-element.45) | copy-start | bytes 5160964
  326.4 2.2 copy-start.7
  326.4 2.8 copy-start.6
  326.4 3.5 %copy-start.5 = (f32[48,1536]{1,0:T(8,128)S(1)}, f32[48,1536]{1,0:T(8,128)}, u32[]{:S(2)}) copy-start(f32[48,1536]{1,0:T(8,128)} %get-tuple-element.63) | copy-start | bytes 884740

commit v4 on v3

--- a/solution.py
+++ b/solution.py
@@ -32,18 +32,12 @@
     return lax.broadcasted_iota(jnp.int32, (rows, 1), 0)
 
 
-def attn_kernel(lens, off, x_ref, w_ref, bias_ref, qkv_ref, att_ref, prob_ref, hid_ref, n1_ref, n2_ref, vec_ref):
-    p = pl.program_id(0)
-    rows, width = x_ref.shape[1], x_ref.shape[2]
+def attn_body(p, count, x, w_ref, bias_ref, vec_ref, qkv_ref, att_ref, prob_ref, hid_ref, n1_ref, n2_ref, hook):
+    rows, width = x.shape
     groups = w_ref.shape[0]
     lw = width // groups
     tiles = lw // 128
-
-    @pl.when(p == 0)
-    def _():
-        vec_ref[...] = w_ref[0, :, 4 * lw :].astype(F32).T[:8]
-
-    x = x_ref[0].astype(F32)
+    x = x.astype(F32)
     xhat, _ = moments(x)
     n1 = (xhat * vec_ref[0:1] + vec_ref[1:2]).astype(LOW)
     n1_ref[0] = n1
@@ -55,12 +49,11 @@
         qkv_ref[0, :, base + 2 * lw : base + 3 * lw] = (
             y[:, 2 * lw :] + bias_ref[m, 0:1, lw : 2 * lw]
         ).astype(LOW)
-    count = lens[p]
     keep = row_ids(rows) < count
     first = lax.broadcasted_iota(jnp.int32, (1, 128), 1) < HEAD_DIM
 
     def pair(hp, carry):
-        base = (hp // tiles) * 3 * lw + (hp % tiles) * 128
+        base = (hp // tiles) * 3 * lw + lax.rem(hp, tiles) * 128
 
         def cols(t):
             return pl.ds(pl.multiple_of(base + t * lw, 128), 128)
@@ -78,6 +71,7 @@
             prob_ref[0, hp * 2 + h] = pt
             outs.append(dot(v2t[h * HEAD_DIM : (h + 1) * HEAD_DIM], pt))
         att_ref[0, :, pl.ds(pl.multiple_of(hp * 128, 128), 128)] = jnp.concatenate(outs, axis=0).T.astype(LOW)
+        hook(hp)
         return carry
 
     lax.fori_loop(0, groups * tiles, pair, 0)
@@ -86,6 +80,18 @@
     hid_ref[0] = hid
     xhat2, _ = moments(hid)
     n2_ref[0] = (xhat2 * vec_ref[3:4] + vec_ref[4:5]).astype(LOW)
+
+
+def attn_kernel(lens, off, x_ref, w_ref, bias_ref, qkv_ref, att_ref, prob_ref, hid_ref, n1_ref, n2_ref, vec_ref):
+    p = pl.program_id(0)
+    lw = x_ref.shape[2] // w_ref.shape[0]
+
+    @pl.when(p == 0)
+    def _():
+        vec_ref[...] = w_ref[0, :, 4 * lw :].astype(F32).T[:8]
+
+    attn_body(p, lens[p], x_ref[0], w_ref, bias_ref, vec_ref, qkv_ref, att_ref, prob_ref, hid_ref, n1_ref, n2_ref,
+              lambda hp: None)
 
 
 def const_spec(shape):
@@ -322,120 +328,198 @@
     return peers
 
 
-def gather_kernel(s0, s1, s2, b_in, w_one, w_two, b_out, send, recv, bsem, local):
+def gather_attn_kernel(lens, tok_all, first_ref, second_ref, b_in,
+                       w_one_out, w_two, b_out, qkv_ref, att_ref, prob_ref, hid_ref, n1_ref, n2_ref, vec_ref,
+                       w_one, bias, xbuf, send, recv, bsem, local):
+    p = pl.program_id(0)
     z, y, c, m = place()
     (y1, m1), (y2, m2) = flips(y, c, m)
-    part, cols = s1.shape
-    peers = greet(z, y, c, m)
-    pz, one, two, sib = peers[:3], peers[3], peers[4], peers[5]
-    shards = (s0, s1, s2)
+    pairs, rows, width = xbuf.shape
+    part = first_ref.shape[0]
+    cols = second_ref.shape[1] // 2
+    lw = width // 2
+    per_pair = width // 128
+    me = index(z, y, c)
+    one, two, sib = (index(z, y1, c), m1), (index(z, y2, c), m2), (index(z, y, 1 - c), m)
 
     def spot(g, dp, mp):
-        rows = pl.ds(pl.multiple_of(dp * part, part), part)
-        if g == 0:
-            return w_one.at[mp, rows]
-        return w_two.at[mp, rows, (g - 1) * cols : g * cols]
-
-    started = []
-    count = [0, 0, 0]
-
-    def push(g, src, dp, mp, to):
-        copy = pltpu.make_async_remote_copy(
-            src_ref=src, dst_ref=spot(g, dp, mp), send_sem=send.at[g, count[g]],
-            recv_sem=recv.at[g, mp * (Z * Y * C) + dp],
+        at = pl.ds(pl.multiple_of(dp * part, part), part)
+        if g is None:
+            return w_one.at[mp, at]
+        return w_two.at[mp, at, pl.ds(pl.multiple_of(g * cols, 128), cols)]
+
+    def shard(g):
+        return first_ref if g is None else second_ref.at[:, pl.ds(pl.multiple_of(g * cols, 128), cols)]
+
+    def row(g):
+        return 0 if g is None else g + 1
+
+    def copy_of(g, src, dst, out_sem, in_sem, to):
+        return pltpu.make_async_remote_copy(
+            src_ref=src, dst_ref=dst, send_sem=send.at[row(g), out_sem], recv_sem=recv.at[row(g), in_sem],
             device_id={"dp": to[0], "mp": to[1]}, device_id_type=MESH_ID,
         )
-        count[g] += 1
-        copy.start()
-        started.append(copy)
+
+    def push(g, src, dp, mp, to, sem):
+        copy_of(g, src, spot(g, dp, mp), sem, mp * (Z * Y * C) + dp, to).start()
 
     def arrived(g, dp, mp):
         at = spot(g, dp, mp)
-        pltpu.make_async_remote_copy(
-            src_ref=at, dst_ref=at, send_sem=send.at[g, 0], recv_sem=recv.at[g, mp * (Z * Y * C) + dp],
-            device_id={"dp": sib[0], "mp": sib[1]}, device_id_type=MESH_ID,
-        ).wait_recv()
+        copy_of(g, at, at, 0, mp * (Z * Y * C) + dp, sib).wait_recv()
         return at
 
-    me = index(z, y, c)
+    def own_z(g):
+        for k in (1, 3, 2):
+            push(g, shard(g), me, m, (index(lax.rem(z + k, Z), y, c), m), k - 1)
+
+    def own_near(g):
+        for n, to in enumerate((one, two, sib)):
+            push(g, shard(g), me, m, to, 3 + n)
+
+    def event_z(g, i):
+        dp = index(lax.rem(z + 1 + lax.rem(2 * i, 3), Z), y, c)
+        at = arrived(g, dp, m)
+        for n, to in enumerate((one, two, sib)):
+            push(g, at, dp, m, to, 6 + 3 * i + n)
+
+    def event_one(g, i):
+        dp = index(lax.rem(z + i, Z), y1, c)
+        at = arrived(g, dp, m1)
+        for n, to in enumerate((two, sib)):
+            push(g, at, dp, m1, to, 15 + 2 * i + n)
+
+    def event_two(g, i):
+        far = lax.rem(i, 2)
+        yy = y2 + far * (1 - y - y2)
+        mm = m2 + far * (1 - m - m2)
+        dp = index(lax.rem(z + i // 2, Z), yy, c)
+        push(g, arrived(g, dp, mm), dp, mm, sib, 23 + i)
+
+    def event_core(g, i):
+        arrived(g, index(i // 4, lax.rem(i // 2, 2), 1 - c), lax.rem(i, 2))
+
+    def loop(n, event, g):
+        def run(i, carry):
+            event(g, i)
+            return carry
+
+        lax.fori_loop(0, n, run, 0)
+
     bias_copy = pltpu.make_async_remote_copy(
-        src_ref=b_in, dst_ref=b_out.at[m], send_sem=bsem.at[0], recv_sem=bsem.at[1],
+        src_ref=b_in, dst_ref=bias.at[m], send_sem=bsem.at[0], recv_sem=bsem.at[1],
         device_id={"dp": me, "mp": 1 - m}, device_id_type=MESH_ID,
     )
-    bias_copy.start()
-    locals_ = [pltpu.make_async_copy(b_in, b_out.at[m], local.at[3])]
-    for g in range(3):
-        for to in pz + [one, two, sib]:
-            push(g, shards[g], me, m, to)
-        locals_.append(pltpu.make_async_copy(shards[g], spot(g, me, m), local.at[g]))
-    for copy in locals_:
-        copy.start()
-
-    def stage_z(g):
-        for k in (1, 3, 2):
-            dp = index(lax.rem(z + k, Z), y, c)
-            at = arrived(g, dp, m)
-            for to in (one, two, sib):
-                push(g, at, dp, m, to)
-
-    def stage_one(g):
-        for k in (0, 1, 3, 2):
-            dp = index(lax.rem(z + k, Z), y1, c)
-            at = arrived(g, dp, m1)
-            for to in (two, sib):
-                push(g, at, dp, m1, to)
-
-    def stage_two(g):
-        for k in (0, 1, 3, 2):
-            for yy, mm in ((y2, m2), (1 - y, 1 - m)):
-                dp = index(lax.rem(z + k, Z), yy, c)
-                push(g, arrived(g, dp, mm), dp, mm, sib)
-
-    def stage_core(g):
-        for k in range(Z):
-            for yy in range(Y):
-                for mm in range(2):
-                    arrived(g, index(k, yy, 1 - c), mm)
-
-    stage_z(0)
-    stage_one(0)
-    stage_z(1)
-    stage_two(0)
-    stage_one(1)
-    stage_z(2)
-    stage_two(1)
-    stage_one(2)
-    stage_two(2)
-    for g in range(3):
-        stage_core(g)
-    bias_copy.wait()
-    for copy in locals_:
-        copy.wait()
-    for copy in started:
-        copy.wait_send()
-
-
-def gather_weights(first, second_a, second_b, bias):
-    part, cols = second_a.shape
-    vm = pl.BlockSpec(memory_space=pltpu.VMEM)
+    x_copy = pltpu.make_async_copy(tok_all.at[pl.ds(m * pairs, pairs)], xbuf, local.at[0])
+    mine = [
+        pltpu.make_async_copy(b_in, bias.at[m], local.at[1]),
+        pltpu.make_async_copy(first_ref, spot(None, me, m), local.at[2]),
+    ]
+    mine_two = [pltpu.make_async_copy(shard(g), spot(g, me, m), local.at[3 + g]) for g in range(2)]
+    keep_one = pltpu.make_async_copy(w_one, w_one_out, local.at[5])
+    keep_bias = pltpu.make_async_copy(bias, b_out, local.at[6])
+
+    @pl.when(p == 0)
+    def _():
+        for copy in mine + mine_two:
+            copy.start()
+        x_copy.start()
+        greet(z, y, c, m)
+        own_z(None)
+        own_near(None)
+        bias_copy.start()
+        own_z(0)
+        own_z(1)
+        loop(3, event_z, None)
+        loop(4, event_one, None)
+        loop(8, event_two, None)
+        for copy in mine + [x_copy, bias_copy]:
+            copy.wait()
+        loop(16, event_core, None)
+        keep_one.start()
+        keep_bias.start()
+        vec_ref[...] = w_one[0, :, 4 * lw :].astype(F32).T[:8]
+
+    def hook(hp):
+        step = p * per_pair + hp
+
+        def event(e, carry):
+            g = e // 16
+            i = lax.rem(e, 16)
+
+            @pl.when(i == 0)
+            def _():
+                own_near(g)
+
+            @pl.when((i >= 1) & (i < 4))
+            def _():
+                event_z(g, i - 1)
+
+            @pl.when((i >= 4) & (i < 8))
+            def _():
+                event_one(g, i - 4)
+
+            @pl.when(i >= 8)
+            def _():
+                event_two(g, i - 8)
+
+            return carry
+
+        total = pairs * per_pair
+        lax.fori_loop(step * 32 // total, (step + 1) * 32 // total, event, 0)
+
+    attn_body(p, lens[p], xbuf[p], w_one, bias, vec_ref, qkv_ref, att_ref, prob_ref, hid_ref, n1_ref, n2_ref, hook)
+
+    @pl.when(p == pairs - 1)
+    def _():
+        for g in range(2):
+            loop(16, event_core, g)
+        for copy in mine_two + [keep_one, keep_bias]:
+            copy.wait()
+        for g in (None, 0, 1):
+            def sent(i, carry):
+                copy_of(g, shard(g), shard(g), i, 0, sib).wait_send()
+                return carry
+
+            lax.fori_loop(0, 31, sent, 0)
+
+
+def gather_attention(lens, tokens, first, second, bias):
+    pairs = lens.shape[0]
+    _, rows, width = tokens.shape
+    part = first.shape[0]
+    total = Z * Y * C
     hbm = pl.BlockSpec(memory_space=pl.ANY)
-    total = Z * Y * C
+    out = lambda dt, *s: jax.ShapeDtypeStruct((pairs,) + s, dt)
     return pl.pallas_call(
-        gather_kernel,
-        in_specs=[vm] * 4,
-        out_specs=[hbm] * 3,
+        gather_attn_kernel,
+        grid_spec=pltpu.PrefetchScalarGridSpec(
+            num_scalar_prefetch=1,
+            grid=(pairs,),
+            in_specs=[hbm, const_spec(first.shape), const_spec(second.shape), const_spec(bias.shape)],
+            out_specs=[
+                hbm, hbm, hbm,
+                pair_spec(rows, 3 * width), pair_spec(rows, width), pair_spec(HEADS, rows, rows),
+                pair_spec(rows, width), pair_spec(rows, width), pair_spec(rows, width),
+                pl.BlockSpec((8, width), lambda *_: (0, 0)),
+            ],
+            scratch_shapes=[
+                pltpu.VMEM((2, total * part, first.shape[1]), LOW), pltpu.VMEM((2,) + bias.shape, F32),
+                pltpu.VMEM((pairs, rows, width), LOW),
+                pltpu.SemaphoreType.DMA((3, 31)), pltpu.SemaphoreType.DMA((3, 32)),
+                pltpu.SemaphoreType.DMA((2,)), pltpu.SemaphoreType.DMA((7,)),
+            ],
+        ),
         out_shape=[
             jax.ShapeDtypeStruct((2, total * part, first.shape[1]), LOW),
-            jax.ShapeDtypeStruct((2, total * part, 2 * cols), LOW),
+            jax.ShapeDtypeStruct((2, total * part, second.shape[1]), LOW),
             jax.ShapeDtypeStruct((2,) + bias.shape, F32),
+            out(LOW, rows, 3 * width), out(LOW, rows, width), out(LOW, HEADS, rows, rows),
+            out(F32, rows, width), out(LOW, rows, width), out(LOW, rows, width),
+            jax.ShapeDtypeStruct((8, width), F32),
         ],
-        scratch_shapes=[
-            pltpu.SemaphoreType.DMA((3, 31)), pltpu.SemaphoreType.DMA((3, 32)),
-            pltpu.SemaphoreType.DMA((2,)), pltpu.SemaphoreType.DMA((4,)),
-        ],
-        compiler_params=pltpu.CompilerParams(collective_id=0, has_side_effects=True, vmem_limit_bytes=32 * 2**20),
-        name="gather_weights",
-    )(first, second_a, second_b, bias)
+        compiler_params=pltpu.CompilerParams(collective_id=0, has_side_effects=True, vmem_limit_bytes=60 * 2**20),
+        name="gather_attention",
+    )(lens, tokens, first, second, bias)
 
 
 BLOCKS = 31
@@ -775,20 +859,17 @@
     first = jnp.concatenate(
         [w_qkv.reshape(part, 3 * lw), w_proj.T, vectors, jnp.zeros((part, EXTRA - 6), F32)], axis=1
     ).astype(LOW)
-    second_a = w_up.astype(LOW)
-    second_b = w_down.T.astype(LOW)
+    second = jnp.concatenate([w_up, w_down.T], axis=1).astype(LOW)
     bias = jnp.concatenate([b_qv.reshape(-1), b_up]).astype(LOW).astype(F32)
     bias = jnp.broadcast_to(bias, (8,) + bias.shape)
     if direct:
-        w_one, w_two, bias = gather_weights(first, second_a, second_b, bias)
+        w_one, w_two, bias, qkv, att, prob, hid, n1, n2, vec = gather_attention(lens, tokens, first, second, bias)
     else:
         both_axes = ("mp", "dp")
         w_one = lax.all_gather(first, both_axes, axis=0, tiled=True).reshape(n_mp, width, -1)
-        second = jnp.concatenate([second_a, second_b], axis=1)
         w_two = lax.all_gather(second, both_axes, axis=0, tiled=True).reshape(n_mp, width, -1)
         bias = lax.all_gather(bias, "mp", axis=0)
-
-    qkv, att, prob, hid, n1, n2, vec = attention_forward(lens, off, tokens, w_one, bias)
+        qkv, att, prob, hid, n1, n2, vec = attention_forward(lens, off, tokens, w_one, bias)
     out_here, act, dpre, dhid, dlow, upl, sums_two, bsum_up = ffn(lens, off, n2, hid, cotangent, w_two, bias, vec)
 
     def grad(left, right):

time: 331 us -> 313 us (0.946)
  Pallas kernels: 272 us -> 260 us
  local copies, waits for them, and re-layouts: 16 us -> 10.8 us
    pallas_call x2 -> x1, Pallas kernels: 116 us -> 94.1 us  [gather_attention(): pl.pallas_call(gather_attn_kernel, grid_spec=pltpu.PrefetchScalarGridSpec...]
    pallas_call x1, Pallas kernels: 122 us -> 131 us  [backward_reduce(): pl.pallas_call(back_kernel, grid=(pairs,), in_specs=[hbm, pair_spec(rows,...]
    unnamed x31 -> x25, local copies, waits for them, and re-layouts: 9.67 us -> 3.14 us
  transfers between devices with their start and end apart: 1 -> 1, of which waited for: 0 -> 0; matrix products, arithmetic and copies ran while one was open for 10% -> 10% of each run, Pallas kernels for 37% -> 42%
where the time goes in v4:
time: 313 us; the launch traced here: 312 us
  Pallas kernels  260 us (83%)
  matrix products  21.8 us (7%)
  other arithmetic  18.6 us (6%)
  local copies, waits for them, and re-layouts  10.8 us (3%)
    pallas_call x1, Pallas kernels, backward_reduce(): pl.pallas_call(back_kernel, grid=(pairs,), in_specs=[hbm, pair_spec(rows,...  131 us
    pallas_call x1, Pallas kernels, gather_attention(): pl.pallas_call(gather_attn_kernel, grid_spec=pltpu.PrefetchScalarGridSpec...  94.1 us
    pallas_call x1, Pallas kernels, ffn(): pl.pallas_call(ffn_kernel, grid_spec=pltpu.PrefetchScalarGridSpec(num_sca...  34.7 us
    dot_general x3, matrix products, grad(): jnp.einsum('rd,rf->df', left.reshape(pairs * rows, width), right.reshape(...  21.8 us
    select_n x2, other arithmetic, both(): jnp.where(mine == 0, jnp.concatenate([array, other]), jnp.concatenate([ot...  6.88 us
  transfers between devices with their start and end apart: 1, of which 0 were waited for; matrix products, arithmetic and copies ran while one was open for 10% of the time, Pallas kernels for 42%

profile of v4, /device:TPU:8, one launch (start us, length us, event | category | flops | bytes accessed | tf_op | source)
XLA Modules:
  0.0 312.5 jit_solution(1741028311591743402)
XLA Ops:
  0.7 1.0 convert.56
  1.6 1.0 convert_bitcast_fusion
  2.6 1.0 convert_bitcast_fusion.1
  3.6 0.9 convert_bitcast_fusion.2
  4.5 0.7 convert_bitcast_fusion.8
  5.1 0.1 copy.38
  5.3 0.7 convert_bitcast_fusion.7
  5.9 0.1 copy.39
  6.0 0.7 convert_bitcast_fusion.6
  6.7 0.1 copy.40
  6.8 0.7 convert_bitcast_fusion.5
  7.5 0.1 copy.41
  7.6 0.7 convert_bitcast_fusion.4
  8.2 0.1 copy.42
  8.3 0.7 convert_bitcast_fusion.3
  9.0 0.1 copy.43
  9.1 0.7 convert.59
  9.8 0.7 convert.58
  10.5 1.2 dynamic-slice_add_fusion.lens
  11.7 0.7 pad_maximum_fusion.second_ref
  12.5 0.8 concatenate.30.first_ref
  13.3 0.6 broadcast_in_dim.7.b_in
  13.9 94.1 %gather_attention.1 = (bf16[2,768,1664]{2,1,0:T(8,128)(2,1)}, bf16[2,768,3072]{2,1,0:T(8,128)(2,1)}, f32[2,8,2304]{2,1,0:T(8,128)}, bf16[4,280,2304]{2,1,0:T(8,1...) custom-call(s32[4]{0:T(128)} %dynamic-slice_add_fusion.lens, ...), custom_call_target="tpu_custom_call" | custom-call | tf_op jit(solution)/shard_map/gather_attention/pallas_call | solution.py:493
  108.0 0.0 copy-start
  108.0 34.7 %feed_forward.1 = (bf16[4,280,768]{2,1,0:T(8,128)(2,1)}, bf16[4,280,3072]{2,1,0:T(8,128)(2,1)}, bf16[4,280,3072]{2,1,0:T(8,128)(2,1)}, f32[4,280,768]{2,1,0:T(8,...) custom-call(s32[4]{0:T(128)} %dynamic-slice_add_fusion.lens, ...), custom_call_target="tpu_custom_call" | custom-call | tf_op jit(solution)/shard_map/feed_forward/pallas_call | solution.py:184
  142.7 0.9 collective-permute-start
  143.6 11.0 %bitcast_convert_fusion.1 = bf16[768,3072]{1,0:T(8,128)(2,1)} fusion(bf16[4,280,768]{2,1,0:T(8,128)(2,1)S(1)} %copy-done, bf16[4,280,3072]{2,1,0:T(8,128)(2,1)} %get-tuple-element.50), kind=kOutput, calls=%fused_computation.1 | convolution fusion | flops 5287182336 | bytes 13320192 | tf_op jit(solution)/shard_map/rd,rf->df/dot_general | solution.py:876
  154.6 0.0 copy-done.8
  154.6 2.8 bitcast_convert_fusion.2
  157.4 0.5 copy-done.5
  157.9 0.5 copy-done.7
  158.4 8.0 %bitcast_convert_fusion = bf16[768,3072]{1,0:T(8,128)(2,1)} fusion(bf16[4,280,768]{2,1,0:T(8,128)(2,1)S(1)} %copy-done.7, bf16[4,280,3072]{2,1,0:T(8,128)(2,1)S(1)} %copy-done.5), kind=kOutput, calls=%fused_computation | convolution fusion | flops 5287182336 | bytes 13320192 | tf_op jit(solution)/shard_map/rd,rf->df/dot_general | solution.py:876
  166.4 130.8 %backward_reduce.1 = (bf16[4,280,768]{2,1,0:T(8,128)(2,1)}, bf16[4,280,768]{2,1,0:T(8,128)(2,1)}, f32[48,1536]{1,0:T(8,128)}, f32[48,1536]{1,0:T(8,128)}, f32[48...) custom-call(bf16[8,280,768]{2,1,0:T(8,128)(2,1)} %tok_all.3, f32[4,280,768]{2,1,0:T(8,128)} %get-tuple-element.45.dhid_ref, ...), custom_call_target="tpu_custom_call" | custom-call | tf_op jit(solution)/shard_map/backward_reduce/pallas_call | solution.py:822
  297.2 0.9 fusion
  298.2 0.8 slice_reduce_fusion
  299.1 0.7 dynamic_slice.38
  299.7 0.1 fusion.2
  299.8 1.6 copy.48
  301.5 0.6 pad_maximum_fusion.2
  302.0 0.8 slice_reduce_fusion.1
  302.9 0.6 fusion.1
  303.5 4.7 %maximum_select_fusion.1 = bf16[8,280,768]{2,1,0:T(8,128)(2,1)} fusion(bf16[4,280,768]{2,1,0:T(8,128)(2,1)} %get-tuple-element.58, bf16[4,280,768]{2,1,0:T(8,128)(2,1)} %get-tuple-element.57, pred[]{:T(512)S(6)} %eq.4), kind=kLoop, calls=%fused_computation.3 | loop fusion | flops 5160960 | bytes 6881281 | tf_op jit(solution)/shard_map/jit(_where)/select_n | solution.py:897
  308.2 0.0 collective-permute-done
  308.2 0.0 copy-done.1
  308.2 2.2 maximum_select_fusion
  310.4 0.6 copy.56
  311.0 0.7 copy.57
  311.8 0.7 copy.58
  (29 shorter events, 0.2 us)
Async XLA Ops:
  108.0 35.6 %copy-start = (bf16[4,280,768]{2,1,0:T(8,128)(2,1)S(1)}, bf16[4,280,768]{2,1,0:T(8,128)(2,1)}, u32[]{:S(2)}) copy-start(bf16[4,280,768]{2,1,0:T(8,128)(2,1)} %get-tuple-element.39.n2_ref) | copy-start | bytes 5160964
  142.7 165.5 %collective-permute-start = (bf16[4,280,768]{2,1,0:T(8,128)(2,1)}, bf16[4,280,768]{2,1,0:T(8,128)(2,1)S(1)}, u32[]{:S(2)}, u32[]{:S(2)}) collective-permute-start(bf16[4,280,768]{2,1,0:T(8,128)(2,1)} %get-tuple-element.44), channel_id=1, source_target_pairs={{0,1},{1,0},{2,3},{3,2},{4,5},{5,4},{6,7},{7,6},{8,9},{9,8},{10,11... | collective-permute-start | bytes 5160968 | tf_op jit(solution)/shard_map/ppermute | solution.py:896
  143.6 11.0 %copy-start.6 = (bf16[4,280,768]{2,1,0:T(8,128)(2,1)S(1)}, bf16[4,280,768]{2,1,0:T(8,128)(2,1)}, u32[]{:S(2)}) copy-start(bf16[4,280,768]{2,1,0:T(8,128)(2,1)} %get-tuple-element.54) | copy-start | bytes 5160964
  143.6 11.0 %copy-start.8 = (bf16[4,280,768]{2,1,0:T(8,128)(2,1)S(1)}, bf16[4,280,768]{2,1,0:T(8,128)(2,1)}, u32[]{:S(2)}) copy-start(bf16[4,280,768]{2,1,0:T(8,128)(2,1)} %get-tuple-element.53) | copy-start | bytes 5160964
  154.6 3.4 %copy-start.5 = (bf16[4,280,3072]{2,1,0:T(8,128)(2,1)S(1)}, bf16[4,280,3072]{2,1,0:T(8,128)(2,1)}, u32[]{:S(2)}) copy-start(bf16[4,280,3072]{2,1,0:T(8,128)(2,1)} %get-tuple-element.52) | copy-start | bytes 20643844
  154.6 3.8 %copy-start.7 = (bf16[4,280,768]{2,1,0:T(8,128)(2,1)S(1)}, bf16[4,280,768]{2,1,0:T(8,128)(2,1)}, u32[]{:S(2)}) copy-start(bf16[4,280,768]{2,1,0:T(8,128)(2,1)} %get-tuple-element.51) | copy-start | bytes 5160964
  303.5 4.7 %copy-start.1 = (bf16[4,280,768]{2,1,0:T(8,128)(2,1)S(1)}, bf16[4,280,768]{2,1,0:T(8,128)(2,1)}, u32[]{:S(2)}) copy-start(bf16[4,280,768]{2,1,0:T(8,128)(2,1)} %get-tuple-element.44) | copy-start | bytes 5160964
  308.2 2.2 copy-start.4
  308.2 2.8 copy-start.3
  308.2 3.5 %copy-start.2 = (f32[48,1536]{1,0:T(8,128)S(1)}, f32[48,1536]{1,0:T(8,128)}, u32[]{:S(2)}) copy-start(f32[48,1536]{1,0:T(8,128)} %get-tuple-element.63) | copy-start | bytes 884740

commit v5 on v4

--- a/solution.py
+++ b/solution.py
@@ -431,6 +431,8 @@
         own_z(1)
         loop(3, event_z, None)
         loop(4, event_one, None)
+        own_near(0)
+        loop(3, event_z, 0)
         loop(8, event_two, None)
         for copy in mine + [x_copy, bias_copy]:
             copy.wait()
@@ -443,29 +445,28 @@
         step = p * per_pair + hp
 
         def event(e, carry):
-            g = e // 16
-            i = lax.rem(e, 16)
-
-            @pl.when(i == 0)
+            @pl.when(e == 0)
             def _():
-                own_near(g)
-
-            @pl.when((i >= 1) & (i < 4))
+                own_near(1)
+
+            @pl.when(((e >= 1) & (e < 5)) | ((e >= 16) & (e < 20)))
             def _():
-                event_z(g, i - 1)
-
-            @pl.when((i >= 4) & (i < 8))
+                g = e // 16
+                event_one(g, e - 1 - 15 * g)
+
+            @pl.when((e >= 5) & (e < 8))
             def _():
-                event_one(g, i - 4)
-
-            @pl.when(i >= 8)
+                event_z(1, e - 5)
+
+            @pl.when(((e >= 8) & (e < 16)) | (e >= 20))
             def _():
-                event_two(g, i - 8)
+                g = e // 20
+                event_two(g, e - 8 - 12 * g)
 
             return carry
 
         total = pairs * per_pair
-        lax.fori_loop(step * 32 // total, (step + 1) * 32 // total, event, 0)
+        lax.fori_loop(step * 28 // total, (step + 1) * 28 // total, event, 0)
 
     attn_body(p, lens[p], xbuf[p], w_one, bias, vec_ref, qkv_ref, att_ref, prob_ref, hid_ref, n1_ref, n2_ref, hook)
 
@@ -525,318 +526,495 @@
 BLOCKS = 31
 
 
-def back_kernel(tok_all, dhid_ref, qkv_ref, prob_ref, n1_ref, w_ref, vec_ref, g_up, g_down, g_proj, sums_two, bsum_up,
-                tok_ref, tok_other, r_up, r_down, r_proj, r_qkv, small_out,
-                do_ref, xbuf, tokbuf, n1t, dq_all, gq, sums, bsum,
-                own_up, own_down, own_proj, rc0, rs0, rz0, rx0, rc1, rs1, rz1, rx1, rc2, rs2, rz2, rx2,
-                rc3, rs3, rz3, rx3, sbuf, send, recv, local, tsem, ssem):
-    p = pl.program_id(0)
-    pairs, rows, width = xbuf.shape
-    groups = w_ref.shape[0]
+def back_kernel(lens, cot, hid_in, n2_in, att_in, n1_all, qkv_all, prob_all, tok_all, w_one_in, w_two, bias_ref, vec_ref,
+                block_out, tok_out, r_ff, r_proj, r_qkv, small_out,
+                g_ff, g_proj, g_qkv, rc_ff, rs_ff, rz_ff, rx_ff, rc_p, rs_p, rz_p, rx_p, rc_q, rs_q, rz_q, rx_q,
+                dhid_ref, outbuf, sums, bsum, bsum_up, sbuf, send, recv, local, osem, tsem, ssem):
+    flat, width = outbuf.shape
+    pairs, rows = qkv_all.shape[0], qkv_all.shape[1]
+    groups = w_two.shape[0]
+    fw = w_two.shape[2] // 2
+    fc = fw // 3
     lw = width // groups
     tiles = lw // 128
+    half = flat // 2
+    part = r_proj.shape[1]
     z, y, c, m = place()
-    outs = (r_up, r_down, r_proj, r_qkv)
-    grads = (g_up, g_down, g_proj, gq)
-    owns = (own_up, own_down, own_proj)
-    rcs, rss, rzs, rxs = (rc0, rc1, rc2, rc3), (rs0, rs1, rs2, rs3), (rz0, rz1, rz2, rz3), (rx0, rx1, rx2, rx3)
-    part = r_up.shape[0]
     me = index(z, y, c)
     sib = (index(z, y, 1 - c), m)
 
     def beside(k):
         return (index(lax.rem(z + k, Z), y, c), m)
 
-    def x_first(g, cc):
-        return cc if g == 0 else 0
-
-    def target(g, cc, ra, rb):
-        fx = x_first(g, cc)
-        dy = fx * rb + (1 - fx) * ra
-        dm = fx * ra + (1 - fx) * rb
-        return y + dy * (1 - 2 * y), m + dm * (1 - 2 * m)
-
-    def chip(g, ra, rb):
-        yy, mm = target(g, c, ra, rb)
-        return (index(z, yy, c), mm)
-
-    def column(g, mm):
-        cols = outs[g].shape[1]
-        return pl.ds(pl.multiple_of(mm * cols, 128), cols)
-
-    def copy_of(g, src, dst, out_sem, in_sem, to):
-        return pltpu.make_async_remote_copy(
-            src_ref=src, dst_ref=dst, send_sem=send.at[g, out_sem], recv_sem=recv.at[g, in_sem],
-            device_id={"dp": to[0], "mp": to[1]}, device_id_type=MESH_ID,
-        )
-
-    def to_sibling(g):
+    def loop(n, event):
         def one(i, carry):
-            slot = 15 - i
-            ra, rb, k = slot // 8, lax.rem(slot // 4, 2), lax.rem(slot, 4)
-            yy, mm = target(g, 1 - c, ra, rb)
-            src = grads[g].at[lax.rem(z + k, Z) * Y + yy, 1 - c, :, column(g, mm)]
-            copy_of(g, src, rcs[g].at[slot], slot, slot, sib).start()
+            event(i)
             return carry
 
-        lax.fori_loop(0, 16, one, 0)
-
-    def arrived(g, ref, sem):
-        copy_of(g, ref, ref, 0, sem, sib).wait_recv()
-
-    def base(g, ra, rb, k):
-        slot = (ra * 2 + rb) * 4 + k
-        arrived(g, rcs[g].at[slot], slot)
-        yy, mm = target(g, c, ra, rb)
-        row = lax.rem(z + k, Z) * Y + yy
-        mine = owns[g][row, :, column(g, mm)] if g < 3 else gq[row, c, :, column(g, mm)]
-        return mine.astype(F32) + rcs[g][slot].astype(F32)
-
-    def level(g, rb, k):
-        value = base(g, 0, rb, k)
-        at = rb * 4 + k
-        arrived(g, rss[g].at[at], 16 + at)
-        return value + rss[g][at].astype(F32)
-
-    def lined(g, rb):
-        value = level(g, rb, 0)
-        for k in (1, 2, 3):
+        lax.fori_loop(0, n, one, 0)
+
+    def family(grad, rc, rs, rz, rx, out, row0):
+        cols = rc.shape[2]
+
+        def copy_of(u, src, dst, out_sem, in_sem, to):
+            return pltpu.make_async_remote_copy(
+                src_ref=src, dst_ref=dst, send_sem=send.at[row0 + u, out_sem], recv_sem=recv.at[row0 + u, in_sem],
+                device_id={"dp": to[0], "mp": to[1]}, device_id_type=MESH_ID,
+            )
+
+        def block(u, ra, rb, k, cc):
+            yy = y + ra * (1 - 2 * y)
+            mm = m + rb * (1 - 2 * m)
+            return u, lax.rem(z + k, Z) * Y + yy, cc, slice(None), pl.ds(pl.multiple_of(mm * cols, 128), cols)
+
+        def to_sibling(u, rb):
+            def one(i):
+                ra, k = 1 - i // 4, lax.rem(i + 1, 4)
+                slot = (ra * 2 + rb) * 4 + k
+                copy_of(u, grad.at[block(u, ra, rb, k, 1 - c)], rc.at[u * 16 + slot], slot, slot, sib).start()
+
+            loop(8, one)
+
+        def arrived(u, ref, sem):
+            copy_of(u, ref, ref, 0, sem, sib).wait_recv()
+
+        def base(u, ra, rb, k):
+            slot = (ra * 2 + rb) * 4 + k
+            arrived(u, rc.at[u * 16 + slot], slot)
+            return grad[block(u, ra, rb, k, c)].astype(F32) + rc[u * 16 + slot].astype(F32)
+
+        def level(u, rb, k):
+            at = rb * 4 + k
+            value = base(u, 0, rb, k)
+            arrived(u, rs.at[u * 8 + at], 16 + at)
+            return value + rs[u * 8 + at].astype(F32)
+
+        def lined(u, rb):
+            value = level(u, rb, 0)
+            for k in (1, 2, 3):
+                at = (k - 1) * 2 + rb
+                arrived(u, rz.at[u * 6 + at], 24 + at)
+                value = value + rz[u * 6 + at].astype(F32)
+            return value
+
+        def event_y(u, rb, i):
+            k = lax.rem(i + 1, 4)
+            slot = u * 16 + (2 + rb) * 4 + k
+            at = rb * 4 + k
+            rc[slot] = base(u, 1, rb, k).astype(LOW)
+            copy_of(u, rc.at[slot], rs.at[u * 8 + at], 16 + at, 16 + at, (index(z, 1 - y, c), m)).start()
+
+        def event_z(u, rb, i):
+            k = 1 + i
+            slot = u * 16 + rb * 4 + k
             at = (k - 1) * 2 + rb
-            arrived(g, rzs[g].at[at], 24 + at)
-            value = value + rzs[g][at].astype(F32)
-        return value
-
-    def event_s(g, r):
-        rb, k = 1 - r // 4, lax.rem(r + 1, 4)
-        slot = (2 + rb) * 4 + k
-        at = rb * 4 + k
-        rcs[g][slot] = base(g, 1, rb, k).astype(LOW)
-        copy_of(g, rcs[g].at[slot], rss[g].at[at], 16 + at, 16 + at, chip(g, 1, 0)).start()
-
-    def event_z(g, r):
-        rb, k = 1 - lax.rem(r, 2), 1 + r // 2
-        slot = rb * 4 + k
-        at = (k - 1) * 2 + rb
-        rcs[g][slot] = level(g, rb, k).astype(LOW)
-        copy_of(g, rcs[g].at[slot], rzs[g].at[at], 24 + at, 24 + at, beside(k)).start()
-
-    def event_x(g):
-        rcs[g][4] = lined(g, 1).astype(LOW)
-        copy_of(g, rcs[g].at[4], rxs[g].at[0], 30, 30, chip(g, 0, 1)).start()
-
-    def final(g):
-        value = lined(g, 0)
-        arrived(g, rxs[g].at[0], 30)
-        outs[g][...] = value + rxs[g][0].astype(F32)
-
-        def one(i, carry):
-            copy_of(g, rcs[g].at[0], rcs[g].at[0], i, 0, sib).wait_send()
-            return carry
-
-        lax.fori_loop(0, BLOCKS, one, 0)
-
-    def tok_copy(i):
-        return pltpu.make_async_remote_copy(
-            src_ref=tokbuf.at[i], dst_ref=tok_other.at[i], send_sem=tsem.at[0, i], recv_sem=tsem.at[1, i],
+            rc[slot] = level(u, rb, k).astype(LOW)
+            copy_of(u, rc.at[slot], rz.at[u * 6 + at], 24 + at, 24 + at, beside(k)).start()
+
+        def event_x(u):
+            rc[u * 16 + 4] = lined(u, 1).astype(LOW)
+            copy_of(u, rc.at[u * 16 + 4], rx.at[u], 30, 30, (me, 1 - m)).start()
+
+        def final(u):
+            value = lined(u, 0)
+            arrived(u, rx.at[u], 30)
+            out[u] = value + rx[u].astype(F32)
+
+            def one(i):
+                copy_of(u, rc.at[0], rc.at[0], i, 0, sib).wait_send()
+
+            loop(BLOCKS, one)
+
+        return to_sibling, event_y, event_z, event_x, final
+
+    ff_sib, ff_y, ff_z, ff_x, ff_final = family(g_ff, rc_ff, rs_ff, rz_ff, rx_ff, r_ff, 0)
+    p_sib, p_y, p_z, p_x, p_final = family(g_proj, rc_p, rs_p, rz_p, rx_p, r_proj, 2)
+    q_sib, q_y, q_z, q_x, q_final = family(g_qkv, rc_q, rs_q, rz_q, rx_q, r_qkv, 3)
+
+    def out_copies(r):
+        src = outbuf.at[pl.ds(pl.multiple_of(r * half, 16), half)]
+        dst = block_out.at[pl.ds(pl.multiple_of(m * flat + r * half, 16), half)]
+        return pltpu.make_async_copy(src, dst, osem.at[0, r]), pltpu.make_async_remote_copy(
+            src_ref=src, dst_ref=dst, send_sem=osem.at[1, r], recv_sem=osem.at[2, r],
             device_id={"dp": me, "mp": 1 - m}, device_id_type=MESH_ID,
         )
 
-    def own_copy(g):
-        return pltpu.make_async_copy(grads[g].at[:, c], owns[g], local.at[g])
-
-    x_copy = pltpu.make_async_copy(tok_all.at[pl.ds(m * pairs, pairs)], xbuf, local.at[3])
-
-    @pl.when(p == 0)
-    def _():
-        for g in range(3):
-            own_copy(g).start()
-        x_copy.start()
+    def keep_of(r):
+        ids = row_ids(half)
+        return ids < jnp.where(ids < rows, lens[2 * r], lens[2 * r + 1] + rows)
+
+    def span(r):
+        return pl.ds(pl.multiple_of(r * half, 16), half)
+
+    sums[...] = jnp.zeros_like(sums)
+    bsum[...] = jnp.zeros_like(bsum)
+    bsum_up[...] = jnp.zeros_like(bsum_up)
+
+    def feed_forward(n2, n2t, upl, uplt, hid, acc, slope, chunk, wbuf):
+        def place_of(f):
+            i = lax.rem(f, 6)
+            return lax.rem(m + 1 + i // 3, 2), lax.rem(i, 3) * fc
+
+        def weights(f):
+            mm, at = place_of(f)
+            slot = lax.rem(f, 2)
+            return [
+                pltpu.make_async_copy(
+                    w_two.at[mm, :, pl.ds(pl.multiple_of(t * fw + at, 128), fc)], wbuf.at[slot, t], local.at[slot * 2 + t])
+                for t in range(2)
+            ]
+
+        n2_copy = pltpu.make_async_copy(n2_in, n2, local.at[4])
+        up_copy = pltpu.make_async_copy(cot.at[pl.ds(pl.multiple_of(m * flat, 16), flat)], upl, local.at[5])
+        hid_copy = pltpu.make_async_copy(hid_in, hid, local.at[6])
+        att_copy = pltpu.make_async_copy(att_in, slope.at[:, pl.ds(0, width)], local.at[7])
+        n2_copy.start()
+        up_copy.start()
+        for copy in weights(0):
+            copy.start()
+        hid_copy.start()
         greet(z, y, c, m)
-        for g in range(3):
-            to_sibling(g)
-        sums[...] = jnp.zeros_like(sums)
-        bsum[...] = jnp.zeros_like(bsum)
-        for g in range(3):
-            own_copy(g).wait()
-        x_copy.wait()
-
-    dhid = dhid_ref[0]
-    dlow = dhid.astype(LOW)
-    for mm in range(groups):
-        do_ref[:, mm * lw : (mm + 1) * lw] = dot(dlow, w_ref[mm, :, 3 * lw : 4 * lw]).astype(LOW)
-    n1t[p] = n1_ref[0].T
-    first = lax.broadcasted_iota(jnp.int32, (1, 128), 1) < HEAD_DIM
-
-    def pair(hp, carry):
-        lane = (hp // tiles) * 3 * lw + lax.rem(hp, tiles) * 128
-
-        def cols(t):
-            return pl.ds(pl.multiple_of(lane + t * lw, 128), 128)
-
-        q2 = qkv_ref[0, :, cols(0)] * 0.125
-        k2t = qkv_ref[0, :, cols(1)].T
-        v2 = qkv_ref[0, :, cols(2)]
-        do2 = do_ref[:, pl.ds(pl.multiple_of(hp * 128, 128), 128)]
-        dq_t = []
-        dk = dv = 0.0
-        for h in range(2):
-            mine = first if h == 0 else ~first
-            doh = jnp.where(mine, do2, 0)
-            qh = jnp.where(mine, q2, 0)
-            dpt = dot(v2, doh, NT)
-            plow = prob_ref[0, hp * 2 + h]
-            pt = plow.astype(F32)
-            inner = jnp.sum(pt * dpt, axis=0, keepdims=True)
-            dst = (pt * (dpt - inner)).astype(LOW)
-            dv = dv + dot(plow, doh)
-            dk = dk + dot(dst, qh)
-            dq_t.append(dot(k2t[h * HEAD_DIM : (h + 1) * HEAD_DIM], dst))
-        dq = (jnp.concatenate(dq_t, axis=0) * 0.125).T
-        dq_all[p, :, cols(0)] = dq.astype(LOW)
-        dq_all[p, :, cols(1)] = dk.astype(LOW)
-        dq_all[p, :, cols(2)] = dv.astype(LOW)
-        bsum[0:1, cols(0)] += jnp.sum(dq, axis=0, keepdims=True)
-        bsum[0:1, cols(2)] += jnp.sum(dv, axis=0, keepdims=True)
-
-        step = p * (groups * tiles) + hp
-        for g in range(3):
-
-            @pl.when((step >= 4 * g) & (step < 4 * g + 4))
+        up_copy.wait()
+
+        def prepare(r):
+            value = jnp.where(keep_of(r), upl[span(r)], 0)
+            upl[span(r)] = value
+            sums[3:4] += jnp.sum(value.astype(F32), axis=0, keepdims=True)
+            acc[span(r)] = jnp.zeros((half, width), F32)
+
+        loop(2, prepare)
+        uplt[...] = upl[...].T
+        n2_copy.wait()
+        n2t[...] = n2[...].T
+
+        def traffic(f):
+            @pl.when(lax.rem(f, 3) == 2)
             def _():
-                event_s(g, 2 * step - 8 * g)
-                event_s(g, 2 * step - 8 * g + 1)
-
-        @pl.when((step >= 17) & (step < 23))
-        def _():
-            event_z(0, step - 17)
-
-        return carry
-
-    lax.fori_loop(0, groups * tiles, pair, 0)
-    done = sum(dot(dq_all[p, :, mm * 3 * lw : (mm + 1) * 3 * lw], w_ref[mm, :, : 3 * lw], NT) for mm in range(groups))
-    xhat, r = moments(xbuf[p].astype(F32))
-    dg = done * vec_ref[0:1]
-    dn = r * (dg - jnp.mean(dg, axis=-1, keepdims=True) - xhat * jnp.mean(dg * xhat, axis=-1, keepdims=True))
-    tok = (dhid + dn).astype(LOW)
-    tok_ref[0] = tok
-    tokbuf[p] = tok
-    tok_copy(p).start()
-    sums[0:1] += jnp.sum(done * xhat, axis=0, keepdims=True)
-    sums[1:2] += jnp.sum(done, axis=0, keepdims=True)
-
-    def small_copy(slot, src, to, sem):
-        return pltpu.make_async_remote_copy(
-            src_ref=sbuf.at[src], dst_ref=sbuf.at[slot], send_sem=ssem.at[0, sem], recv_sem=ssem.at[1, sem],
-            device_id={"dp": to[0], "mp": to[1]}, device_id_type=MESH_ID,
-        )
-
-    @pl.when(p == pairs - 1)
-    def _():
+                n = f // 3
+                ff_sib(n // 2, 1 - lax.rem(n, 2))
+
+            @pl.when((lax.rem(f, 3) == 0) & (f > 0))
+            def _():
+                n = f // 3 - 1
+                loop(4, lambda i: ff_y(n // 2, 1 - lax.rem(n, 2), i))
+
+            @pl.when((lax.rem(f, 3) == 1) & (f > 4))
+            def _():
+                n = (f - 7) // 3
+                loop(3, lambda i: ff_z(n // 2, 1 - lax.rem(n, 2), i))
+
+        def store(u, at, value):
+            g_ff[u, :, :, :, at] = value.astype(LOW).reshape(Z * Y, C, part, fc)
+
+        def forward(f):
+            slot = lax.rem(f, 2)
+            for copy in weights(f + 1):
+                copy.start()
+            for copy in weights(f):
+                copy.wait()
+            mm, off = place_of(f)
+            at = pl.ds(pl.multiple_of(mm * fw + off, 128), fc)
+            shift = bias_ref[mm, 0:1, pl.ds(pl.multiple_of(2 * lw + off, 128), fc)]
+
+            def block(r):
+                pre = dot(n2[span(r)], wbuf[slot, 0]) + shift
+                cdf = 0.5 * (1.0 + lax.erf(pre * (2.0 ** -0.5)))
+                chunk[span(r)] = (pre * cdf).astype(LOW)
+                slope[span(r), at] = (cdf + pre * (0.3989422804014327 * jnp.exp(-0.5 * pre * pre))).astype(LOW)
+                acc[span(r)] += dot(chunk[span(r)], wbuf[slot, 1], NT)
+
+            loop(2, block)
+            store(0, at, dot(uplt[...], chunk[...]))
+            traffic(f)
+
+        loop(6, forward)
+        hid_copy.wait()
+
+        def leave(r):
+            outbuf[span(r)] = jnp.where(keep_of(r), hid[span(r)] + acc[span(r)] + vec_ref[5:6], 0.0).astype(LOW)
+            acc[span(r)] = jnp.zeros((half, width), F32)
+            for copy in out_copies(r):
+                copy.start()
+
+        loop(2, leave)
+
+        def backward(i):
+            f = 6 + i
+            slot = lax.rem(f, 2)
+
+            @pl.when(f < 11)
+            def _():
+                for copy in weights(f + 1):
+                    copy.start()
+
+            for copy in weights(f):
+                copy.wait()
+            mm, off = place_of(f)
+            at = pl.ds(pl.multiple_of(mm * fw + off, 128), fc)
+
+            def block(r):
+                dpre = slope[span(r), at].astype(F32) * dot(upl[span(r)], wbuf[slot, 1])
+                chunk[span(r)] = dpre.astype(LOW)
+                bsum_up[0:1, at] += jnp.sum(dpre, axis=0, keepdims=True)
+                acc[span(r)] += dot(chunk[span(r)], wbuf[slot, 0], NT)
+
+            loop(2, block)
+            store(1, at, dot(n2t[...], chunk[...]))
+            traffic(f)
+
+        loop(6, backward)
+        att_copy.start()
+
+        def norm_back(r):
+            dtwo = acc[span(r)]
+            xhat, rr = moments(hid[span(r)])
+            dg = dtwo * vec_ref[3:4]
+            dn = rr * (dg - jnp.mean(dg, axis=-1, keepdims=True) - xhat * jnp.mean(dg * xhat, axis=-1, keepdims=True))
+            dhid = upl[span(r)].astype(F32) + dn
+            dhid_ref[span(r)] = dhid
+            n2[span(r)] = dhid.astype(LOW)
+            sums[4:5] += jnp.sum(dtwo * xhat, axis=0, keepdims=True)
+            sums[5:6] += jnp.sum(dtwo, axis=0, keepdims=True)
+            sums[2:3] += jnp.sum(dhid, axis=0, keepdims=True)
+
+        loop(2, norm_back)
+        att_copy.wait()
+        n2t[...] = n2[...].T
+        for mm in range(groups):
+            at = slice(mm * lw, (mm + 1) * lw)
+            g_proj[0, :, :, :, at] = dot(n2t[...], slope[:, at]).astype(LOW).reshape(Z * Y, C, part, lw)
+        p_sib(0, 1)
+        p_sib(0, 0)
+
+    pl.run_scoped(
+        feed_forward,
+        pltpu.VMEM((flat, width), LOW), pltpu.VMEM((width, flat), LOW),
+        pltpu.VMEM((flat, width), LOW), pltpu.VMEM((width, flat), LOW),
+        pltpu.VMEM((flat, width), F32), pltpu.VMEM((flat, width), F32),
+        pltpu.VMEM((flat, groups * fw), LOW), pltpu.VMEM((flat, fc), LOW), pltpu.VMEM((2, 2, width, fc), LOW),
+    )
+
+    def attention(w_ref, qkv_buf, prob_buf, n1_buf, x_buf, do_ref, n1t, dq_all, tokbuf):
+        w_copy = pltpu.make_async_copy(w_one_in, w_ref, local.at[8])
+
+        def loads(p):
+            slot = lax.rem(p, 2)
+            pieces = [
+                (qkv_all.at[p], qkv_buf), (prob_all.at[p], prob_buf), (n1_all.at[p], n1_buf),
+                (tok_all.at[m * pairs + p], x_buf),
+            ]
+            return [
+                pltpu.make_async_copy(src, dst.at[slot], local.at[slot * 4 + t])
+                for t, (src, dst) in enumerate(pieces)
+            ]
+
+        def tok_copies(p):
+            src, dst = tokbuf.at[p], tok_out.at[m * pairs + p]
+            return pltpu.make_async_copy(src, dst, tsem.at[0, p]), pltpu.make_async_remote_copy(
+                src_ref=src, dst_ref=dst, send_sem=tsem.at[1, p], recv_sem=tsem.at[2, p],
+                device_id={"dp": me, "mp": 1 - m}, device_id_type=MESH_ID,
+            )
+
+        w_copy.start()
+        for copy in loads(0):
+            copy.start()
+        w_copy.wait()
+        first = lax.broadcasted_iota(jnp.int32, (1, 128), 1) < HEAD_DIM
+
+        def one_pair(p):
+            slot = lax.rem(p, 2)
+
+            @pl.when(p < pairs - 1)
+            def _():
+                for copy in loads(p + 1):
+                    copy.start()
+
+            dhid = dhid_ref[pl.ds(pl.multiple_of(p * rows, 8), rows)]
+            dlow = dhid.astype(LOW)
+            for mm in range(groups):
+                do_ref[:, mm * lw : (mm + 1) * lw] = dot(dlow, w_ref[mm, :, 3 * lw : 4 * lw]).astype(LOW)
+            for copy in loads(p):
+                copy.wait()
+            n1t[p] = n1_buf[slot].T
+
+            def heads(hp):
+                lane = (hp // tiles) * 3 * lw + lax.rem(hp, tiles) * 128
+
+                def cols(t):
+                    return pl.ds(pl.multiple_of(lane + t * lw, 128), 128)
+
+                q2 = qkv_buf[slot, :, cols(0)] * 0.125
+                k2t = qkv_buf[slot, :, cols(1)].T
+                v2 = qkv_buf[slot, :, cols(2)]
+                do2 = do_ref[:, pl.ds(pl.multiple_of(hp * 128, 128), 128)]
+                dq_t = []
+                dk = dv = 0.0
+                for h in range(2):
+                    mine = first if h == 0 else ~first
+                    doh = jnp.where(mine, do2, 0)
+                    qh = jnp.where(mine, q2, 0)
+                    dpt = dot(v2, doh, NT)
+                    plow = prob_buf[slot, hp * 2 + h]
+                    pt = plow.astype(F32)
+                    inner = jnp.sum(pt * dpt, axis=0, keepdims=True)
+                    dst = (pt * (dpt - inner)).astype(LOW)
+                    dv = dv + dot(plow, doh)
+                    dk = dk + dot(dst, qh)
+                    dq_t.append(dot(k2t[h * HEAD_DIM : (h + 1) * HEAD_DIM], dst))
+                dq = (jnp.concatenate(dq_t, axis=0) * 0.125).T
+                dq_all[p, :, cols(0)] = dq.astype(LOW)
+                dq_all[p, :, cols(1)] = dk.astype(LOW)
+                dq_all[p, :, cols(2)] = dv.astype(LOW)
+                bsum[0:1, cols(0)] += jnp.sum(dq, axis=0, keepdims=True)
+                bsum[0:1, cols(2)] += jnp.sum(dv, axis=0, keepdims=True)
+                step = p * (groups * tiles) + hp
+
+                @pl.when(step == 0)
+                def _():
+                    loop(4, lambda i: ff_y(1, 0, i))
+
+                @pl.when((step == 2) | (step == 11))
+                def _():
+                    loop(3, lambda i: ff_z(1, 1 - step // 11, i))
+
+                @pl.when((step >= 3) & (step < 7))
+                def _():
+                    loop(2, lambda i: p_y(0, 1 - (step - 3) // 2, 2 * lax.rem(step - 3, 2) + i))
+
+                @pl.when((step == 13) | (step == 14))
+                def _():
+                    loop(3, lambda i: p_z(0, 14 - step, i))
+
+                @pl.when((step == 16) | (step == 18))
+                def _():
+                    ff_x((step - 16) // 2)
+
+                @pl.when(step == 20)
+                def _():
+                    p_x(0)
+
+            loop(groups * tiles, heads)
+            done = sum(
+                dot(dq_all[p, :, mm * 3 * lw : (mm + 1) * 3 * lw], w_ref[mm, :, : 3 * lw], NT) for mm in range(groups))
+            xhat, r = moments(x_buf[slot].astype(F32))
+            dg = done * vec_ref[0:1]
+            dn = r * (dg - jnp.mean(dg, axis=-1, keepdims=True) - xhat * jnp.mean(dg * xhat, axis=-1, keepdims=True))
+            tokbuf[p] = (dhid + dn).astype(LOW)
+            for copy in tok_copies(p):
+                copy.start()
+            sums[0:1] += jnp.sum(done * xhat, axis=0, keepdims=True)
+            sums[1:2] += jnp.sum(done, axis=0, keepdims=True)
+
+        loop(pairs, one_pair)
+
+        def small_copy(slot, src, to, sem):
+            return pltpu.make_async_remote_copy(
+                src_ref=sbuf.at[src], dst_ref=sbuf.at[slot], send_sem=ssem.at[0, sem], recv_sem=ssem.at[1, sem],
+                device_id={"dp": to[0], "mp": to[1]}, device_id_type=MESH_ID,
+            )
+
         sbuf[6] = jnp.zeros_like(sbuf[6])
         sbuf[6, 0:1] = bsum_up[0:1]
         sbuf[6, 1:2, : 3 * width] = bsum[0:1]
-        sbuf[6, 2:3, :width] = sums[0:1]
-        sbuf[6, 2:3, width : 2 * width] = sums[1:2]
-        sbuf[6, 2:3, 2 * width : 3 * width] = sums_two[2:3]
-        sbuf[6, 2:3, 3 * width :] = sums_two[0:1]
-        sbuf[6, 3:4, :width] = sums_two[1:2]
-        sbuf[6, 3:4, width : 2 * width] = sums_two[3:4]
+        for n, (line, at) in enumerate(((2, 0), (2, 1), (2, 2), (3, 1), (2, 3), (3, 0))):
+            sbuf[6, line : line + 1, at * width : (at + 1) * width] = sums[n : n + 1]
         s0 = small_copy(0, 6, sib, 0)
         s0.start()
 
-        def chunk(i, carry):
-            at = pl.ds(pl.multiple_of(i * lw, 128), lw)
+        def chunk(i):
+            mm = lax.rem(m + 1 + i // 3, 2)
+            at = pl.ds(pl.multiple_of(mm * 3 * lw + lax.rem(i, 3) * lw, 128), lw)
             acc = dot(n1t[0], dq_all[0, :, at])
             for q in range(1, pairs):
                 acc = acc + dot(n1t[q], dq_all[q, :, at])
-            gq[:, :, :, at] = acc.astype(LOW).reshape(Z * Y, C, part, lw)
-            event_z(1, i)
-            return carry
-
-        lax.fori_loop(0, 3 * groups, chunk, 0)
-        to_sibling(3)
+            g_qkv[0, :, :, :, at] = acc.astype(LOW).reshape(Z * Y, C, part, lw)
+
+            @pl.when(lax.rem(i, 3) == 2)
+            def _():
+                q_sib(0, 1 - i // 3)
+
+            @pl.when(i == 4)
+            def _():
+                loop(4, lambda k: q_y(0, 1, k))
+
+        loop(6, chunk)
         s0.wait()
         sbuf[7] = sbuf[6] + sbuf[0]
-        s1 = small_copy(1, 7, chip(1, 1, 0), 1)
+        s1 = small_copy(1, 7, (index(z, 1 - y, c), m), 1)
         s1.start()
-
-        def loop(n, event, g):
-            def one(i, carry):
-                event(g, i)
-                return carry
-
-            lax.fori_loop(0, n, one, 0)
-
-        loop(8, event_s, 3)
+        loop(4, lambda i: q_y(0, 0, i))
         s1.wait()
         sbuf[8] = sbuf[7] + sbuf[1]
-        s2 = small_copy(2, 8, chip(1, 0, 1), 2)
+        s2 = small_copy(2, 8, (me, 1 - m), 2)
         s2.start()
-        event_x(0)
-        loop(6, event_z, 2)
+        ff_final(0)
+        loop(3, lambda i: q_z(0, 1, i))
         s2.wait()
         sbuf[9] = sbuf[8] + sbuf[2]
         zs = [small_copy(2 + k, 9, beside(k), 2 + k) for k in (1, 2, 3)]
         for copy in zs:
             copy.start()
-        event_x(1)
-        loop(6, event_z, 3)
-        final(0)
-        event_x(2)
+        ff_final(1)
+        loop(3, lambda i: q_z(0, 0, i))
+        p_final(0)
         for copy in zs:
             copy.wait()
         small_out[...] = (sbuf[9] + sbuf[3] + sbuf[4] + sbuf[5])[:4]
-        final(1)
-        event_x(3)
-        final(2)
-        final(3)
-
-        def finish(i, carry):
-            tok_copy(i).wait()
-            return carry
-
-        lax.fori_loop(0, pairs, finish, 0)
-
-
-def backward_reduce(tokens, dhid, qkv, prob, n1, w_one, vec, grads, sums_two, bsum_up):
-    pairs, rows, width = dhid.shape
-    total = Z * Y * C
-    part = grads[0].shape[0] // total
-    grads = [g.reshape(Z * Y, C, part, g.shape[1]) for g in grads]
-    widths = [g.shape[3] // 2 for g in grads] + [3 * width // 2]
+        q_x(0)
+        q_final(0)
+
+        def finish(p):
+            for copy in tok_copies(p):
+                copy.wait()
+
+        loop(pairs, finish)
+
+        def finish_out(r):
+            for copy in out_copies(r):
+                copy.wait()
+
+        loop(2, finish_out)
+
+    pl.run_scoped(
+        attention,
+        pltpu.VMEM(w_one_in.shape, LOW), pltpu.VMEM((2, rows, 3 * width), LOW), pltpu.VMEM((2, HEADS, rows, rows), LOW),
+        pltpu.VMEM((2, rows, width), LOW), pltpu.VMEM((2, rows, width), LOW), pltpu.VMEM((rows, width), LOW),
+        pltpu.VMEM((pairs, width, rows), LOW), pltpu.VMEM((pairs, rows, 3 * width), LOW),
+        pltpu.VMEM((pairs, rows, width), LOW),
+    )
+
+
+def backward_reduce(lens, tokens, cotangent, hid, n2, att, n1, qkv, prob, w_one, w_two, bias, vec):
+    pairs, rows, width = n1.shape
+    flat = pairs * rows
+    part = width // (Z * Y * C)
+    fw = w_two.shape[2] // 2
     hbm = pl.BlockSpec(memory_space=pl.ANY)
-    scratch = [
-        pltpu.VMEM((rows, width), LOW), pltpu.VMEM((pairs, rows, width), LOW), pltpu.VMEM((pairs, rows, width), LOW),
-        pltpu.VMEM((pairs, width, rows), LOW), pltpu.VMEM((pairs, rows, 3 * width), LOW),
-        pltpu.VMEM((Z * Y, C, part, 3 * width), LOW), pltpu.VMEM((8, width), F32), pltpu.VMEM((8, 3 * width), F32),
+    vm = pl.BlockSpec(memory_space=pltpu.VMEM)
+    kinds = ((2, fw), (1, width // 2), (1, 3 * width // 2))
+    scratch = [pltpu.VMEM((n, Z * Y, C, part, 2 * w), LOW) for n, w in kinds]
+    for n, w in kinds:
+        scratch += [pltpu.VMEM((n * k, part, w), LOW) for k in (16, 8, 6, 1)]
+    scratch += [
+        pltpu.VMEM((flat, width), F32), pltpu.VMEM((flat, width), LOW), pltpu.VMEM((8, width), F32),
+        pltpu.VMEM((8, 3 * width), F32), pltpu.VMEM((8, 2 * fw), F32), pltpu.VMEM((10, 8, 2 * fw), F32),
+        pltpu.SemaphoreType.DMA((4, BLOCKS)), pltpu.SemaphoreType.DMA((4, BLOCKS)), pltpu.SemaphoreType.DMA((9,)),
+        pltpu.SemaphoreType.DMA((3, 2)), pltpu.SemaphoreType.DMA((3, pairs)), pltpu.SemaphoreType.DMA((2, 6)),
     ]
-    scratch += [pltpu.VMEM((Z * Y, part, 2 * w), LOW) for w in widths[:3]]
-    for w in widths:
-        scratch += [pltpu.VMEM((n, part, w), LOW) for n in (16, 8, 6, 1)]
-    scratch += [
-        pltpu.VMEM((10, 8, bsum_up.shape[1]), F32),
-        pltpu.SemaphoreType.DMA((4, BLOCKS)), pltpu.SemaphoreType.DMA((4, BLOCKS)), pltpu.SemaphoreType.DMA((4,)),
-        pltpu.SemaphoreType.DMA((2, pairs)), pltpu.SemaphoreType.DMA((2, 6)),
-    ]
-    whole = lambda *s: pl.BlockSpec(s, lambda p: (0,) * len(s))
+    plane = lambda a: a.reshape(-1, width)
     return pl.pallas_call(
         back_kernel,
-        grid=(pairs,),
-        in_specs=[
-            hbm, pair_spec(rows, width), pair_spec(rows, 3 * width), pair_spec(HEADS, rows, rows),
-            pair_spec(rows, width), const_spec(w_one.shape), const_spec(vec.shape), hbm, hbm, hbm,
-            const_spec(sums_two.shape), const_spec(bsum_up.shape),
-        ],
-        out_specs=[pair_spec(rows, width), hbm] + [whole(part, w) for w in widths] + [whole(4, bsum_up.shape[1])],
+        in_specs=[pl.BlockSpec(memory_space=pltpu.SMEM)] + [hbm] * 10 + [vm] * 2,
+        out_specs=[hbm] * 2 + [vm] * 4,
         out_shape=[
-            jax.ShapeDtypeStruct((pairs, rows, width), LOW), jax.ShapeDtypeStruct((pairs, rows, width), LOW),
+            jax.ShapeDtypeStruct((2 * flat, width), LOW), jax.ShapeDtypeStruct((2 * pairs, rows, width), LOW),
         ]
-        + [jax.ShapeDtypeStruct((part, w), F32) for w in widths]
-        + [jax.ShapeDtypeStruct((4, bsum_up.shape[1]), F32)],
+        + [jax.ShapeDtypeStruct((n, part, w), F32) for n, w in kinds]
+        + [jax.ShapeDtypeStruct((4, 2 * fw), F32)],
         scratch_shapes=scratch,
-        compiler_params=pltpu.CompilerParams(collective_id=1, has_side_effects=True, vmem_limit_bytes=62 * 2**20),
+        compiler_params=pltpu.CompilerParams(collective_id=1, has_side_effects=True, vmem_limit_bytes=63 * 2**20),
         name="backward_reduce",
-    )(tokens, dhid, qkv, prob, n1, w_one, vec, *grads, sums_two, bsum_up)
+    )(lens, plane(cotangent), plane(hid), plane(n2), plane(att), n1, qkv, prob, tokens, w_one, w_two, bias, vec)
 
 
 def per_device(
@@ -846,8 +1024,8 @@
     pairs_all, rows, width = tokens.shape
     n_mp = lax.axis_size("mp")
     n_dp = lax.axis_size("dp")
-    direct = n_dp == Z * Y * C and n_mp == 2
     pairs = pairs_all // n_mp
+    direct = n_dp == Z * Y * C and n_mp == 2 and pairs == 4
     part = w_qkv.shape[0]
     lw = w_qkv.shape[2]
     fw = w_up.shape[1]
@@ -870,7 +1048,6 @@
         w_two = lax.all_gather(second, both_axes, axis=0, tiled=True).reshape(n_mp, width, -1)
         bias = lax.all_gather(bias, "mp", axis=0)
         qkv, att, prob, hid, n1, n2, vec = attention_forward(lens, off, tokens, w_one, bias)
-    out_here, act, dpre, dhid, dlow, upl, sums_two, bsum_up = ffn(lens, off, n2, hid, cotangent, w_two, bias, vec)
 
     def grad(left, right):
         return jnp.einsum(
@@ -887,32 +1064,31 @@
             )
             for g in grads
         ]
-        if small is not None:
-            done.append(lax.psum(small, axes))
-        return done
-
-    def both(array, other=None):
-        if other is None:
-            other = lax.ppermute(array, "mp", [(0, 1), (1, 0)])
+        return done + [lax.psum(small, axes)]
+
+    def both(array):
+        other = lax.ppermute(array, "mp", [(0, 1), (1, 0)])
         return jnp.where(mine == 0, jnp.concatenate([array, other]), jnp.concatenate([other, array]))
 
-    block_out = both(out_here)
-    grads = [grad(n2, dpre), grad(upl, act), grad(dlow, att)]
     if direct:
-        tok_here, tok_other, r_up, r_down, r_proj, r_qkv, small = backward_reduce(
-            tokens, dhid, qkv, prob, n1, w_one, vec, [g.astype(LOW) for g in grads], sums_two, bsum_up)
-        tokens_grad = both(tok_here, tok_other)
+        block_out, tokens_grad, r_ff, r_proj, r_qkv, small = backward_reduce(
+            lens, tokens, cotangent, hid, n2, att, n1, qkv, prob, w_one, w_two, bias, vec)
+        block_out = block_out.reshape(tokens.shape)
+        r_down, r_up, r_proj, r_qkv = r_ff[0], r_ff[1], r_proj[0], r_qkv[0]
         flat = small[1, : 3 * width].reshape(n_mp, 3, lw)
         small = jnp.concatenate([
             small[2], small[3, : 2 * width], flat[:, 0].reshape(-1), flat[:, 2].reshape(-1), small[0]])
     else:
+        out_here, act, dpre, dhid, dlow, upl, sums_two, bsum_up = ffn(lens, off, n2, hid, cotangent, w_two, bias, vec)
+        block_out = both(out_here)
         tok_here, dqkv, sums_one, bsum_qkv = attention_backward(lens, off, tokens, dhid, qkv, prob, w_one, vec)
         tokens_grad = both(tok_here)
         flat = bsum_qkv[0].reshape(n_mp, 3, lw)
         small = jnp.concatenate([
             sums_one[0], sums_one[1], sums_two[2], sums_two[0], sums_two[1], sums_two[3],
             flat[:, 0].reshape(-1), flat[:, 2].reshape(-1), bsum_up[0]])
-        r_up, r_down, r_proj, r_qkv, small = reduce(grads + [grad(n1, dqkv)], small)
+        r_up, r_down, r_proj, r_qkv, small = reduce(
+            [grad(n2, dpre), grad(upl, act), grad(dlow, att), grad(n1, dqkv)], small)
     place_dp = lax.axis_index("dp") * part
 
     def piece(i):

time: 313 us -> 271 us (0.87)
  matrix products: 21.8 us -> 0 us
  Pallas kernels: 260 us -> 241 us
  other arithmetic: 18.6 us -> 11.7 us
  local copies, waits for them, and re-layouts: 10.8 us -> 16.2 us
    dot_general x3 -> x0, matrix products: 21.8 us -> none  [grad(): jnp.einsum('rd,rf->df', left.reshape(pairs * rows, width), right.reshape(...]
    pallas_call x1, Pallas kernels: 94.1 us -> 80.3 us  [gather_attention(): pl.pallas_call(gather_attn_kernel, grid_spec=pltpu.PrefetchScalarGridSpec...]
    select_n x2 -> x0, other arithmetic: 6.88 us -> none  [both(): jnp.where(mine == 0, jnp.concatenate([array, other]), jnp.concatenate([ot...]
    pallas_call x2 -> x1, Pallas kernels: 166 us -> 161 us  [backward_reduce(): pl.pallas_call(back_kernel, in_specs=[pl.BlockSpec(memory_space=pltpu.SME...]
    unnamed x25 -> x12, local copies, waits for them, and re-layouts: 3.14 us -> 7.22 us
  transfers between devices with their start and end apart: 1 -> 0, of which waited for: 0 -> 0; matrix products, arithmetic and copies ran while one was open for 10% -> 0% of each run, Pallas kernels for 42% -> 0%
where the time goes in v5:
time: 271 us; the launch traced here: 270 us
  Pallas kernels  241 us (89%)
  local copies, waits for them, and re-layouts  16.2 us (6%)
  other arithmetic  11.7 us (4%)
    pallas_call x1, Pallas kernels, backward_reduce(): pl.pallas_call(back_kernel, in_specs=[pl.BlockSpec(memory_space=pltpu.SME...  161 us
    pallas_call x1, Pallas kernels, gather_attention(): pl.pallas_call(gather_attn_kernel, grid_spec=pltpu.PrefetchScalarGridSpec...  80.3 us
    unnamed x12, local copies, waits for them, and re-layouts  7.22 us

profile of v5, /device:TPU:8, one launch (start us, length us, event | category | flops | bytes accessed | tf_op | source)
XLA Modules:
  0.0 270.0 jit_solution(7385711698727505953)
XLA Ops:
  0.6 1.2 dynamic-slice_add_fusion.lens
  1.9 1.0 convert.56
  2.9 1.0 convert_bitcast_fusion
  3.9 0.7 pad_maximum_fusion.second_ref
  4.6 0.9 convert_bitcast_fusion.1
  5.6 0.9 convert_bitcast_fusion.2
  6.5 0.7 convert_bitcast_fusion.8
  7.1 0.1 copy.38
  7.2 0.7 convert_bitcast_fusion.7
  7.9 0.1 copy.39
  8.0 0.7 convert_bitcast_fusion.6
  8.7 0.1 copy.40
  8.8 0.7 convert_bitcast_fusion.5
  9.4 0.1 copy.41
  9.5 0.7 convert_bitcast_fusion.4
  10.2 0.1 copy.42
  10.3 0.7 convert_bitcast_fusion.3
  11.0 0.1 copy.43
  11.1 0.8 concatenate.18.first_ref
  11.9 0.7 convert.59
  12.6 0.7 convert.58
  13.3 0.6 broadcast_in_dim.7.b_in
  13.9 80.3 %gather_attention.1 = (bf16[2,768,1664]{2,1,0:T(8,128)(2,1)}, bf16[2,768,3072]{2,1,0:T(8,128)(2,1)}, f32[2,8,2304]{2,1,0:T(8,128)}, bf16[4,280,2304]{2,1,0:T(8,1...) custom-call(s32[4]{0:T(128)} %dynamic-slice_add_fusion.lens, ...), custom_call_target="tpu_custom_call" | custom-call | tf_op jit(solution)/shard_map/gather_attention/pallas_call | solution.py:494
  94.2 161.1 %backward_reduce.1 = (bf16[2240,768]{1,0:T(8,128)(2,1)}, bf16[8,280,768]{2,1,0:T(8,128)(2,1)}, f32[2,48,1536]{2,1,0:T(8,128)}, f32[1,48,384]{2,1,0:T(8,128)}, f32[1,48,1152]{2,1,0:T(8,128)}, /*index=5*/f32[4,3072]{1,0:T(4,128)}) custom-call(s32[4]{0:T(128)} %dynamic-slice_add_fusion.lens, bf16[2240,768]{1,0:T(8,128)(2,1)} %bitcast.35, f32[1120,768]{1,0:T(8,128)} %bitcast.36, ...), custom_call_target="tpu_custom_call" | custom-call | tf_op jit(solution)/shard_map/backward_reduce/pallas_call | solution.py:1005
  255.3 0.8 slice_reduce_fusion
  256.2 0.9 fusion
  257.1 0.7 dynamic_slice.38
  257.8 0.1 fusion.2
  257.9 0.6 pad_maximum_fusion.2
  258.5 0.8 slice_reduce_fusion.1
  259.3 0.6 fusion.1
  259.9 1.9 slice_bitcast_fusion
  261.8 1.0 reshape_squeeze.15
  262.8 0.7 copy.44
  263.5 0.0 copy-start
  263.5 4.1 %copy.53 = bf16[8,280,768]{2,1,0:T(8,128)(2,1)} copy(bf16[8,280,768]{2,1,0:T(8,128)(2,1)} %bitcast.37) | data formatting | bytes 6881280
  267.6 0.0 copy-done
  267.6 0.0 copy-start.1
  267.7 1.8 copy.54
  269.4 0.0 copy-done.1
  269.4 0.6 copy.55
  (16 shorter events, 0.1 us)
Async XLA Ops:
  263.5 4.1 %copy-start = (bf16[8,280,768]{2,1,0:T(8,128)(2,1)S(1)}, bf16[8,280,768]{2,1,0:T(8,128)(2,1)}, u32[]{:S(2)}) copy-start(bf16[8,280,768]{2,1,0:T(8,128)(2,1)} %get-tuple-element.103) | copy-start | bytes 10321924
  267.6 1.8 copy-start.1

commit v6 on v5

--- a/solution.py
+++ b/solution.py
@@ -328,9 +328,9 @@
     return peers
 
 
-def gather_attn_kernel(lens, tok_all, first_ref, second_ref, b_in,
+def gather_attn_kernel(counts, tok_all, wq_in, wp_in, wu_in, wd_in, bq_in, bu_in, v0, v1, v2, v3, v4, v5,
                        w_one_out, w_two, b_out, qkv_ref, att_ref, prob_ref, hid_ref, n1_ref, n2_ref, vec_ref,
-                       w_one, bias, xbuf, send, recv, bsem, local):
+                       w_one, bias, xbuf, first_ref, second_ref, b_in, vbuf, send, recv, bsem, local):
     p = pl.program_id(0)
     z, y, c, m = place()
     (y1, m1), (y2, m2) = flips(y, c, m)
@@ -420,13 +420,26 @@
 
     @pl.when(p == 0)
     def _():
-        for copy in mine + mine_two:
-            copy.start()
         x_copy.start()
+        for t in range(3):
+            first_ref[:, t * lw : (t + 1) * lw] = wq_in[t].astype(LOW)
+        first_ref[:, 3 * lw : 4 * lw] = wp_in[...].astype(LOW)
+        vbuf[...] = jnp.zeros_like(vbuf)
+        for n, v in enumerate((v0, v1, v2, v3, v4, v5)):
+            vbuf[n : n + 1, :part] = v[...]
+        first_ref[:, 4 * lw :] = vbuf[...].T[:part].astype(LOW)
+        second_ref[:, :cols] = wu_in[...].astype(LOW)
+        second_ref[:, cols:] = wd_in[...].astype(LOW)
+        b_in[...] = jnp.zeros_like(b_in)
+        b_in[0:1, :lw] = bq_in[0:1].astype(LOW).astype(F32)
+        b_in[0:1, lw : 2 * lw] = bq_in[1:2].astype(LOW).astype(F32)
+        b_in[0:1, 2 * lw :] = bu_in[...].astype(LOW).astype(F32)
         greet(z, y, c, m)
         own_z(None)
         own_near(None)
         bias_copy.start()
+        for copy in mine + mine_two:
+            copy.start()
         own_z(0)
         own_z(1)
         loop(3, event_z, None)
@@ -468,7 +481,7 @@
         total = pairs * per_pair
         lax.fori_loop(step * 28 // total, (step + 1) * 28 // total, event, 0)
 
-    attn_body(p, lens[p], xbuf[p], w_one, bias, vec_ref, qkv_ref, att_ref, prob_ref, hid_ref, n1_ref, n2_ref, hook)
+    attn_body(p, TEXT + counts[m * pairs + p], xbuf[p], w_one, bias, vec_ref, qkv_ref, att_ref, prob_ref, hid_ref, n1_ref, n2_ref, hook)
 
     @pl.when(p == pairs - 1)
     def _():
@@ -484,19 +497,23 @@
             lax.fori_loop(0, 31, sent, 0)
 
 
-def gather_attention(lens, tokens, first, second, bias):
-    pairs = lens.shape[0]
+def gather_attention(counts, tokens, w_qkv, w_proj, w_up, w_down, b_qv, b_up, vectors):
+    pairs = counts.shape[0] // 2
     _, rows, width = tokens.shape
-    part = first.shape[0]
+    part, fw = w_up.shape
+    lw = width // 2
     total = Z * Y * C
     hbm = pl.BlockSpec(memory_space=pl.ANY)
     out = lambda dt, *s: jax.ShapeDtypeStruct((pairs,) + s, dt)
+    small = [w_qkv.transpose(1, 0, 2), w_proj.T, w_up, w_down.T, b_qv, b_up.reshape(1, fw)]
+    small += [v.reshape(1, part) for v in vectors]
+    one, two, bias = 4 * lw + EXTRA, 2 * fw, (8, 2 * lw + fw)
     return pl.pallas_call(
         gather_attn_kernel,
         grid_spec=pltpu.PrefetchScalarGridSpec(
             num_scalar_prefetch=1,
             grid=(pairs,),
-            in_specs=[hbm, const_spec(first.shape), const_spec(second.shape), const_spec(bias.shape)],
+            in_specs=[hbm] + [const_spec(a.shape) for a in small],
             out_specs=[
                 hbm, hbm, hbm,
                 pair_spec(rows, 3 * width), pair_spec(rows, width), pair_spec(HEADS, rows, rows),
@@ -504,33 +521,34 @@
                 pl.BlockSpec((8, width), lambda *_: (0, 0)),
             ],
             scratch_shapes=[
-                pltpu.VMEM((2, total * part, first.shape[1]), LOW), pltpu.VMEM((2,) + bias.shape, F32),
-                pltpu.VMEM((pairs, rows, width), LOW),
+                pltpu.VMEM((2, width, one), LOW), pltpu.VMEM((2,) + bias, F32), pltpu.VMEM((pairs, rows, width), LOW),
+                pltpu.VMEM((part, one), LOW), pltpu.VMEM((part, two), LOW), pltpu.VMEM(bias, F32),
+                pltpu.VMEM((EXTRA, EXTRA), F32),
                 pltpu.SemaphoreType.DMA((3, 31)), pltpu.SemaphoreType.DMA((3, 32)),
                 pltpu.SemaphoreType.DMA((2,)), pltpu.SemaphoreType.DMA((7,)),
             ],
         ),
         out_shape=[
-            jax.ShapeDtypeStruct((2, total * part, first.shape[1]), LOW),
-            jax.ShapeDtypeStruct((2, total * part, second.shape[1]), LOW),
-            jax.ShapeDtypeStruct((2,) + bias.shape, F32),
+            jax.ShapeDtypeStruct((2, width, one), LOW),
+            jax.ShapeDtypeStruct((2, width, two), LOW),
+            jax.ShapeDtypeStruct((2,) + bias, F32),
             out(LOW, rows, 3 * width), out(LOW, rows, width), out(LOW, HEADS, rows, rows),
             out(F32, rows, width), out(LOW, rows, width), out(LOW, rows, width),
             jax.ShapeDtypeStruct((8, width), F32),
         ],
         compiler_params=pltpu.CompilerParams(collective_id=0, has_side_effects=True, vmem_limit_bytes=60 * 2**20),
         name="gather_attention",
-    )(lens, tokens, first, second, bias)
+    )(counts, tokens, *small)
 
 
 BLOCKS = 31
 
 
-def back_kernel(lens, cot, hid_in, n2_in, att_in, n1_all, qkv_all, prob_all, tok_all, w_one_in, w_two, bias_ref, vec_ref,
-                block_out, tok_out, r_ff, r_proj, r_qkv, small_out,
+def back_kernel(counts, cot, hid_in, n2_in, att_in, n1_all, qkv_all, prob_all, tok_all, w_one_in, w_two, bias_ref, vec_ref,
+                block_out, tok_out, r_ff, r_proj, r_qkv, o_up, o_qv, o_vec,
                 g_ff, g_proj, g_qkv, rc_ff, rs_ff, rz_ff, rx_ff, rc_p, rs_p, rz_p, rx_p, rc_q, rs_q, rz_q, rx_q,
                 dhid_ref, outbuf, sums, bsum, bsum_up, sbuf, send, recv, local, osem, tsem, ssem):
-    flat, width = outbuf.shape
+    flat, width = dhid_ref.shape
     pairs, rows = qkv_all.shape[0], qkv_all.shape[1]
     groups = w_two.shape[0]
     fw = w_two.shape[2] // 2
@@ -618,7 +636,7 @@
         def final(u):
             value = lined(u, 0)
             arrived(u, rx.at[u], 30)
-            out[u] = value + rx[u].astype(F32)
+            out(u, value + rx[u].astype(F32))
 
             def one(i):
                 copy_of(u, rc.at[0], rc.at[0], i, 0, sib).wait_send()
@@ -627,21 +645,32 @@
 
         return to_sibling, event_y, event_z, event_x, final
 
-    ff_sib, ff_y, ff_z, ff_x, ff_final = family(g_ff, rc_ff, rs_ff, rz_ff, rx_ff, r_ff, 0)
-    p_sib, p_y, p_z, p_x, p_final = family(g_proj, rc_p, rs_p, rz_p, rx_p, r_proj, 2)
-    q_sib, q_y, q_z, q_x, q_final = family(g_qkv, rc_q, rs_q, rz_q, rx_q, r_qkv, 3)
-
-    def out_copies(r):
-        src = outbuf.at[pl.ds(pl.multiple_of(r * half, 16), half)]
-        dst = block_out.at[pl.ds(pl.multiple_of(m * flat + r * half, 16), half)]
-        return pltpu.make_async_copy(src, dst, osem.at[0, r]), pltpu.make_async_remote_copy(
-            src_ref=src, dst_ref=dst, send_sem=osem.at[1, r], recv_sem=osem.at[2, r],
+    def put(ref):
+        def store(u, value):
+            ref[u] = value
+
+        return store
+
+    def put_qkv(u, value):
+        for t in range(3):
+            r_qkv[t] = value[:, t * lw : (t + 1) * lw]
+
+    ff_sib, ff_y, ff_z, ff_x, ff_final = family(g_ff, rc_ff, rs_ff, rz_ff, rx_ff, put(r_ff), 0)
+    p_sib, p_y, p_z, p_x, p_final = family(g_proj, rc_p, rs_p, rz_p, rx_p, put(r_proj), 2)
+    q_sib, q_y, q_z, q_x, q_final = family(g_qkv, rc_q, rs_q, rz_q, rx_q, put_qkv, 3)
+
+    def out_copies(q):
+        src = outbuf.at[q]
+        dst = block_out.at[m * pairs + q]
+        return pltpu.make_async_copy(src, dst, osem.at[0, q]), pltpu.make_async_remote_copy(
+            src_ref=src, dst_ref=dst, send_sem=osem.at[1, q], recv_sem=osem.at[2, q],
             device_id={"dp": me, "mp": 1 - m}, device_id_type=MESH_ID,
         )
 
     def keep_of(r):
         ids = row_ids(half)
-        return ids < jnp.where(ids < rows, lens[2 * r], lens[2 * r + 1] + rows)
+        here = m * pairs + 2 * r
+        return ids < TEXT + jnp.where(ids < rows, counts[here], counts[here + 1] + rows)
 
     def span(r):
         return pl.ds(pl.multiple_of(r * half, 16), half)
@@ -731,10 +760,12 @@
         hid_copy.wait()
 
         def leave(r):
-            outbuf[span(r)] = jnp.where(keep_of(r), hid[span(r)] + acc[span(r)] + vec_ref[5:6], 0.0).astype(LOW)
+            value = jnp.where(keep_of(r), hid[span(r)] + acc[span(r)] + vec_ref[5:6], 0.0)
             acc[span(r)] = jnp.zeros((half, width), F32)
-            for copy in out_copies(r):
-                copy.start()
+            for n in range(2):
+                outbuf[2 * r + n] = value[n * rows : (n + 1) * rows].astype(LOW)
+                for copy in out_copies(2 * r + n):
+                    copy.start()
 
         loop(2, leave)
 
@@ -873,25 +904,21 @@
                 def _():
                     loop(4, lambda i: ff_y(1, 0, i))
 
-                @pl.when((step == 2) | (step == 11))
+                @pl.when((step == 2) | (step == 13))
                 def _():
-                    loop(3, lambda i: ff_z(1, 1 - step // 11, i))
+                    loop(3, lambda i: ff_z(1, 1 - step // 13, i))
 
                 @pl.when((step >= 3) & (step < 7))
                 def _():
                     loop(2, lambda i: p_y(0, 1 - (step - 3) // 2, 2 * lax.rem(step - 3, 2) + i))
 
-                @pl.when((step == 13) | (step == 14))
+                @pl.when((step == 18) | (step == 19))
                 def _():
-                    loop(3, lambda i: p_z(0, 14 - step, i))
-
-                @pl.when((step == 16) | (step == 18))
+                    loop(3, lambda i: p_z(0, 19 - step, i))
+
+                @pl.when((step == 16) | (step == 21))
                 def _():
-                    ff_x((step - 16) // 2)
-
-                @pl.when(step == 20)
-                def _():
-                    p_x(0)
+                    ff_x((step - 16) // 5)
 
             loop(groups * tiles, heads)
             done = sum(
@@ -919,6 +946,9 @@
         for n, (line, at) in enumerate(((2, 0), (2, 1), (2, 2), (3, 1), (2, 3), (3, 0))):
             sbuf[6, line : line + 1, at * width : (at + 1) * width] = sums[n : n + 1]
         s0 = small_copy(0, 6, sib, 0)
+        s1 = small_copy(1, 7, (index(z, 1 - y, c), m), 1)
+        zs = [small_copy(1 + k, 8, beside(k), 1 + k) for k in (1, 2, 3)]
+        s2 = small_copy(5, 9, (me, 1 - m), 5)
         s0.start()
 
         def chunk(i):
@@ -929,37 +959,57 @@
                 acc = acc + dot(n1t[q], dq_all[q, :, at])
             g_qkv[0, :, :, :, at] = acc.astype(LOW).reshape(Z * Y, C, part, lw)
 
+            @pl.when(i == 0)
+            def _():
+                s0.wait()
+                sbuf[7] = sbuf[6] + sbuf[0]
+                s1.start()
+
+            @pl.when(i == 1)
+            def _():
+                p_x(0)
+
             @pl.when(lax.rem(i, 3) == 2)
             def _():
                 q_sib(0, 1 - i // 3)
 
+            @pl.when(i == 2)
+            def _():
+                s1.wait()
+                sbuf[8] = sbuf[7] + sbuf[1]
+                for copy in zs:
+                    copy.start()
+
+            @pl.when(i == 3)
+            def _():
+                loop(4, lambda k: q_y(0, 1, k))
+
             @pl.when(i == 4)
             def _():
-                loop(4, lambda k: q_y(0, 1, k))
+                for copy in zs:
+                    copy.wait()
+                sbuf[9] = sbuf[8] + sbuf[2] + sbuf[3] + sbuf[4]
+                s2.start()
 
         loop(6, chunk)
-        s0.wait()
-        sbuf[7] = sbuf[6] + sbuf[0]
-        s1 = small_copy(1, 7, (index(z, 1 - y, c), m), 1)
-        s1.start()
+        ff_final(0)
         loop(4, lambda i: q_y(0, 0, i))
-        s1.wait()
-        sbuf[8] = sbuf[7] + sbuf[1]
-        s2 = small_copy(2, 8, (me, 1 - m), 2)
-        s2.start()
-        ff_final(0)
         loop(3, lambda i: q_z(0, 1, i))
+        ff_final(1)
         s2.wait()
-        sbuf[9] = sbuf[8] + sbuf[2]
-        zs = [small_copy(2 + k, 9, beside(k), 2 + k) for k in (1, 2, 3)]
-        for copy in zs:
-            copy.start()
-        ff_final(1)
+        sbuf[6] = sbuf[9] + sbuf[5]
+        o_up[...] = sbuf[6, 0:1, pl.ds(pl.multiple_of(m * fw, 128), fw)]
+        for n in range(2):
+            o_qv[n : n + 1] = sbuf[6, 1:2, pl.ds(pl.multiple_of((3 * m + 2 * n) * lw, 128), lw)]
+        dp = lax.axis_index("dp")
+        for n, (line, at) in enumerate(((2, 0), (2, 1), (2, 2), (3, 1), (2, 3), (3, 0))):
+            row = sbuf[6, line : line + 1, at * width : (at + 1) * width]
+            pick = row[:, :part]
+            for d in range(1, Z * Y * C):
+                pick = jnp.where(dp == d, row[:, d * part : (d + 1) * part], pick)
+            o_vec[n : n + 1] = pick
         loop(3, lambda i: q_z(0, 0, i))
         p_final(0)
-        for copy in zs:
-            copy.wait()
-        small_out[...] = (sbuf[9] + sbuf[3] + sbuf[4] + sbuf[5])[:4]
         q_x(0)
         q_final(0)
 
@@ -969,11 +1019,11 @@
 
         loop(pairs, finish)
 
-        def finish_out(r):
-            for copy in out_copies(r):
+        def finish_out(q):
+            for copy in out_copies(q):
                 copy.wait()
 
-        loop(2, finish_out)
+        loop(pairs, finish_out)
 
     pl.run_scoped(
         attention,
@@ -984,7 +1034,7 @@
     )
 
 
-def backward_reduce(lens, tokens, cotangent, hid, n2, att, n1, qkv, prob, w_one, w_two, bias, vec):
+def backward_reduce(counts, tokens, cotangent, hid, n2, att, n1, qkv, prob, w_one, w_two, bias, vec):
     pairs, rows, width = n1.shape
     flat = pairs * rows
     part = width // (Z * Y * C)
@@ -996,25 +1046,26 @@
     for n, w in kinds:
         scratch += [pltpu.VMEM((n * k, part, w), LOW) for k in (16, 8, 6, 1)]
     scratch += [
-        pltpu.VMEM((flat, width), F32), pltpu.VMEM((flat, width), LOW), pltpu.VMEM((8, width), F32),
+        pltpu.VMEM((flat, width), F32), pltpu.VMEM((pairs, rows, width), LOW), pltpu.VMEM((8, width), F32),
         pltpu.VMEM((8, 3 * width), F32), pltpu.VMEM((8, 2 * fw), F32), pltpu.VMEM((10, 8, 2 * fw), F32),
         pltpu.SemaphoreType.DMA((4, BLOCKS)), pltpu.SemaphoreType.DMA((4, BLOCKS)), pltpu.SemaphoreType.DMA((9,)),
-        pltpu.SemaphoreType.DMA((3, 2)), pltpu.SemaphoreType.DMA((3, pairs)), pltpu.SemaphoreType.DMA((2, 6)),
+        pltpu.SemaphoreType.DMA((3, pairs)), pltpu.SemaphoreType.DMA((3, pairs)), pltpu.SemaphoreType.DMA((2, 6)),
     ]
     plane = lambda a: a.reshape(-1, width)
     return pl.pallas_call(
         back_kernel,
         in_specs=[pl.BlockSpec(memory_space=pltpu.SMEM)] + [hbm] * 10 + [vm] * 2,
-        out_specs=[hbm] * 2 + [vm] * 4,
+        out_specs=[hbm] * 2 + [vm] * 6,
         out_shape=[
-            jax.ShapeDtypeStruct((2 * flat, width), LOW), jax.ShapeDtypeStruct((2 * pairs, rows, width), LOW),
-        ]
-        + [jax.ShapeDtypeStruct((n, part, w), F32) for n, w in kinds]
-        + [jax.ShapeDtypeStruct((4, 2 * fw), F32)],
+            jax.ShapeDtypeStruct((2 * pairs, rows, width), LOW), jax.ShapeDtypeStruct((2 * pairs, rows, width), LOW),
+            jax.ShapeDtypeStruct((2, part, fw), F32), jax.ShapeDtypeStruct((1, part, width // 2), F32),
+            jax.ShapeDtypeStruct((3, part, width // 2), F32), jax.ShapeDtypeStruct((1, fw), F32),
+            jax.ShapeDtypeStruct((2, width // 2), F32), jax.ShapeDtypeStruct((6, part), F32),
+        ],
         scratch_shapes=scratch,
         compiler_params=pltpu.CompilerParams(collective_id=1, has_side_effects=True, vmem_limit_bytes=63 * 2**20),
         name="backward_reduce",
-    )(lens, plane(cotangent), plane(hid), plane(n2), plane(att), n1, qkv, prob, tokens, w_one, w_two, bias, vec)
+    )(counts, plane(cotangent), plane(hid), plane(n2), plane(att), n1, qkv, prob, tokens, w_one, w_two, bias, vec)
 
 
 def per_device(
@@ -1030,24 +1081,31 @@
     lw = w_qkv.shape[2]
     fw = w_up.shape[1]
     mine = lax.axis_index("mp")
+    vectors = [attn_gain, attn_shift, b_proj, ffn_gain, ffn_shift, b_down]
+    if direct:
+        w_one, w_two, bias, qkv, att, prob, hid, n1, n2, vec = gather_attention(
+            patch_counts, tokens, w_qkv, w_proj, w_up, w_down, b_qv, b_up, vectors)
+        block_out, tokens_grad, r_ff, r_proj, r_qkv, o_b_up, o_b_qv, o_vec = backward_reduce(
+            patch_counts, tokens, cotangent, hid, n2, att, n1, qkv, prob, w_one, w_two, bias, vec)
+        o_gain, o_shift, o_b_proj, o_b_down, o_ffn_gain, o_ffn_shift = [o_vec[i] for i in range(6)]
+        return (
+            block_out, tokens_grad, o_gain, o_shift, r_qkv.transpose(1, 0, 2), o_b_qv,
+            r_proj[0].T, o_b_proj, o_ffn_gain, o_ffn_shift, r_ff[1], o_b_up[0], r_ff[0].T, o_b_down,
+        )
+
     off = jnp.reshape(mine * pairs, (1,)).astype(jnp.int32)
     lens = TEXT + lax.dynamic_slice_in_dim(patch_counts, mine * pairs, pairs, 0)
-
-    vectors = jnp.stack([attn_gain, attn_shift, b_proj, ffn_gain, ffn_shift, b_down], axis=1)
     first = jnp.concatenate(
-        [w_qkv.reshape(part, 3 * lw), w_proj.T, vectors, jnp.zeros((part, EXTRA - 6), F32)], axis=1
+        [w_qkv.reshape(part, 3 * lw), w_proj.T, jnp.stack(vectors, axis=1), jnp.zeros((part, EXTRA - 6), F32)], axis=1
     ).astype(LOW)
     second = jnp.concatenate([w_up, w_down.T], axis=1).astype(LOW)
     bias = jnp.concatenate([b_qv.reshape(-1), b_up]).astype(LOW).astype(F32)
     bias = jnp.broadcast_to(bias, (8,) + bias.shape)
-    if direct:
-        w_one, w_two, bias, qkv, att, prob, hid, n1, n2, vec = gather_attention(lens, tokens, first, second, bias)
-    else:
-        both_axes = ("mp", "dp")
-        w_one = lax.all_gather(first, both_axes, axis=0, tiled=True).reshape(n_mp, width, -1)
-        w_two = lax.all_gather(second, both_axes, axis=0, tiled=True).reshape(n_mp, width, -1)
-        bias = lax.all_gather(bias, "mp", axis=0)
-        qkv, att, prob, hid, n1, n2, vec = attention_forward(lens, off, tokens, w_one, bias)
+    both_axes = ("mp", "dp")
+    w_one = lax.all_gather(first, both_axes, axis=0, tiled=True).reshape(n_mp, width, -1)
+    w_two = lax.all_gather(second, both_axes, axis=0, tiled=True).reshape(n_mp, width, -1)
+    bias = lax.all_gather(bias, "mp", axis=0)
+    qkv, att, prob, hid, n1, n2, vec = attention_forward(lens, off, tokens, w_one, bias)
 
     def grad(left, right):
         return jnp.einsum(
@@ -1070,25 +1128,16 @@
         other = lax.ppermute(array, "mp", [(0, 1), (1, 0)])
         return jnp.where(mine == 0, jnp.concatenate([array, other]), jnp.concatenate([other, array]))
 
-    if direct:
-        block_out, tokens_grad, r_ff, r_proj, r_qkv, small = backward_reduce(
-            lens, tokens, cotangent, hid, n2, att, n1, qkv, prob, w_one, w_two, bias, vec)
-        block_out = block_out.reshape(tokens.shape)
-        r_down, r_up, r_proj, r_qkv = r_ff[0], r_ff[1], r_proj[0], r_qkv[0]
-        flat = small[1, : 3 * width].reshape(n_mp, 3, lw)
-        small = jnp.concatenate([
-            small[2], small[3, : 2 * width], flat[:, 0].reshape(-1), flat[:, 2].reshape(-1), small[0]])
-    else:
-        out_here, act, dpre, dhid, dlow, upl, sums_two, bsum_up = ffn(lens, off, n2, hid, cotangent, w_two, bias, vec)
-        block_out = both(out_here)
-        tok_here, dqkv, sums_one, bsum_qkv = attention_backward(lens, off, tokens, dhid, qkv, prob, w_one, vec)
-        tokens_grad = both(tok_here)
-        flat = bsum_qkv[0].reshape(n_mp, 3, lw)
-        small = jnp.concatenate([
-            sums_one[0], sums_one[1], sums_two[2], sums_two[0], sums_two[1], sums_two[3],
-            flat[:, 0].reshape(-1), flat[:, 2].reshape(-1), bsum_up[0]])
-        r_up, r_down, r_proj, r_qkv, small = reduce(
-            [grad(n2, dpre), grad(upl, act), grad(dlow, att), grad(n1, dqkv)], small)
+    out_here, act, dpre, dhid, dlow, upl, sums_two, bsum_up = ffn(lens, off, n2, hid, cotangent, w_two, bias, vec)
+    block_out = both(out_here)
+    tok_here, dqkv, sums_one, bsum_qkv = attention_backward(lens, off, tokens, dhid, qkv, prob, w_one, vec)
+    tokens_grad = both(tok_here)
+    flat = bsum_qkv[0].reshape(n_mp, 3, lw)
+    small = jnp.concatenate([
+        sums_one[0], sums_one[1], sums_two[2], sums_two[0], sums_two[1], sums_two[3],
+        flat[:, 0].reshape(-1), flat[:, 2].reshape(-1), bsum_up[0]])
+    r_up, r_down, r_proj, r_qkv, small = reduce(
+        [grad(n2, dpre), grad(upl, act), grad(dlow, att), grad(n1, dqkv)], small)
     place_dp = lax.axis_index("dp") * part
 
     def piece(i):

time: 271 us -> 240 us (0.89)
  Pallas kernels: 241 us -> 224 us
  other arithmetic: 11.7 us -> 1.31 us
  local copies, waits for them, and re-layouts: 16.2 us -> 12.4 us
    pallas_call x1, Pallas kernels: 161 us -> 144 us  [backward_reduce(): pl.pallas_call(back_kernel, in_specs=[pl.BlockSpec(memory_space=pltpu.SME...]
    another operation x10 -> x0, other arithmetic: 6.9 us -> none  [the longest x6 3.95 us: per_device(): jnp.stack([attn_gain, attn_shift, b_proj, ffn_gain, ffn_shift, b_down], a...]
    unnamed x12 -> x13, local copies, waits for them, and re-layouts: 7.22 us -> 7.78 us
where the time goes in v6:
time: 240 us; the launch traced here: 239 us
  Pallas kernels  224 us (93%)
  local copies, waits for them, and re-layouts  12.4 us (5%)
    pallas_call x1, Pallas kernels, backward_reduce(): pl.pallas_call(back_kernel, in_specs=[pl.BlockSpec(memory_space=pltpu.SME...  144 us
    pallas_call x1, Pallas kernels, gather_attention(): pl.pallas_call(gather_attn_kernel, grid_spec=pltpu.PrefetchScalarGridSpec...  80.5 us
    unnamed x13, local copies, waits for them, and re-layouts  7.78 us

profile of v6, /device:TPU:8, one launch (start us, length us, event | category | flops | bytes accessed | tf_op | source)
XLA Modules:
  0.0 238.6 jit_solution(7420685975031246353)
XLA Ops:
  0.6 1.3 reshape.62.bu_in
  1.9 80.5 %gather_attention.1 = (bf16[2,768,1664]{2,1,0:T(8,128)(2,1)}, bf16[2,768,3072]{2,1,0:T(8,128)(2,1)}, f32[2,8,2304]{2,1,0:T(8,128)}, bf16[4,280,2304]{2,1,0:T(8,1...) custom-call(s32[8]{0:T(128)} %counts.3, ...), custom_call_target="tpu_custom_call" | custom-call | tf_op jit(solution)/shard_map/gather_attention/pallas_call | solution.py:511
  82.4 143.7 %backward_reduce.1 = (bf16[8,280,768]{2,1,0:T(8,128)(2,1)}, bf16[8,280,768]{2,1,0:T(8,128)(2,1)}, f32[2,48,1536]{2,1,0:T(8,128)}, f32[1,48,384]{2,1,0:T(8,128)},...) custom-call(s32[8]{0:T(128)} %counts.3, bf16[2240,768]{1,0:T(8,128)(2,1)} %bitcast.35, ...), custom_call_target="tpu_custom_call" | custom-call | tf_op jit(solution)/shard_map/backward_reduce/pallas_call | solution.py:1055
  226.2 1.4 slice_bitcast_fusion.2
  227.6 1.3 reduce
  228.9 1.9 slice_bitcast_fusion
  230.8 0.0 copy-start
  230.8 4.1 %copy.34 = bf16[8,280,768]{2,1,0:T(8,128)(2,1)} copy(bf16[8,280,768]{2,1,0:T(8,128)(2,1)} %get-tuple-element.72) | data formatting | bytes 6881280
  234.9 0.0 copy-done
  234.9 0.0 copy-start.1
  234.9 0.0 copy-start.3
  234.9 0.0 copy-start.2
  234.9 1.8 copy.35
  236.7 0.0 copy-done.1
  236.7 0.7 copy.36
  237.4 0.0 copy-done.3
  237.4 0.6 copy.37
  238.0 0.0 copy-done.2
  238.0 0.6 copy.38
Async XLA Ops:
  230.8 4.1 %copy-start = (bf16[8,280,768]{2,1,0:T(8,128)(2,1)S(1)}, bf16[8,280,768]{2,1,0:T(8,128)(2,1)}, u32[]{:S(2)}) copy-start(bf16[8,280,768]{2,1,0:T(8,128)(2,1)} %get-tuple-element.73) | copy-start | bytes 10321924
  234.9 1.8 copy-start.1
  234.9 2.5 %copy-start.3 = (f32[2,384]{1,0:T(2,128)S(1)}, f32[2,384]{1,0:T(2,128)}, u32[]{:S(2)}) copy-start(f32[2,384]{1,0:T(2,128)} %get-tuple-element.77) | copy-start | bytes 9220
  234.9 3.0 %copy-start.2 = (f32[1,48,384]{2,1,0:T(8,128)S(1)}, f32[1,48,384]{2,1,0:T(8,128)}, u32[]{:S(2)}) copy-start(f32[1,48,384]{2,1,0:T(8,128)} %get-tuple-element.47) | copy-start | bytes 221188

commit v7 on v6

--- a/solution.py
+++ b/solution.py
@@ -440,9 +440,9 @@
         bias_copy.start()
         for copy in mine + mine_two:
             copy.start()
+        loop(3, event_z, None)
         own_z(0)
         own_z(1)
-        loop(3, event_z, None)
         loop(4, event_one, None)
         own_near(0)
         loop(3, event_z, 0)
@@ -545,9 +545,9 @@
 
 
 def back_kernel(counts, cot, hid_in, n2_in, att_in, n1_all, qkv_all, prob_all, tok_all, w_one_in, w_two, bias_ref, vec_ref,
-                block_out, tok_out, r_ff, r_proj, r_qkv, o_up, o_qv, o_vec,
+                block_out, tok_out, r_down, r_up, r_proj, r_qkv, o_up, o_qv, o_vec,
                 g_ff, g_proj, g_qkv, rc_ff, rs_ff, rz_ff, rx_ff, rc_p, rs_p, rz_p, rx_p, rc_q, rs_q, rz_q, rx_q,
-                dhid_ref, outbuf, sums, bsum, bsum_up, sbuf, send, recv, local, osem, tsem, ssem):
+                dhid_ref, outbuf, sums, bsum, bsum_up, sbuf, send, recv, local, osem, tsem, ssem, n1_sem):
     flat, width = dhid_ref.shape
     pairs, rows = qkv_all.shape[0], qkv_all.shape[1]
     groups = w_two.shape[0]
@@ -557,6 +557,7 @@
     tiles = lw // 128
     half = flat // 2
     part = r_proj.shape[1]
+    high = pairs * (rows + (-rows) % 16)
     z, y, c, m = place()
     me = index(z, y, c)
     sib = (index(z, y, 1 - c), m)
@@ -651,11 +652,14 @@
 
         return store
 
+    def put_ff(u, value):
+        (r_down, r_up)[u][...] = value
+
     def put_qkv(u, value):
         for t in range(3):
             r_qkv[t] = value[:, t * lw : (t + 1) * lw]
 
-    ff_sib, ff_y, ff_z, ff_x, ff_final = family(g_ff, rc_ff, rs_ff, rz_ff, rx_ff, put(r_ff), 0)
+    ff_sib, ff_y, ff_z, ff_x, ff_final = family(g_ff, rc_ff, rs_ff, rz_ff, rx_ff, put_ff, 0)
     p_sib, p_y, p_z, p_x, p_final = family(g_proj, rc_p, rs_p, rz_p, rx_p, put(r_proj), 2)
     q_sib, q_y, q_z, q_x, q_final = family(g_qkv, rc_q, rs_q, rz_q, rx_q, put_qkv, 3)
 
@@ -825,22 +829,22 @@
         pltpu.VMEM((flat, groups * fw), LOW), pltpu.VMEM((flat, fc), LOW), pltpu.VMEM((2, 2, width, fc), LOW),
     )
 
-    def attention(w_ref, qkv_buf, prob_buf, n1_buf, x_buf, do_ref, n1t, dq_all, tokbuf):
+    def attention(w_ref, qkv_buf, prob_buf, x_buf, do_ref, n1, n1t, dq_all):
+        high = n1.shape[0] // pairs
         w_copy = pltpu.make_async_copy(w_one_in, w_ref, local.at[8])
 
         def loads(p):
             slot = lax.rem(p, 2)
             pieces = [
-                (qkv_all.at[p], qkv_buf), (prob_all.at[p], prob_buf), (n1_all.at[p], n1_buf),
-                (tok_all.at[m * pairs + p], x_buf),
+                (qkv_all.at[p], qkv_buf), (prob_all.at[p], prob_buf), (tok_all.at[m * pairs + p], x_buf),
             ]
             return [
-                pltpu.make_async_copy(src, dst.at[slot], local.at[slot * 4 + t])
+                pltpu.make_async_copy(src, dst.at[slot], local.at[slot * 3 + t])
                 for t, (src, dst) in enumerate(pieces)
             ]
 
         def tok_copies(p):
-            src, dst = tokbuf.at[p], tok_out.at[m * pairs + p]
+            src, dst = n1.at[pl.ds(pl.multiple_of(p * high, 16), rows)], tok_out.at[m * pairs + p]
             return pltpu.make_async_copy(src, dst, tsem.at[0, p]), pltpu.make_async_remote_copy(
                 src_ref=src, dst_ref=dst, send_sem=tsem.at[1, p], recv_sem=tsem.at[2, p],
                 device_id={"dp": me, "mp": 1 - m}, device_id_type=MESH_ID,
@@ -849,7 +853,26 @@
         w_copy.start()
         for copy in loads(0):
             copy.start()
+        n1_copies = [
+            pltpu.make_async_copy(n1_all.at[p], n1.at[pl.ds(p * high, rows)], n1_sem.at[p]) for p in range(pairs)
+        ]
+        for copy in n1_copies:
+            copy.start()
         w_copy.wait()
+
+        def attended_back(r):
+            dlow = dhid_ref[span(r)].astype(LOW)
+            for mm in range(groups):
+                value = dot(dlow, w_ref[mm, :, 3 * lw : 4 * lw])
+                for n in range(2):
+                    do_ref[2 * r + n, :, mm * lw : (mm + 1) * lw] = value[n * rows : (n + 1) * rows].astype(LOW)
+
+        loop(2, attended_back)
+        for p, copy in enumerate(n1_copies):
+            copy.wait()
+            n1[p * high + rows : (p + 1) * high] = jnp.zeros((high - rows, width), LOW)
+            dq_all[p * high + rows : (p + 1) * high] = jnp.zeros((high - rows, 3 * width), LOW)
+        n1t[...] = n1[...].T
         first = lax.broadcasted_iota(jnp.int32, (1, 128), 1) < HEAD_DIM
 
         def one_pair(p):
@@ -861,12 +884,9 @@
                     copy.start()
 
             dhid = dhid_ref[pl.ds(pl.multiple_of(p * rows, 8), rows)]
-            dlow = dhid.astype(LOW)
-            for mm in range(groups):
-                do_ref[:, mm * lw : (mm + 1) * lw] = dot(dlow, w_ref[mm, :, 3 * lw : 4 * lw]).astype(LOW)
+            here = pl.ds(pl.multiple_of(p * high, 16), rows)
             for copy in loads(p):
                 copy.wait()
-            n1t[p] = n1_buf[slot].T
 
             def heads(hp):
                 lane = (hp // tiles) * 3 * lw + lax.rem(hp, tiles) * 128
@@ -877,7 +897,7 @@
                 q2 = qkv_buf[slot, :, cols(0)] * 0.125
                 k2t = qkv_buf[slot, :, cols(1)].T
                 v2 = qkv_buf[slot, :, cols(2)]
-                do2 = do_ref[:, pl.ds(pl.multiple_of(hp * 128, 128), 128)]
+                do2 = do_ref[p, :, pl.ds(pl.multiple_of(hp * 128, 128), 128)]
                 dq_t = []
                 dk = dv = 0.0
                 for h in range(2):
@@ -893,9 +913,9 @@
                     dk = dk + dot(dst, qh)
                     dq_t.append(dot(k2t[h * HEAD_DIM : (h + 1) * HEAD_DIM], dst))
                 dq = (jnp.concatenate(dq_t, axis=0) * 0.125).T
-                dq_all[p, :, cols(0)] = dq.astype(LOW)
-                dq_all[p, :, cols(1)] = dk.astype(LOW)
-                dq_all[p, :, cols(2)] = dv.astype(LOW)
+                dq_all[here, cols(0)] = dq.astype(LOW)
+                dq_all[here, cols(1)] = dk.astype(LOW)
+                dq_all[here, cols(2)] = dv.astype(LOW)
                 bsum[0:1, cols(0)] += jnp.sum(dq, axis=0, keepdims=True)
                 bsum[0:1, cols(2)] += jnp.sum(dv, axis=0, keepdims=True)
                 step = p * (groups * tiles) + hp
@@ -922,11 +942,11 @@
 
             loop(groups * tiles, heads)
             done = sum(
-                dot(dq_all[p, :, mm * 3 * lw : (mm + 1) * 3 * lw], w_ref[mm, :, : 3 * lw], NT) for mm in range(groups))
+                dot(dq_all[here, mm * 3 * lw : (mm + 1) * 3 * lw], w_ref[mm, :, : 3 * lw], NT) for mm in range(groups))
             xhat, r = moments(x_buf[slot].astype(F32))
             dg = done * vec_ref[0:1]
             dn = r * (dg - jnp.mean(dg, axis=-1, keepdims=True) - xhat * jnp.mean(dg * xhat, axis=-1, keepdims=True))
-            tokbuf[p] = (dhid + dn).astype(LOW)
+            n1[here] = (dhid + dn).astype(LOW)
             for copy in tok_copies(p):
                 copy.start()
             sums[0:1] += jnp.sum(done * xhat, axis=0, keepdims=True)
@@ -954,10 +974,7 @@
         def chunk(i):
             mm = lax.rem(m + 1 + i // 3, 2)
             at = pl.ds(pl.multiple_of(mm * 3 * lw + lax.rem(i, 3) * lw, 128), lw)
-            acc = dot(n1t[0], dq_all[0, :, at])
-            for q in range(1, pairs):
-                acc = acc + dot(n1t[q], dq_all[q, :, at])
-            g_qkv[0, :, :, :, at] = acc.astype(LOW).reshape(Z * Y, C, part, lw)
+            g_qkv[0, :, :, :, at] = dot(n1t[...], dq_all[:, at]).astype(LOW).reshape(Z * Y, C, part, lw)
 
             @pl.when(i == 0)
             def _():
@@ -1028,9 +1045,8 @@
     pl.run_scoped(
         attention,
         pltpu.VMEM(w_one_in.shape, LOW), pltpu.VMEM((2, rows, 3 * width), LOW), pltpu.VMEM((2, HEADS, rows, rows), LOW),
-        pltpu.VMEM((2, rows, width), LOW), pltpu.VMEM((2, rows, width), LOW), pltpu.VMEM((rows, width), LOW),
-        pltpu.VMEM((pairs, width, rows), LOW), pltpu.VMEM((pairs, rows, 3 * width), LOW),
-        pltpu.VMEM((pairs, rows, width), LOW),
+        pltpu.VMEM((2, rows, width), LOW), pltpu.VMEM((pairs, rows, width), LOW),
+        pltpu.VMEM((high, width), LOW), pltpu.VMEM((width, high), LOW), pltpu.VMEM((high, 3 * width), LOW),
     )
 
 
@@ -1050,15 +1066,17 @@
         pltpu.VMEM((8, 3 * width), F32), pltpu.VMEM((8, 2 * fw), F32), pltpu.VMEM((10, 8, 2 * fw), F32),
         pltpu.SemaphoreType.DMA((4, BLOCKS)), pltpu.SemaphoreType.DMA((4, BLOCKS)), pltpu.SemaphoreType.DMA((9,)),
         pltpu.SemaphoreType.DMA((3, pairs)), pltpu.SemaphoreType.DMA((3, pairs)), pltpu.SemaphoreType.DMA((2, 6)),
+        pltpu.SemaphoreType.DMA((pairs,)),
     ]
     plane = lambda a: a.reshape(-1, width)
     return pl.pallas_call(
         back_kernel,
         in_specs=[pl.BlockSpec(memory_space=pltpu.SMEM)] + [hbm] * 10 + [vm] * 2,
-        out_specs=[hbm] * 2 + [vm] * 6,
+        out_specs=[hbm] * 2 + [vm] * 7,
         out_shape=[
             jax.ShapeDtypeStruct((2 * pairs, rows, width), LOW), jax.ShapeDtypeStruct((2 * pairs, rows, width), LOW),
-            jax.ShapeDtypeStruct((2, part, fw), F32), jax.ShapeDtypeStruct((1, part, width // 2), F32),
+            jax.ShapeDtypeStruct((part, fw), F32), jax.ShapeDtypeStruct((part, fw), F32),
+            jax.ShapeDtypeStruct((1, part, width // 2), F32),
             jax.ShapeDtypeStruct((3, part, width // 2), F32), jax.ShapeDtypeStruct((1, fw), F32),
             jax.ShapeDtypeStruct((2, width // 2), F32), jax.ShapeDtypeStruct((6, part), F32),
         ],
@@ -1085,12 +1103,12 @@
     if direct:
         w_one, w_two, bias, qkv, att, prob, hid, n1, n2, vec = gather_attention(
             patch_counts, tokens, w_qkv, w_proj, w_up, w_down, b_qv, b_up, vectors)
-        block_out, tokens_grad, r_ff, r_proj, r_qkv, o_b_up, o_b_qv, o_vec = backward_reduce(
+        block_out, tokens_grad, r_down, r_up, r_proj, r_qkv, o_b_up, o_b_qv, o_vec = backward_reduce(
             patch_counts, tokens, cotangent, hid, n2, att, n1, qkv, prob, w_one, w_two, bias, vec)
         o_gain, o_shift, o_b_proj, o_b_down, o_ffn_gain, o_ffn_shift = [o_vec[i] for i in range(6)]
         return (
             block_out, tokens_grad, o_gain, o_shift, r_qkv.transpose(1, 0, 2), o_b_qv,
-            r_proj[0].T, o_b_proj, o_ffn_gain, o_ffn_shift, r_ff[1], o_b_up[0], r_ff[0].T, o_b_down,
+            r_proj[0].T, o_b_proj, o_ffn_gain, o_ffn_shift, r_up, o_b_up[0], r_down.T, o_b_down,
         )
 
     off = jnp.reshape(mine * pairs, (1,)).astype(jnp.int32)

time: 240 us -> 234 us (0.975)
  Pallas kernels: 224 us -> 219 us
    pallas_call x1, Pallas kernels: 144 us -> 140 us  [backward_reduce(): pl.pallas_call(back_kernel, in_specs=[pl.BlockSpec(memory_space=pltpu.SME...]
    unnamed x13 -> x19, local copies, waits for them, and re-layouts: 7.78 us -> 9.21 us
where the time goes in v7:
time: 234 us; the launch traced here: 233 us
  Pallas kernels  219 us (94%)
  local copies, waits for them, and re-layouts  11.9 us (5%)
    pallas_call x1, Pallas kernels, backward_reduce(): pl.pallas_call(back_kernel, in_specs=[pl.BlockSpec(memory_space=pltpu.SME...  140 us
    pallas_call x1, Pallas kernels, gather_attention(): pl.pallas_call(gather_attn_kernel, grid_spec=pltpu.PrefetchScalarGridSpec...  79.6 us
    unnamed x19, local copies, waits for them, and re-layouts  9.21 us

profile of v7, /device:TPU:8, one launch (start us, length us, event | category | flops | bytes accessed | tf_op | source)
XLA Modules:
  0.0 233.1 jit_solution(39078740400575643)
XLA Ops:
  0.6 1.3 reshape.62.bu_in
  1.9 79.6 %gather_attention.1 = (bf16[2,768,1664]{2,1,0:T(8,128)(2,1)}, bf16[2,768,3072]{2,1,0:T(8,128)(2,1)}, f32[2,8,2304]{2,1,0:T(8,128)}, bf16[4,280,2304]{2,1,0:T(8,1...) custom-call(s32[8]{0:T(128)} %counts.3, ...), custom_call_target="tpu_custom_call" | custom-call | tf_op jit(solution)/shard_map/gather_attention/pallas_call | solution.py:511
  81.5 139.5 %backward_reduce.1 = (bf16[8,280,768]{2,1,0:T(8,128)(2,1)}, bf16[8,280,768]{2,1,0:T(8,128)(2,1)}, f32[48,1536]{1,0:T(8,128)}, f32[48,1536]{1,0:T(8,128)}, f32[1,...) custom-call(s32[8]{0:T(128)} %counts.3, ...), custom_call_target="tpu_custom_call" | custom-call | tf_op jit(solution)/shard_map/backward_reduce/pallas_call | solution.py:1072
  221.1 1.4 slice_bitcast_fusion
  222.5 1.3 reduce
  223.8 0.0 copy-start
  223.8 4.1 %copy.36 = bf16[8,280,768]{2,1,0:T(8,128)(2,1)} copy(bf16[8,280,768]{2,1,0:T(8,128)(2,1)} %get-tuple-element.72) | data formatting | bytes 6881280
  227.9 0.0 copy-done
  227.9 0.0 copy-start.3
  227.9 0.0 copy-start.5
  227.9 0.0 copy-start.4
  227.9 0.0 copy-start.2
  227.9 0.0 copy-start.1
  228.0 1.8 copy.37
  229.7 0.0 copy-done.3
  229.7 0.7 copy.38
  230.4 0.0 copy-done.5
  230.4 0.6 copy.39
  231.0 0.0 copy-done.4
  231.0 0.6 copy.40
  231.6 0.0 copy-done.2
  231.6 0.7 copy.41
  232.3 0.0 copy-done.1
  232.3 0.7 copy.42
Async XLA Ops:
  223.8 4.1 %copy-start = (bf16[8,280,768]{2,1,0:T(8,128)(2,1)S(1)}, bf16[8,280,768]{2,1,0:T(8,128)(2,1)}, u32[]{:S(2)}) copy-start(bf16[8,280,768]{2,1,0:T(8,128)(2,1)} %get-tuple-element.73) | copy-start | bytes 10321924
  227.9 1.8 copy-start.3
  227.9 2.5 %copy-start.5 = (f32[2,384]{1,0:T(2,128)S(1)}, f32[2,384]{1,0:T(2,128)}, u32[]{:S(2)}) copy-start(f32[2,384]{1,0:T(2,128)} %get-tuple-element.77) | copy-start | bytes 9220
  227.9 3.1 %copy-start.4 = (f32[1,48,384]{2,1,0:T(8,128)S(1)}, f32[1,48,384]{2,1,0:T(8,128)}, u32[]{:S(2)}) copy-start(f32[1,48,384]{2,1,0:T(8,128)} %get-tuple-element.48) | copy-start | bytes 221188
  227.9 3.7 %copy-start.2 = (f32[48,1536]{1,0:T(8,128)S(1)}, f32[48,1536]{1,0:T(8,128)}, u32[]{:S(2)}) copy-start(f32[48,1536]{1,0:T(8,128)} %get-tuple-element.82) | copy-start | bytes 884740
  227.9 4.4 %copy-start.1 = (f32[48,1536]{1,0:T(8,128)S(1)}, f32[48,1536]{1,0:T(8,128)}, u32[]{:S(2)}) copy-start(f32[48,1536]{1,0:T(8,128)} %get-tuple-element.51) | copy-start | bytes 884740

commit v8 on v7

--- a/solution.py
+++ b/solution.py
@@ -433,7 +433,7 @@
         b_in[...] = jnp.zeros_like(b_in)
         b_in[0:1, :lw] = bq_in[0:1].astype(LOW).astype(F32)
         b_in[0:1, lw : 2 * lw] = bq_in[1:2].astype(LOW).astype(F32)
-        b_in[0:1, 2 * lw :] = bu_in[...].astype(LOW).astype(F32)
+        b_in[0:1, 2 * lw :] = bu_in[...].reshape(1, cols).astype(LOW).astype(F32)
         greet(z, y, c, m)
         own_z(None)
         own_near(None)
@@ -505,7 +505,7 @@
     total = Z * Y * C
     hbm = pl.BlockSpec(memory_space=pl.ANY)
     out = lambda dt, *s: jax.ShapeDtypeStruct((pairs,) + s, dt)
-    small = [w_qkv.transpose(1, 0, 2), w_proj.T, w_up, w_down.T, b_qv, b_up.reshape(1, fw)]
+    small = [w_qkv.transpose(1, 0, 2), w_proj.T, w_up, w_down.T, b_qv, b_up]
     small += [v.reshape(1, part) for v in vectors]
     one, two, bias = 4 * lw + EXTRA, 2 * fw, (8, 2 * lw + fw)
     return pl.pallas_call(
@@ -572,8 +572,11 @@
 
         lax.fori_loop(0, n, one, 0)
 
-    def family(grad, rc, rs, rz, rx, out, row0):
+    def family(grad, rc, rs, rz, rx, out, row0, split):
         cols = rc.shape[2]
+        fx = c * split
+        near = (index(z, y + (1 - fx) * (1 - 2 * y), c), m + fx * (1 - 2 * m))
+        far = (index(z, y + fx * (1 - 2 * y), c), m + (1 - fx) * (1 - 2 * m))
 
         def copy_of(u, src, dst, out_sem, in_sem, to):
             return pltpu.make_async_remote_copy(
@@ -581,14 +584,20 @@
                 device_id={"dp": to[0], "mp": to[1]}, device_id_type=MESH_ID,
             )
 
+        def swap(ra, rb, cc):
+            f = cc * split
+            return f * rb + (1 - f) * ra, f * ra + (1 - f) * rb
+
         def block(u, ra, rb, k, cc):
-            yy = y + ra * (1 - 2 * y)
-            mm = m + rb * (1 - 2 * m)
+            dy, dm = swap(ra, rb, cc)
+            yy = y + dy * (1 - 2 * y)
+            mm = m + dm * (1 - 2 * m)
             return u, lax.rem(z + k, Z) * Y + yy, cc, slice(None), pl.ds(pl.multiple_of(mm * cols, 128), cols)
 
-        def to_sibling(u, rb):
+        def to_sibling(u, dm):
             def one(i):
-                ra, k = 1 - i // 4, lax.rem(i + 1, 4)
+                ra, rb = swap(1 - i // 4, dm, 1 - c)
+                k = lax.rem(i + 1, 4)
                 slot = (ra * 2 + rb) * 4 + k
                 copy_of(u, grad.at[block(u, ra, rb, k, 1 - c)], rc.at[u * 16 + slot], slot, slot, sib).start()
 
@@ -621,7 +630,7 @@
             slot = u * 16 + (2 + rb) * 4 + k
             at = rb * 4 + k
             rc[slot] = base(u, 1, rb, k).astype(LOW)
-            copy_of(u, rc.at[slot], rs.at[u * 8 + at], 16 + at, 16 + at, (index(z, 1 - y, c), m)).start()
+            copy_of(u, rc.at[slot], rs.at[u * 8 + at], 16 + at, 16 + at, near).start()
 
         def event_z(u, rb, i):
             k = 1 + i
@@ -632,7 +641,7 @@
 
         def event_x(u):
             rc[u * 16 + 4] = lined(u, 1).astype(LOW)
-            copy_of(u, rc.at[u * 16 + 4], rx.at[u], 30, 30, (me, 1 - m)).start()
+            copy_of(u, rc.at[u * 16 + 4], rx.at[u], 30, 30, far).start()
 
         def final(u):
             value = lined(u, 0)
@@ -659,9 +668,9 @@
         for t in range(3):
             r_qkv[t] = value[:, t * lw : (t + 1) * lw]
 
-    ff_sib, ff_y, ff_z, ff_x, ff_final = family(g_ff, rc_ff, rs_ff, rz_ff, rx_ff, put_ff, 0)
-    p_sib, p_y, p_z, p_x, p_final = family(g_proj, rc_p, rs_p, rz_p, rx_p, put(r_proj), 2)
-    q_sib, q_y, q_z, q_x, q_final = family(g_qkv, rc_q, rs_q, rz_q, rx_q, put_qkv, 3)
+    ff_sib, ff_y, ff_z, ff_x, ff_final = family(g_ff, rc_ff, rs_ff, rz_ff, rx_ff, put_ff, 0, 0)
+    p_sib, p_y, p_z, p_x, p_final = family(g_proj, rc_p, rs_p, rz_p, rx_p, put(r_proj), 2, 0)
+    q_sib, q_y, q_z, q_x, q_final = family(g_qkv, rc_q, rs_q, rz_q, rx_q, put_qkv, 3, 1)
 
     def out_copies(q):
         src = outbuf.at[q]
@@ -1015,7 +1024,7 @@
         ff_final(1)
         s2.wait()
         sbuf[6] = sbuf[9] + sbuf[5]
-        o_up[...] = sbuf[6, 0:1, pl.ds(pl.multiple_of(m * fw, 128), fw)]
+        o_up[...] = sbuf[6, 0:1, pl.ds(pl.multiple_of(m * fw, 128), fw)].reshape(fw)
         for n in range(2):
             o_qv[n : n + 1] = sbuf[6, 1:2, pl.ds(pl.multiple_of((3 * m + 2 * n) * lw, 128), lw)]
         dp = lax.axis_index("dp")
@@ -1077,7 +1086,7 @@
             jax.ShapeDtypeStruct((2 * pairs, rows, width), LOW), jax.ShapeDtypeStruct((2 * pairs, rows, width), LOW),
             jax.ShapeDtypeStruct((part, fw), F32), jax.ShapeDtypeStruct((part, fw), F32),
             jax.ShapeDtypeStruct((1, part, width // 2), F32),
-            jax.ShapeDtypeStruct((3, part, width // 2), F32), jax.ShapeDtypeStruct((1, fw), F32),
+            jax.ShapeDtypeStruct((3, part, width // 2), F32), jax.ShapeDtypeStruct((fw,), F32),
             jax.ShapeDtypeStruct((2, width // 2), F32), jax.ShapeDtypeStruct((6, part), F32),
         ],
         scratch_shapes=scratch,
@@ -1108,7 +1117,7 @@
         o_gain, o_shift, o_b_proj, o_b_down, o_ffn_gain, o_ffn_shift = [o_vec[i] for i in range(6)]
         return (
             block_out, tokens_grad, o_gain, o_shift, r_qkv.transpose(1, 0, 2), o_b_qv,
-            r_proj[0].T, o_b_proj, o_ffn_gain, o_ffn_shift, r_up, o_b_up[0], r_down.T, o_b_down,
+            r_proj[0].T, o_b_proj, o_ffn_gain, o_ffn_shift, r_up, o_b_up, r_down.T, o_b_down,
         )
 
     off = jnp.reshape(mine * pairs, (1,)).astype(jnp.int32)

time: 234 us -> 235 us (level)
    unnamed x19 -> x22, local copies, waits for them, and re-layouts: 9.21 us -> 9.82 us
where the time goes in v8:
time: 235 us; the launch traced here: 232 us
  Pallas kernels  220 us (94%)
  local copies, waits for them, and re-layouts  11.3 us (5%)
    pallas_call x1, Pallas kernels, backward_reduce(): pl.pallas_call(back_kernel, in_specs=[pl.BlockSpec(memory_space=pltpu.SME...  140 us
    pallas_call x1, Pallas kernels, gather_attention(): pl.pallas_call(gather_attn_kernel, grid_spec=pltpu.PrefetchScalarGridSpec...  79.5 us
    unnamed x22, local copies, waits for them, and re-layouts  9.82 us

profile of v8, /device:TPU:8, one launch (start us, length us, event | category | flops | bytes accessed | tf_op | source)
XLA Modules:
  0.0 231.8 jit_solution(12962728747979602424)
XLA Ops:
  0.6 79.5 %gather_attention.1 = (bf16[2,768,1664]{2,1,0:T(8,128)(2,1)}, bf16[2,768,3072]{2,1,0:T(8,128)(2,1)}, f32[2,8,2304]{2,1,0:T(8,128)}, bf16[4,280,2304]{2,1,0:T(8,1...) custom-call(s32[8]{0:T(128)} %counts.3, ...), custom_call_target="tpu_custom_call" | custom-call | tf_op jit(solution)/shard_map/gather_attention/pallas_call | solution.py:511
  80.2 140.2 %backward_reduce.1 = (bf16[8,280,768]{2,1,0:T(8,128)(2,1)}, bf16[8,280,768]{2,1,0:T(8,128)(2,1)}, f32[48,1536]{1,0:T(8,128)}, f32[48,1536]{1,0:T(8,128)}, f32[1,...) custom-call(s32[8]{0:T(128)} %counts.3, ...), custom_call_target="tpu_custom_call" | custom-call | tf_op jit(solution)/shard_map/backward_reduce/pallas_call | solution.py:1081
  220.4 1.5 slice_bitcast_fusion
  221.9 0.0 copy-start
  221.9 4.1 %copy.37 = bf16[8,280,768]{2,1,0:T(8,128)(2,1)} copy(bf16[8,280,768]{2,1,0:T(8,128)(2,1)} %get-tuple-element.72) | data formatting | bytes 6881280
  226.1 0.0 copy-done
  226.1 0.0 copy-start.3
  226.1 0.0 copy-start.6
  226.1 0.0 copy-start.4
  226.1 0.0 copy-start.2
  226.1 0.0 copy-start.5
  226.1 0.0 copy-start.1
  226.1 1.8 copy.38
  227.9 0.0 copy-done.3
  227.9 0.7 copy.39
  228.5 0.0 copy-done.6
  228.6 0.6 copy.40
  229.1 0.0 copy-done.4
  229.1 0.6 copy.41
  229.8 0.0 copy-done.2
  229.8 0.7 copy.42
  230.5 0.0 copy-done.5
  230.5 0.6 copy.43
  231.1 0.0 copy-done.1
  231.1 0.7 copy.44
Async XLA Ops:
  221.9 4.1 %copy-start = (bf16[8,280,768]{2,1,0:T(8,128)(2,1)S(1)}, bf16[8,280,768]{2,1,0:T(8,128)(2,1)}, u32[]{:S(2)}) copy-start(bf16[8,280,768]{2,1,0:T(8,128)(2,1)} %get-tuple-element.73) | copy-start | bytes 10321924
  226.1 1.8 copy-start.3
  226.1 2.5 %copy-start.6 = (f32[2,384]{1,0:T(2,128)S(1)}, f32[2,384]{1,0:T(2,128)}, u32[]{:S(2)}) copy-start(f32[2,384]{1,0:T(2,128)} %get-tuple-element.77) | copy-start | bytes 9220
  226.1 3.1 %copy-start.4 = (f32[1,48,384]{2,1,0:T(8,128)S(1)}, f32[1,48,384]{2,1,0:T(8,128)}, u32[]{:S(2)}) copy-start(f32[1,48,384]{2,1,0:T(8,128)} %get-tuple-element.48) | copy-start | bytes 221188
  226.1 3.7 %copy-start.2 = (f32[48,1536]{1,0:T(8,128)S(1)}, f32[48,1536]{1,0:T(8,128)}, u32[]{:S(2)}) copy-start(f32[48,1536]{1,0:T(8,128)} %get-tuple-element.82) | copy-start | bytes 884740
  226.1 4.4 %copy-start.5 = (f32[1536]{0:T(1024)S(1)}, f32[1536]{0:T(1024)}, u32[]{:S(2)}) copy-start(f32[1536]{0:T(1024)} %get-tuple-element.83) | copy-start | bytes 18436
  226.1 5.0 %copy-start.1 = (f32[48,1536]{1,0:T(8,128)S(1)}, f32[48,1536]{1,0:T(8,128)}, u32[]{:S(2)}) copy-start(f32[48,1536]{1,0:T(8,128)} %get-tuple-element.51) | copy-start | bytes 884740

commit v9 on v8

--- a/solution.py
+++ b/solution.py
@@ -670,7 +670,7 @@
 
     ff_sib, ff_y, ff_z, ff_x, ff_final = family(g_ff, rc_ff, rs_ff, rz_ff, rx_ff, put_ff, 0, 0)
     p_sib, p_y, p_z, p_x, p_final = family(g_proj, rc_p, rs_p, rz_p, rx_p, put(r_proj), 2, 0)
-    q_sib, q_y, q_z, q_x, q_final = family(g_qkv, rc_q, rs_q, rz_q, rx_q, put_qkv, 3, 1)
+    q_sib, q_y, q_z, q_x, q_final = family(g_qkv, rc_q, rs_q, rz_q, rx_q, put_qkv, 3, 0)
 
     def out_copies(q):
         src = outbuf.at[q]
@@ -840,7 +840,10 @@
 
     def attention(w_ref, qkv_buf, prob_buf, x_buf, do_ref, n1, n1t, dq_all):
         high = n1.shape[0] // pairs
-        w_copy = pltpu.make_async_copy(w_one_in, w_ref, local.at[8])
+        proj_cols = pl.ds(3 * lw, lw)
+        qkv_cols = pl.ds(0, 3 * lw)
+        w_copy = pltpu.make_async_copy(w_one_in.at[:, :, proj_cols], w_ref.at[:, :, proj_cols], local.at[8])
+        w_qkv_copy = pltpu.make_async_copy(w_one_in.at[:, :, qkv_cols], w_ref.at[:, :, qkv_cols], local.at[6])
 
         def loads(p):
             slot = lax.rem(p, 2)
@@ -867,6 +870,7 @@
         ]
         for copy in n1_copies:
             copy.start()
+        w_qkv_copy.start()
         w_copy.wait()
 
         def attended_back(r):
@@ -950,6 +954,11 @@
                     ff_x((step - 16) // 5)
 
             loop(groups * tiles, heads)
+
+            @pl.when(p == 0)
+            def _():
+                w_qkv_copy.wait()
+
             done = sum(
                 dot(dq_all[here, mm * 3 * lw : (mm + 1) * 3 * lw], w_ref[mm, :, : 3 * lw], NT) for mm in range(groups))
             xhat, r = moments(x_buf[slot].astype(F32))
@@ -1034,9 +1043,9 @@
             for d in range(1, Z * Y * C):
                 pick = jnp.where(dp == d, row[:, d * part : (d + 1) * part], pick)
             o_vec[n : n + 1] = pick
-        loop(3, lambda i: q_z(0, 0, i))
         p_final(0)
         q_x(0)
+        loop(3, lambda i: q_z(0, 0, i))
         q_final(0)
 
         def finish(p):

time: 235 us -> 232 us (0.987); the launches traced: 232 us -> 232 us
  no operation moved by 1% of the time
where the time goes in v9:
time: 232 us
  Pallas kernels  220 us (95%)
  local copies, waits for them, and re-layouts  11.3 us (5%)
    pallas_call x1, Pallas kernels, backward_reduce(): pl.pallas_call(back_kernel, in_specs=[pl.BlockSpec(memory_space=pltpu.SME...  140 us
    pallas_call x1, Pallas kernels, gather_attention(): pl.pallas_call(gather_attn_kernel, grid_spec=pltpu.PrefetchScalarGridSpec...  79.5 us
    unnamed x22, local copies, waits for them, and re-layouts  9.82 us

profile of v9, /device:TPU:8, one launch (start us, length us, event | category | flops | bytes accessed | tf_op | source)
XLA Modules:
  0.0 231.7 jit_solution(11488434477614461008)
XLA Ops:
  0.6 79.5 %gather_attention.1 = (bf16[2,768,1664]{2,1,0:T(8,128)(2,1)}, bf16[2,768,3072]{2,1,0:T(8,128)(2,1)}, f32[2,8,2304]{2,1,0:T(8,128)}, bf16[4,280,2304]{2,1,0:T(8,1...) custom-call(s32[8]{0:T(128)} %counts.3, ...), custom_call_target="tpu_custom_call" | custom-call | tf_op jit(solution)/shard_map/gather_attention/pallas_call | solution.py:511
  80.2 140.1 %backward_reduce.1 = (bf16[8,280,768]{2,1,0:T(8,128)(2,1)}, bf16[8,280,768]{2,1,0:T(8,128)(2,1)}, f32[48,1536]{1,0:T(8,128)}, f32[48,1536]{1,0:T(8,128)}, f32[1,...) custom-call(s32[8]{0:T(128)} %counts.3, ...), custom_call_target="tpu_custom_call" | custom-call | tf_op jit(solution)/shard_map/backward_reduce/pallas_call | solution.py:1090
  220.3 1.5 slice_bitcast_fusion
  221.8 0.0 copy-start
  221.8 4.1 %copy.37 = bf16[8,280,768]{2,1,0:T(8,128)(2,1)} copy(bf16[8,280,768]{2,1,0:T(8,128)(2,1)} %get-tuple-element.72) | data formatting | bytes 6881280
  225.9 0.0 copy-done
  225.9 0.0 copy-start.3
  225.9 0.0 copy-start.6
  225.9 0.0 copy-start.4
  225.9 0.0 copy-start.2
  225.9 0.0 copy-start.5
  225.9 0.0 copy-start.1
  225.9 1.8 copy.38
  227.7 0.0 copy-done.3
  227.7 0.7 copy.39
  228.4 0.0 copy-done.6
  228.4 0.6 copy.40
  229.0 0.0 copy-done.4
  229.0 0.6 copy.41
  229.6 0.0 copy-done.2
  229.6 0.7 copy.42
  230.3 0.0 copy-done.5
  230.3 0.6 copy.43
  230.9 0.0 copy-done.1
  230.9 0.7 copy.44
Async XLA Ops:
  221.8 4.1 %copy-start = (bf16[8,280,768]{2,1,0:T(8,128)(2,1)S(1)}, bf16[8,280,768]{2,1,0:T(8,128)(2,1)}, u32[]{:S(2)}) copy-start(bf16[8,280,768]{2,1,0:T(8,128)(2,1)} %get-tuple-element.73) | copy-start | bytes 10321924
  225.9 1.8 copy-start.3
  225.9 2.5 %copy-start.6 = (f32[2,384]{1,0:T(2,128)S(1)}, f32[2,384]{1,0:T(2,128)}, u32[]{:S(2)}) copy-start(f32[2,384]{1,0:T(2,128)} %get-tuple-element.77) | copy-start | bytes 9220
  225.9 3.1 %copy-start.4 = (f32[1,48,384]{2,1,0:T(8,128)S(1)}, f32[1,48,384]{2,1,0:T(8,128)}, u32[]{:S(2)}) copy-start(f32[1,48,384]{2,1,0:T(8,128)} %get-tuple-element.48) | copy-start | bytes 221188
  225.9 3.7 %copy-start.2 = (f32[48,1536]{1,0:T(8,128)S(1)}, f32[48,1536]{1,0:T(8,128)}, u32[]{:S(2)}) copy-start(f32[48,1536]{1,0:T(8,128)} %get-tuple-element.82) | copy-start | bytes 884740
  225.9 4.4 %copy-start.5 = (f32[1536]{0:T(1024)S(1)}, f32[1536]{0:T(1024)}, u32[]{:S(2)}) copy-start(f32[1536]{0:T(1024)} %get-tuple-element.83) | copy-start | bytes 18436
  225.9 5.0 %copy-start.1 = (f32[48,1536]{1,0:T(8,128)S(1)}, f32[48,1536]{1,0:T(8,128)}, u32[]{:S(2)}) copy-start(f32[48,1536]{1,0:T(8,128)} %get-tuple-element.51) | copy-start | bytes 884740

commit v10 on v9

--- a/solution.py
+++ b/solution.py
@@ -888,6 +888,21 @@
         n1t[...] = n1[...].T
         first = lax.broadcasted_iota(jnp.int32, (1, 128), 1) < HEAD_DIM
 
+        def finish_pair(p):
+            slot = lax.rem(p, 2)
+            here = pl.ds(pl.multiple_of(p * high, 16), rows)
+            dhid = dhid_ref[pl.ds(pl.multiple_of(p * rows, 8), rows)]
+            done = sum(
+                dot(dq_all[here, mm * 3 * lw : (mm + 1) * 3 * lw], w_ref[mm, :, : 3 * lw], NT) for mm in range(groups))
+            xhat, r = moments(x_buf[slot].astype(F32))
+            dg = done * vec_ref[0:1]
+            dn = r * (dg - jnp.mean(dg, axis=-1, keepdims=True) - xhat * jnp.mean(dg * xhat, axis=-1, keepdims=True))
+            n1[here] = (dhid + dn).astype(LOW)
+            for copy in tok_copies(p):
+                copy.start()
+            sums[0:1] += jnp.sum(done * xhat, axis=0, keepdims=True)
+            sums[1:2] += jnp.sum(done, axis=0, keepdims=True)
+
         def one_pair(p):
             slot = lax.rem(p, 2)
 
@@ -896,7 +911,6 @@
                 for copy in loads(p + 1):
                     copy.start()
 
-            dhid = dhid_ref[pl.ds(pl.multiple_of(p * rows, 8), rows)]
             here = pl.ds(pl.multiple_of(p * high, 16), rows)
             for copy in loads(p):
                 copy.wait()
@@ -959,16 +973,9 @@
             def _():
                 w_qkv_copy.wait()
 
-            done = sum(
-                dot(dq_all[here, mm * 3 * lw : (mm + 1) * 3 * lw], w_ref[mm, :, : 3 * lw], NT) for mm in range(groups))
-            xhat, r = moments(x_buf[slot].astype(F32))
-            dg = done * vec_ref[0:1]
-            dn = r * (dg - jnp.mean(dg, axis=-1, keepdims=True) - xhat * jnp.mean(dg * xhat, axis=-1, keepdims=True))
-            n1[here] = (dhid + dn).astype(LOW)
-            for copy in tok_copies(p):
-                copy.start()
-            sums[0:1] += jnp.sum(done * xhat, axis=0, keepdims=True)
-            sums[1:2] += jnp.sum(done, axis=0, keepdims=True)
+            @pl.when(p < pairs - 1)
+            def _():
+                finish_pair(p)
 
         loop(pairs, one_pair)
 
@@ -978,59 +985,54 @@
                 device_id={"dp": to[0], "mp": to[1]}, device_id_type=MESH_ID,
             )
 
+        s0 = small_copy(0, 6, sib, 0)
+        s1 = small_copy(1, 7, (index(z, 1 - y, c), m), 1)
+        zs = [small_copy(1 + k, 8, beside(k), 1 + k) for k in (1, 2, 3)]
+        s2 = small_copy(5, 9, (me, 1 - m), 5)
+
+        def chunk(i):
+            mm = lax.rem(m + 1 + i // 3, 2)
+            at = pl.ds(pl.multiple_of(mm * 3 * lw + lax.rem(i, 3) * lw, 128), lw)
+            g_qkv[0, :, :, :, at] = dot(n1t[...], dq_all[:, at]).astype(LOW).reshape(Z * Y, C, part, lw)
+
+            @pl.when(i == 1)
+            def _():
+                p_x(0)
+
+            @pl.when(lax.rem(i, 3) == 2)
+            def _():
+                q_sib(0, 1 - i // 3)
+
+            @pl.when(i == 3)
+            def _():
+                loop(4, lambda k: q_y(0, 1, k))
+
+        loop(6, chunk)
+        finish_pair(pairs - 1)
         sbuf[6] = jnp.zeros_like(sbuf[6])
         sbuf[6, 0:1] = bsum_up[0:1]
         sbuf[6, 1:2, : 3 * width] = bsum[0:1]
         for n, (line, at) in enumerate(((2, 0), (2, 1), (2, 2), (3, 1), (2, 3), (3, 0))):
             sbuf[6, line : line + 1, at * width : (at + 1) * width] = sums[n : n + 1]
-        s0 = small_copy(0, 6, sib, 0)
-        s1 = small_copy(1, 7, (index(z, 1 - y, c), m), 1)
-        zs = [small_copy(1 + k, 8, beside(k), 1 + k) for k in (1, 2, 3)]
-        s2 = small_copy(5, 9, (me, 1 - m), 5)
         s0.start()
-
-        def chunk(i):
-            mm = lax.rem(m + 1 + i // 3, 2)
-            at = pl.ds(pl.multiple_of(mm * 3 * lw + lax.rem(i, 3) * lw, 128), lw)
-            g_qkv[0, :, :, :, at] = dot(n1t[...], dq_all[:, at]).astype(LOW).reshape(Z * Y, C, part, lw)
-
-            @pl.when(i == 0)
-            def _():
-                s0.wait()
-                sbuf[7] = sbuf[6] + sbuf[0]
-                s1.start()
-
-            @pl.when(i == 1)
-            def _():
-                p_x(0)
-
-            @pl.when(lax.rem(i, 3) == 2)
-            def _():
-                q_sib(0, 1 - i // 3)
-
-            @pl.when(i == 2)
-            def _():
-                s1.wait()
-                sbuf[8] = sbuf[7] + sbuf[1]
-                for copy in zs:
-                    copy.start()
-
-            @pl.when(i == 3)
-            def _():
-                loop(4, lambda k: q_y(0, 1, k))
-
-            @pl.when(i == 4)
-            def _():
-                for copy in zs:
-                    copy.wait()
-                sbuf[9] = sbuf[8] + sbuf[2] + sbuf[3] + sbuf[4]
-                s2.start()
-
-        loop(6, chunk)
         ff_final(0)
+        s0.wait()
+        sbuf[7] = sbuf[6] + sbuf[0]
+        s1.start()
         loop(4, lambda i: q_y(0, 0, i))
         loop(3, lambda i: q_z(0, 1, i))
+        s1.wait()
+        sbuf[8] = sbuf[7] + sbuf[1]
+        for copy in zs:
+            copy.start()
         ff_final(1)
+        p_final(0)
+        q_x(0)
+        for copy in zs:
+            copy.wait()
+        sbuf[9] = sbuf[8] + sbuf[2] + sbuf[3] + sbuf[4]
+        s2.start()
+        loop(3, lambda i: q_z(0, 0, i))
         s2.wait()
         sbuf[6] = sbuf[9] + sbuf[5]
         o_up[...] = sbuf[6, 0:1, pl.ds(pl.multiple_of(m * fw, 128), fw)].reshape(fw)
@@ -1043,9 +1045,6 @@
             for d in range(1, Z * Y * C):
                 pick = jnp.where(dp == d, row[:, d * part : (d + 1) * part], pick)
             o_vec[n : n + 1] = pick
-        p_final(0)
-        q_x(0)
-        loop(3, lambda i: q_z(0, 0, i))
         q_final(0)
 
         def finish(p):

time: 232 us -> 235 us (1.013)
    pallas_call x1, Pallas kernels: 140 us -> 143 us  [backward_reduce(): pl.pallas_call(back_kernel, in_specs=[pl.BlockSpec(memory_space=pltpu.SME...]
where the time goes in v10:
time: 235 us; the launch traced here: 234 us
  Pallas kernels  222 us (94%)
  local copies, waits for them, and re-layouts  11.3 us (5%)
    pallas_call x1, Pallas kernels, backward_reduce(): pl.pallas_call(back_kernel, in_specs=[pl.BlockSpec(memory_space=pltpu.SME...  143 us
    pallas_call x1, Pallas kernels, gather_attention(): pl.pallas_call(gather_attn_kernel, grid_spec=pltpu.PrefetchScalarGridSpec...  79.5 us
    unnamed x22, local copies, waits for them, and re-layouts  9.82 us

profile of v10, /device:TPU:8, one launch (start us, length us, event | category | flops | bytes accessed | tf_op | source)
XLA Modules:
  0.0 234.2 jit_solution(18094600501246518660)
XLA Ops:
  0.6 79.5 %gather_attention.1 = (bf16[2,768,1664]{2,1,0:T(8,128)(2,1)}, bf16[2,768,3072]{2,1,0:T(8,128)(2,1)}, f32[2,8,2304]{2,1,0:T(8,128)}, bf16[4,280,2304]{2,1,0:T(8,1...) custom-call(s32[8]{0:T(128)} %counts.3, ...), custom_call_target="tpu_custom_call" | custom-call | tf_op jit(solution)/shard_map/gather_attention/pallas_call | solution.py:511
  80.2 142.7 %backward_reduce.1 = (bf16[8,280,768]{2,1,0:T(8,128)(2,1)}, bf16[8,280,768]{2,1,0:T(8,128)(2,1)}, f32[48,1536]{1,0:T(8,128)}, f32[48,1536]{1,0:T(8,128)}, f32[1,...) custom-call(s32[8]{0:T(128)} %counts.3, ...), custom_call_target="tpu_custom_call" | custom-call | tf_op jit(solution)/shard_map/backward_reduce/pallas_call | solution.py:1089
  222.9 1.5 slice_bitcast_fusion
  224.4 0.0 copy-start
  224.4 4.1 %copy.37 = bf16[8,280,768]{2,1,0:T(8,128)(2,1)} copy(bf16[8,280,768]{2,1,0:T(8,128)(2,1)} %get-tuple-element.72) | data formatting | bytes 6881280
  228.5 0.0 copy-done
  228.5 0.0 copy-start.3
  228.5 0.0 copy-start.6
  228.5 0.0 copy-start.4
  228.5 0.0 copy-start.2
  228.5 0.0 copy-start.5
  228.5 0.0 copy-start.1
  228.5 1.8 copy.38
  230.3 0.0 copy-done.3
  230.3 0.7 copy.39
  231.0 0.0 copy-done.6
  231.0 0.6 copy.40
  231.6 0.0 copy-done.4
  231.6 0.6 copy.41
  232.2 0.0 copy-done.2
  232.2 0.7 copy.42
  232.9 0.0 copy-done.5
  232.9 0.6 copy.43
  233.5 0.0 copy-done.1
  233.5 0.7 copy.44
Async XLA Ops:
  224.4 4.1 %copy-start = (bf16[8,280,768]{2,1,0:T(8,128)(2,1)S(1)}, bf16[8,280,768]{2,1,0:T(8,128)(2,1)}, u32[]{:S(2)}) copy-start(bf16[8,280,768]{2,1,0:T(8,128)(2,1)} %get-tuple-element.73) | copy-start | bytes 10321924
  228.5 1.8 copy-start.3
  228.5 2.5 %copy-start.6 = (f32[2,384]{1,0:T(2,128)S(1)}, f32[2,384]{1,0:T(2,128)}, u32[]{:S(2)}) copy-start(f32[2,384]{1,0:T(2,128)} %get-tuple-element.77) | copy-start | bytes 9220
  228.5 3.1 %copy-start.4 = (f32[1,48,384]{2,1,0:T(8,128)S(1)}, f32[1,48,384]{2,1,0:T(8,128)}, u32[]{:S(2)}) copy-start(f32[1,48,384]{2,1,0:T(8,128)} %get-tuple-element.48) | copy-start | bytes 221188
  228.5 3.7 %copy-start.2 = (f32[48,1536]{1,0:T(8,128)S(1)}, f32[48,1536]{1,0:T(8,128)}, u32[]{:S(2)}) copy-start(f32[48,1536]{1,0:T(8,128)} %get-tuple-element.82) | copy-start | bytes 884740
  228.5 4.4 %copy-start.5 = (f32[1536]{0:T(1024)S(1)}, f32[1536]{0:T(1024)}, u32[]{:S(2)}) copy-start(f32[1536]{0:T(1024)} %get-tuple-element.83) | copy-start | bytes 18436
  228.5 5.0 %copy-start.1 = (f32[48,1536]{1,0:T(8,128)S(1)}, f32[48,1536]{1,0:T(8,128)}, u32[]{:S(2)}) copy-start(f32[48,1536]{1,0:T(8,128)} %get-tuple-element.51) | copy-start | bytes 884740
